TPU v7x, 32 devices: a whole 2x2x4 slice. The times are simulated.
32 devices in a mesh: dp: 8 (over y, x, core), space: 4 (over z).
Axes of the slice: x: 2, y: 2, z: 4, core: 2. Of those that a mesh axis runs over, the one named last changes fastest.
Arguments:
- inputs: bfloat16 [8, 32, 48, 512], P('dp', 'space'), may hold values from -6 to 6
- pre_act: bfloat16 [8, 32, 48, 512], P('dp', 'space'), may hold values from -8 to 8
- grad_out: bfloat16 [8, 32, 48, 512], P('dp', 'space'), may hold values from -6 to 6
- w_first: bfloat16 [512, 3, 3, 512], P('dp'), may hold values from -0.09375 to 0.09375
- w_second: bfloat16 [512, 3, 3, 512], P('dp'), may hold values from -0.09375 to 0.09375
Outputs:
- input_grad: float32 [8, 32, 48, 512], P('dp', 'space')
- first_grad: float32 [512, 3, 3, 512], P('dp')
- second_grad: float32 [512, 3, 3, 512], P('dp')
All inputs are finite; a program needn't handle non-finite values.
Results may differ from a plain program's by a relative error of at most 0.0029.
Values may be sent and summed in bfloat16 or wider, within the bound.
No kernel may reach another device: no remote copies, remote signals or barrier semaphores. Data moves between devices by JAX's collectives and lax.ppermute only.
A program may use at most 128 MiB of HBM per device.

v0:
```python
import jax
import jax.numpy as jnp
from jax import lax
from jax.sharding import PartitionSpec as P


def extended_2(cells, sides, width):
    for axis, dim in sides:
        count = lax.axis_size(axis)
        ends = count - 1
        head = lax.slice_in_dim(cells, 0, width, axis=dim)
        tail = lax.slice_in_dim(cells, cells.shape[dim] - width, cells.shape[dim], axis=dim)
        cells = jnp.concatenate(
            [
                lax.ppermute(tail, axis, [(i, (i + 1) % count) for i in range(ends)]),
                cells,
                lax.ppermute(head, axis, [((i + 1) % count, i) for i in range(ends)]),
            ],
            axis=dim,
        )
    return cells


def tap_stack(padded, height, width, flipped):
    pieces = []
    for row_tap in range(3):
        for col_tap in range(3):
            row_start = 2 - row_tap if flipped else row_tap
            col_start = 2 - col_tap if flipped else col_tap
            pieces.append(
                padded[..., row_start : row_start + height, col_start : col_start + width, :]
            )
    stacked = jnp.stack(pieces, axis=-2)
    return stacked.reshape(-1, 9, stacked.shape[-1])


def apply_rows(taps, piece):
    count = piece.shape[0]
    part = taps
    part = part.reshape(part.shape[0], 9 * count)
    kernel = jnp.transpose(piece, (1, 2, 0, 3)).reshape(9 * count, piece.shape[3])
    return jnp.dot(part, kernel, preferred_element_type=jnp.float32)


def per_device(inputs, pre_act, grad_out, w_first, w_second):
    height = inputs.shape[1]
    width = inputs.shape[2]
    channels = inputs.shape[3]
    h_flat = pre_act.reshape(-1, channels).astype(jnp.float32)
    sigma = jax.nn.sigmoid(h_flat)
    act = (h_flat * sigma).astype(jnp.bfloat16).reshape(inputs.shape)
    joined = jnp.stack([inputs, act, grad_out])
    extended = extended_2(joined, (("space", 2),), 1)
    extended = jnp.pad(extended, ((0, 0), (0, 0), (0, 0), (1, 1), (0, 0)))
    g_taps = tap_stack(extended[2], height, width, True)
    act_grad = apply_rows(g_taps, lax.all_gather(w_second, "dp", axis=0, tiled=True))
    pre_grad = (act_grad * (sigma * (1.0 + h_flat * (1.0 - sigma)))).astype(jnp.bfloat16)
    grad_field = pre_grad.reshape(inputs.shape)
    grad_ext = extended_2(grad_field, (("space", 1),), 1)
    grad_ext = jnp.pad(grad_ext, ((0, 0), (0, 0), (1, 1), (0, 0)))
    grad_taps = tap_stack(grad_ext, height, width, True)
    in_grad = apply_rows(grad_taps, lax.all_gather(w_first, "dp", axis=0, tiled=True))
    input_grad = in_grad.reshape(inputs.shape)
    act_flat = tap_stack(extended[1], height, width, False).reshape(-1, 9 * channels)
    x_flat = tap_stack(extended[0], height, width, False).reshape(-1, 9 * channels)
    g_flat = grad_out.reshape(-1, channels)
    owned = channels // lax.axis_size("dp")
    cols = g_flat
    term = jnp.dot(cols.T, act_flat, preferred_element_type=jnp.float32)
    second_part = lax.psum_scatter(
        term.reshape(owned * lax.axis_size("dp"), 3, 3, channels),
        "dp",
        scatter_dimension=0,
        tiled=True,
    )
    cols = pre_grad
    term = jnp.dot(cols.T, x_flat, preferred_element_type=jnp.float32)
    first_part = lax.psum_scatter(
        term.reshape(owned * lax.axis_size("dp"), 3, 3, channels),
        "dp",
        scatter_dimension=0,
        tiled=True,
    )
    first_grad, second_grad = lax.psum((first_part, second_part), "space")
    return (input_grad, first_grad, second_grad)


def solution(mesh):
    return jax.shard_map(
        per_device,
        mesh=mesh,
        in_specs=(
            P("dp", "space", None, None),
            P("dp", "space", None, None),
            P("dp", "space", None, None),
            P("dp", None, None, None),
            P("dp", None, None, None),
        ),
        out_specs=(
            P("dp", "space", None, None),
            P("dp", None, None, None),
            P("dp", None, None, None),
        ),
        check_vma=False,
    )
```

profile of v0, /device:TPU:0, one launch (start us, length us, event | category | flops | bytes accessed | tf_op | source)
XLA Modules:
  0.0 361.8 jit_solution(15204915057387501731)
XLA Ops:
  7.2 0.7 all-gather.3.cloned.1.call-update
  7.9 0.0 reduce-scatter.5.cloned.1.call-start
  7.9 1.2 fusion.13
  9.2 0.9 pad_maximum_fusion.4
  10.1 1.3 collective-permute-start.1
  11.4 5.6 %collective-permute-start = (bf16[3,1,1,48,512]{4,3,2,1,0:T(8,128)(2,1)S(1)}, bf16[3,1,1,48,512]{4,3,2,1,0:T(8,128)(2,1)S(1)}, u32[]{:S(2)}, u32[]{:S(2)}) collective-permute-start(bf16[3,1,1,48,512]{4,3,2,1,0:T(8,128)(2,1)S(1)} %get-tuple-element.8), channel_id=1, source_target_pairs={{0,1},{1,2},{2,3},{4,5},{5,6},{6,7},{8,9},{9,10},{10,11},{12,13},{... | collective-permute-start | bytes 442376 | tf_op jit(solution)/shard_map/ppermute | solution.py:15
  17.0 1.9 collective-permute-done.1
  18.9 1.2 collective-permute-done
  20.0 2.0 select_maximum_fusion
  22.1 0.1 slice_bitcast_fusion
  22.2 0.1 fusion.31
  22.3 0.1 fusion.30
  22.5 0.1 fusion.28
  22.6 0.1 fusion.27
  22.7 0.1 fusion.25
  22.9 0.1 fusion.40
  23.0 0.1 fusion.39
  23.1 0.1 fusion.37
  23.2 0.1 fusion.36
  23.4 0.1 fusion.34
  23.5 0.3 fusion.24
  23.8 1.8 copy-done.2
  25.6 2.6 copy.30
  28.2 4.1 %copy.36 = bf16[48,8,9,512]{3,1,2,0:T(8,128)(2,1)S(1)} copy(bf16[48,8,9,512]{3,2,1,0:T(8,128)(2,1)S(1)} %bitcast.218) | data formatting | bytes 7077888
  32.3 5.2 %fusion.64 = f32[4608,512]{1,0:T(8,128)} fusion(bf16[384,4608]{1,0:T(8,128)(2,1)S(1)} %bitcast.221, bf16[384,512]{1,0:T(8,128)(2,1)S(1)} %bitcast.231), kind=kOutput, calls=%fused_computation.117 | convolution fusion | flops 1811939328 | bytes 13369344 | tf_op jit(solution)/shard_map/dot_general | solution.py:69
  37.6 9.6 %copy.31 = f32[512,3,3,512]{3,0,2,1:T(8,128)} copy(f32[512,3,3,512]{0,3,2,1:T(8,128)} %bitcast.217) | data formatting | bytes 18874368 | tf_op jit(solution)/shard_map/reshape | solution.py:71
  47.2 0.2 reduce-scatter.3.cloned.1.call-start
  47.5 0.8 copy-done.5
  48.3 1.1 fusion.18
  49.4 0.1 fusion.60
  49.5 0.1 fusion.59
  49.7 0.1 fusion.57
  49.8 0.1 fusion.56
  49.9 0.1 fusion.54
  50.0 0.1 fusion.53
  50.2 2.6 copy.25
  52.8 6.0 %copy.34 = bf16[48,8,9,512]{3,1,2,0:T(8,128)(2,1)} copy(bf16[48,8,9,512]{3,2,1,0:T(8,128)(2,1)S(1)} %bitcast.219) | data formatting | bytes 7077888
  58.8 2.6 copy.27
  61.4 6.3 %copy.35 = bf16[48,8,9,512]{3,1,2,0:T(8,128)(2,1)} copy(bf16[48,8,9,512]{3,2,1,0:T(8,128)(2,1)S(1)} %bitcast.220) | data formatting | bytes 7077888
  67.8 4.8 %copy.28 = bf16[4608,384]{1,0:T(8,128)(2,1)S(1)} copy(bf16[4608,384]{0,1:T(8,128)(2,1)} %bitcast.223) | data formatting | bytes 7077888 | tf_op jit(solution)/shard_map/dot_general | solution.py:77
  72.6 5.6 %fusion.6 = bf16[384,512]{1,0:T(8,128)(2,1)S(1)} fusion(f32[384,512]{1,0:T(8,128)} %fusion.18, bf16[384,4608]{1,0:T(8,128)(2,1)} %bitcast.232, bf16[4608,512]{1,0:T(8,128)(2,1)} %bitcast.235), kind=kOutput, calls=%fused_computation.14 | convolution fusion | flops 1812332544 | bytes 9437184 | tf_op jit(solution)/shard_map/dot_general | solution.py:42
  78.2 0.7 copy-done
  78.9 6.3 %fusion.61 = f32[512,3,3,512]{3,0,2,1:T(8,128)} fusion(bf16[3,3,512,384]{3,2,1,0:T(8,128)(2,1)S(1)} %bitcast.222, bf16[384,512]{1,0:T(8,128)(2,1)S(1)} %fusion.6), kind=kOutput, calls=%fused_computation.110 | convolution fusion | flops 1811939328 | bytes 13369344 | tf_op jit(solution)/shard_map/dot_general | solution.py:77
  85.3 0.0 all-gather.5.cloned.1.call-start
  85.4 0.5 all-gather.5.cloned.1.call-update
  85.9 0.0 all-reduce.5.cloned.1.call-start
  85.9 0.3 copy-done.1
  86.3 1.3 collective-permute-start.3
  87.6 4.9 %collective-permute-start.2 = (bf16[1,1,48,512]{3,2,1,0:T(8,128)(2,1)S(1)}, bf16[1,1,48,512]{3,2,1,0:T(8,128)(2,1)S(1)}, u32[]{:S(2)}, u32[]{:S(2)}) collective-permute-start(bf16[1,1,48,512]{3,2,1,0:T(8,128)(2,1)S(1)} %get-tuple-element.10), channel_id=1, source_target_pairs={{0,1},{1,2},{2,3},{4,5},{5,6},{6,7},{8,9},{9,10},{10,11},{12,13},{... | collective-permute-start | bytes 147464 | tf_op jit(solution)/shard_map/ppermute | solution.py:15
  92.5 0.1 collective-permute-done.3
  92.6 1.6 collective-permute-done.2
  94.2 0.2 fusion.23
  94.4 37.2 %reduce-scatter.5.cloned.1.call-done = f32[64,3,3,512]{3,0,2,1:T(8,128)} async-done(((f32[512,3,3,512]{3,0,2,1:T(8,128)}), f32[64,3,3,512]{3,0,2,1:T(8,128)}) %reduce-scatter.5.cloned.1.call-update) | async-done | bytes 1179664 | tf_op jit(solution)/shard_map/reduce_scatter | solution.py:70
  131.6 80.0 %reduce-scatter.3.cloned.1.call-done = f32[64,3,3,512]{3,0,2,1:T(8,128)} async-done(((f32[512,3,3,512]{3,0,2,1:T(8,128)}), f32[64,3,3,512]{3,0,2,1:T(8,128)}) %reduce-scatter.3.cloned.1.call-update) | async-done | bytes 1179664 | tf_op jit(solution)/shard_map/reduce_scatter | solution.py:78
  211.6 0.1 fusion.51
  211.8 0.1 fusion.47
  212.0 0.1 fusion.45
  212.2 5.3 %copy.26 = bf16[1,8,48,9,512]{4,3,2,1,0:T(8,128)(2,1)} copy(bf16[1,8,48,9,512]{4,2,1,3,0:T(8,128)(2,1)S(1)} %fusion.42) | data formatting | bytes 7077888 | tf_op jit(solution)/shard_map/stack | solution.py:33
  217.4 6.1 %reshape.67 = bf16[8,48,4608]{2,1,0:T(8,128)(2,1)S(1)} reshape(bf16[1,8,48,9,512]{4,3,2,1,0:T(8,128)(2,1)} %copy.26) | data formatting | bytes 7077888 | tf_op jit(solution)/shard_map/reshape.5
  223.5 28.8 %all-gather.5.cloned.1.call-done = bf16[512,3,3,512]{3,0,2,1:T(8,128)(2,1)} async-done(((bf16[64,3,3,512]{3,0,2,1:T(8,128)(2,1)}), bf16[512,3,3,512]{3,0,2,1:T(8,128)(2,1)}) %all-gather.5.cloned.1.call-update) | async-done | bytes 4718608 | tf_op jit(solution)/shard_map/all_gather | solution.py:62
  252.3 5.2 %convolution_bitcast_fusion = f32[1,8,48,512]{3,2,1,0:T(8,128)} fusion(bf16[8,48,4608]{2,1,0:T(8,128)(2,1)S(1)} %reshape.67, bf16[4608,512,1]{1,0,2:T(8,128)(2,1)} %bitcast.236), kind=kOutput, calls=%fused_computation.12 | convolution fusion | flops 1811939328 | bytes 9043968 | tf_op jit(solution)/shard_map/dot_general | solution.py:42
  257.5 93.1 %all-reduce.5.cloned.1.call-done = (f32[64,3,3,512]{3,0,2,1:T(8,128)}, f32[64,3,3,512]{3,0,2,1:T(8,128)}) async-done(((f32[64,3,3,512]{3,0,2,1:T(8,128)}, f32[64,3,3,512]{3,0,2,1:T(8,128)}), (f32[64,3,3,512]{3,0,2,1:T(8,128)}, f32[64,3,3,512]{3,0,2,1:T(8,128)})) %all-reduce.5.cloned.1.call-update) | async-done | bytes 2359312 | tf_op jit(solution)/shard_map/psum | solution.py:84
  350.6 2.4 copy.71
  353.0 2.4 copy.72
  (29 shorter events, 0.6 us)
Async XLA Ops:
  7.2 65.4 %all-gather.3.cloned.1.call-start = ((), (), s32[]{:S(2)}) async-start(), calls=%async_computation.2 | async-start | bytes 5308416 | tf_op jit(solution)/shard_map/all_gather | solution.py:56
  7.9 123.7 %reduce-scatter.5.cloned.1.call-start = ((), (), s32[]{:S(2)}) async-start(), calls=%async_computation.5 | async-start | bytes 10616832 | tf_op jit(solution)/shard_map/reduce_scatter | solution.py:70
  10.1 8.8 %collective-permute-start.1 = (bf16[3,1,1,48,512]{4,3,2,1,0:T(8,128)(2,1)S(1)}, bf16[3,1,1,48,512]{4,3,2,1,0:T(8,128)(2,1)S(1)}, u32[]{:S(2)}, u32[]{:S(2)}) collective-permute-start(bf16[3,1,1,48,512]{4,3,2,1,0:T(8,128)(2,1)S(1)} %get-tuple-element.9), channel_id=1, source_target_pairs={{1,0},{2,1},{3,2},{5,4},{6,5},{7,6},{9,8},{10,9},{11,10},{13,12},{... | collective-permute-start | bytes 442376 | tf_op jit(solution)/shard_map/ppermute | solution.py:17
  11.4 8.7 %collective-permute-start = (bf16[3,1,1,48,512]{4,3,2,1,0:T(8,128)(2,1)S(1)}, bf16[3,1,1,48,512]{4,3,2,1,0:T(8,128)(2,1)S(1)}, u32[]{:S(2)}, u32[]{:S(2)}) collective-permute-start(bf16[3,1,1,48,512]{4,3,2,1,0:T(8,128)(2,1)S(1)} %get-tuple-element.8), channel_id=1, source_target_pairs={{0,1},{1,2},{2,3},{4,5},{5,6},{6,7},{8,9},{9,10},{10,11},{12,13},{... | collective-permute-start | bytes 442376 | tf_op jit(solution)/shard_map/ppermute | solution.py:15
  23.7 1.8 copy-start.2
  28.2 4.1 %copy-start.4 = (bf16[1,8,48,512]{3,2,1,0:T(8,128)(2,1)S(1)}, bf16[1,8,48,512]{3,2,1,0:T(8,128)(2,1)}, u32[]{:S(2)}) copy-start(bf16[1,8,48,512]{3,2,1,0:T(8,128)(2,1)} %param.7) | copy-start | bytes 1179652
  47.2 1.0 copy-start.5
  47.2 164.3 %reduce-scatter.3.cloned.1.call-start = ((), (), s32[]{:S(2)}) async-start(), calls=%async_computation.4 | async-start | bytes 10616832 | tf_op jit(solution)/shard_map/reduce_scatter | solution.py:78
  52.8 6.0 %copy-start.3 = (bf16[1,8,48,9,512]{4,2,1,3,0:T(8,128)(2,1)S(1)}, bf16[1,8,48,9,512]{4,2,1,3,0:T(8,128)(2,1)}, u32[]{:S(2)}) copy-start(bf16[1,8,48,9,512]{4,2,1,3,0:T(8,128)(2,1)} %copy-done.2) | copy-start | bytes 10616836
  78.2 0.7 copy-start
  85.3 1.0 copy-start.1
  85.3 167.0 %all-gather.5.cloned.1.call-start = ((), (), s32[]{:S(2)}) async-start(), calls=%async_computation.3 | async-start | bytes 5308416 | tf_op jit(solution)/shard_map/all_gather | solution.py:62
  85.9 264.7 %all-reduce.5.cloned.1.call-start = ((), (), s32[]{:S(2)}) async-start(), calls=%async_computation.6 | async-start | bytes 4718592 | tf_op jit(solution)/shard_map/psum | solution.py:84
  86.3 6.3 %collective-permute-start.3 = (bf16[1,1,48,512]{3,2,1,0:T(8,128)(2,1)S(1)}, bf16[1,1,48,512]{3,2,1,0:T(8,128)(2,1)S(1)}, u32[]{:S(2)}, u32[]{:S(2)}) collective-permute-start(bf16[1,1,48,512]{3,2,1,0:T(8,128)(2,1)S(1)} %get-tuple-element.11), channel_id=1, source_target_pairs={{1,0},{2,1},{3,2},{5,4},{6,5},{7,6},{9,8},{10,9},{11,10},{13,12},{... | collective-permute-start | bytes 147464 | tf_op jit(solution)/shard_map/ppermute | solution.py:17
  87.6 6.6 %collective-permute-start.2 = (bf16[1,1,48,512]{3,2,1,0:T(8,128)(2,1)S(1)}, bf16[1,1,48,512]{3,2,1,0:T(8,128)(2,1)S(1)}, u32[]{:S(2)}, u32[]{:S(2)}) collective-permute-start(bf16[1,1,48,512]{3,2,1,0:T(8,128)(2,1)S(1)} %get-tuple-element.10), channel_id=1, source_target_pairs={{0,1},{1,2},{2,3},{4,5},{5,6},{6,7},{8,9},{9,10},{10,11},{12,13},{... | collective-permute-start | bytes 147464 | tf_op jit(solution)/shard_map/ppermute | solution.py:15
Sparse Core Ops, SparseCore 0:
  9.9 41.6 all-gather.2
  55.0 76.4 reduce-scatter.4
  135.1 76.4 reduce-scatter.2
  213.4 38.8 all-gather.4
  254.6 95.9 all-reduce.4
where the time goes:
time: 363 us; the launch traced here: 362 us
  waiting for transfers between devices  245 us (67%)
  local copies, waits for them, and re-layouts  61.2 us (17%)
  matrix products  22.4 us (6%)
  between operations  14.2 us (4%)
  starting transfers between devices  13.4 us (4%)
  other arithmetic  5.53 us (2%)
    reduce_scatter x2, waiting for transfers between devices, per_device(): lax.psum_scatter(term.reshape(owned * lax.axis_size('dp'), 3, 3, channels...  117 us
    psum x1, waiting for transfers between devices, per_device(): first_grad, second_grad = lax.psum((first_part, second_part), 'space')  93.1 us
    all_gather x1, waiting for transfers between devices, per_device(): lax.all_gather(w_first, 'dp', axis=0, tiled=True)  28.8 us
    unnamed x47, local copies, waits for them, and re-layouts  27.1 us
    another operation x7, local copies, waits for them, and re-layouts, tap_stack(): stacked = jnp.stack(pieces, axis=-2)  13.4 us
    dot_general x2, matrix products, apply_rows(): return jnp.dot(part, kernel, preferred_element_type=jnp.float32)  10.8 us
    ppermute x2, starting transfers between devices, extended_2(): lax.ppermute(tail, axis, [(i, (i + 1) % count) for i in range(ends)])  10.4 us
    reshape x1, local copies, waits for them, and re-layouts, per_device(): term.reshape(owned * lax.axis_size('dp'), 3, 3, channels)  9.64 us
  transfers between devices with their start and end apart: 9, of which 8 were waited for; matrix products, arithmetic and copies ran while one was open for 22% of the time, Pallas kernels for 0%

commit v1 on v0

v1 whole, which is shorter than its diff:
```python
import jax
import jax.numpy as jnp
from jax import lax
from jax.experimental import pallas as pl
from jax.experimental.pallas import tpu as pltpu
from jax.sharding import PartitionSpec as P

BF = jnp.bfloat16
F32 = jnp.float32
PARAMS = pltpu.CompilerParams(vmem_limit_bytes=48 * 1024 * 1024)
ANY = pl.BlockSpec(memory_space=pl.ANY)
VM = pl.BlockSpec(memory_space=pltpu.VMEM)
SM = pl.BlockSpec(memory_space=pltpu.SMEM)


def xor_pairs(count, k):
    return [(i, i ^ k) for i in range(count)]


def swap(value, axis, k):
    return lax.ppermute(value, axis, xor_pairs(lax.axis_size(axis), k))


def shifted(flat, width):
    rows = flat.shape[0]
    wide = flat.astype(F32)
    col = lax.broadcasted_iota(jnp.int32, wide.shape, 0) % width
    left = jnp.where(col == 0, 0.0, pltpu.roll(wide, 1, 0)).astype(BF)
    right = jnp.where(col == width - 1, 0.0, pltpu.roll(wide, rows - 1, 0)).astype(BF)
    return left, flat, right


def conv_kernel(count, width, pieces, owned, gated):
    def body(*refs):
        ids = refs[0]
        up, mid, down = refs[1:4]
        weights = refs[4 : 4 + count]
        at = 4 + count
        if gated:
            pre = refs[at]
            at += 1
        out = refs[at]
        at += 1
        parts = refs[at : at + pieces]
        at += pieces
        field, kernel, sems = refs[at : at + 3]
        stage = refs[at + 3] if pieces else None
        copies = []
        for k in range(count):
            rows = weights[k].shape[0]
            start = pl.multiple_of((ids[0] ^ k) * rows, rows) if count > 1 else 0
            copies.append(
                pltpu.make_async_copy(weights[k], kernel.at[pl.ds(start, rows)], sems.at[k])
            )
            copies[-1].start()
        n = mid.shape[0]
        flat = jnp.concatenate([up[...], mid[...], down[...]], axis=0)
        left, same, right = shifted(flat, width)
        field[0] = right
        field[1] = same
        field[2] = left
        for copy in copies:
            copy.wait()
        c = out.shape[1]
        acc = None
        for r in range(3):
            for s in range(3):
                tap = 3 * r + s
                lhs = field[s, (2 - r) * width : (2 - r) * width + n, :]
                part = jnp.dot(
                    lhs, kernel[:, tap * c : (tap + 1) * c], preferred_element_type=F32
                )
                acc = part if acc is None else acc + part
        if gated:
            h = pre[...].astype(F32)
            sig = jax.nn.sigmoid(h)
            acc = acc * (sig * (1.0 + h * (1.0 - sig)))
        res = acc.astype(out.dtype)
        out[...] = res
        if pieces:
            w = c // pieces
            for t in range(pieces):
                stage[t] = res[:, t * w : (t + 1) * w]
            for k in range(pieces):
                parts[k][...] = stage[(ids[0] >> 1) ^ k]

    return body


def conv(ids, up, mid, down, weights, width, pre=None, pieces=0):
    n, c = mid.shape
    count = len(weights)
    owned = weights[0].shape[0]
    out_type = BF if pre is not None else F32
    outs = [jax.ShapeDtypeStruct((n, c), out_type)]
    scratch = [
        pltpu.VMEM((3, n + 2 * width, c), BF),
        pltpu.VMEM((owned * count, weights[0].shape[1]), BF),
        pltpu.SemaphoreType.DMA((count,)),
    ]
    if pieces:
        outs += [jax.ShapeDtypeStruct((n, c // pieces), BF)] * pieces
        scratch.append(pltpu.VMEM((pieces, n, c // pieces), BF))
    args = [ids, up, mid, down, *weights] + ([pre] if pre is not None else [])
    specs = [SM, VM, VM, VM] + [ANY] * count + ([VM] if pre is not None else [])
    return pl.pallas_call(
        conv_kernel(count, width, pieces, owned, pre is not None),
        out_shape=outs,
        in_specs=specs,
        out_specs=[VM] * len(outs),
        scratch_shapes=scratch,
        compiler_params=PARAMS,
        name="conv_gated" if pre is not None else "conv_plain",
    )(*args)


def wgrad_kernel(count, width):
    def body(*refs):
        ids = refs[0]
        fields = refs[1 : 1 + count]
        cots = refs[1 + count : 1 + 2 * count]
        keep, send = refs[1 + 2 * count : 3 + 2 * count]
        taps, cot, acc = refs[3 + 2 * count :]
        n = cots[0].shape[0]
        for i in range(count):
            left, same, right = shifted(fields[i][...], width)
            taps[i, 0] = left
            taps[i, 1] = same
            taps[i, 2] = right
            cot[:, i * n : (i + 1) * n] = cots[i][...].T
        c = fields[0].shape[1]
        for r in range(3):
            for s in range(3):
                total = None
                for i in range(count):
                    part = jnp.dot(
                        cot[:, i * n : (i + 1) * n],
                        taps[i, s, r * width : r * width + n, :],
                        preferred_element_type=F32,
                    )
                    total = part if total is None else total + part
                acc[:, (3 * r + s) * c : (3 * r + s + 1) * c] = total
        half = keep.shape[0]
        mine = ids[0] & 1
        keep[...] = acc[pl.ds(pl.multiple_of(mine * half, half), half), :]
        send[...] = acc[pl.ds(pl.multiple_of((1 - mine) * half, half), half), :]

    return body


def wgrad(ids, fields, cots, width):
    count = len(fields)
    n, w = cots[0].shape
    rows, c = fields[0].shape
    half = jax.ShapeDtypeStruct((w // 2, 9 * c), F32)
    return pl.pallas_call(
        wgrad_kernel(count, width),
        out_shape=[half, half],
        in_specs=[SM] + [VM] * (2 * count),
        out_specs=[VM, VM],
        scratch_shapes=[
            pltpu.VMEM((count, 3, rows, c), BF),
            pltpu.VMEM((w, count * n), BF),
            pltpu.VMEM((w, 9 * c), F32),
        ],
        compiler_params=PARAMS,
        name="wgrad",
    )(ids, *fields, *cots)


def reduced(keep, send):
    total = keep + swap(send, "dp", 1)
    count = lax.axis_size("space")
    at = lax.axis_index("space")
    blocks = total.reshape(count, total.shape[0] // count, total.shape[1])
    mine = lax.dynamic_index_in_dim(blocks, at, 0, keepdims=False)
    for k in range(1, count):
        sent = lax.dynamic_index_in_dim(blocks, at ^ k, 0, keepdims=False).astype(BF)
        mine = mine + swap(sent, "space", k).astype(F32)
    mine = mine.astype(BF)
    got = jnp.stack([mine] + [swap(mine, "space", k) for k in range(1, count)])
    order = jnp.arange(count) ^ at
    whole = jnp.concatenate(
        [lax.dynamic_index_in_dim(got, order[j], 0, keepdims=False) for j in range(count)], axis=0
    )
    return whole.astype(F32)


def per_device(inputs, pre_act, grad_out, w_first, w_second):
    _, height, width, c = inputs.shape
    n = height * width
    dp = lax.axis_size("dp")
    chips = dp // 2
    owned = w_first.shape[0]
    me = lax.axis_index("dp")
    ids = me.astype(jnp.int32).reshape(1)
    chip = me >> 1

    x = inputs.reshape(n, c)
    h = pre_act.reshape(n, c)
    g = grad_out.reshape(n, c)
    hf = h.astype(F32)
    act = (hf * jax.nn.sigmoid(hf)).astype(BF)

    w2 = w_second.reshape(owned, 9 * c)
    w1 = w_first.reshape(owned, 9 * c)
    w1_all = lax.all_gather(w1, "dp", axis=0, tiled=True)

    strips = lax.axis_size("space")
    down_pairs = [(i, i + 1) for i in range(strips - 1)]
    up_pairs = [(i + 1, i) for i in range(strips - 1)]

    def halos(value):
        above = lax.ppermute(value[..., n - width :, :], "space", down_pairs)
        below = lax.ppermute(value[..., :width, :], "space", up_pairs)
        return above, below

    above, below = halos(jnp.stack([x, act, g]))
    x_ext = jnp.concatenate([above[0], x, below[0]], axis=0)
    act_ext = jnp.concatenate([above[1], act, below[1]], axis=0)

    shards = [w2] + [None] * (dp - 1)
    for k in range(2, dp, 2):
        shards[k] = swap(w2, "dp", k)
    for k in range(0, dp, 2):
        shards[k + 1] = swap(shards[k], "dp", 1)

    pre_grad, *cots = conv(ids, above[2], g, below[2], shards, width, pre=h, pieces=chips)

    acts = [act_ext] + [swap(act_ext, "dp", 2 * k) for k in range(1, chips)]
    block = g.reshape(n, chips, c // chips)
    g_cots = []
    for k in range(chips):
        part = lax.dynamic_index_in_dim(block, chip ^ k, 1, keepdims=False)
        g_cots.append(swap(part, "dp", 2 * k) if k else part)
    second = reduced(*wgrad(ids, acts, g_cots, width))

    xs = [x_ext] + [swap(x_ext, "dp", 2 * k) for k in range(1, chips)]
    p_cots = [cots[0]] + [swap(cots[k], "dp", 2 * k) for k in range(1, chips)]
    first = reduced(*wgrad(ids, xs, p_cots, width))

    p_above, p_below = halos(pre_grad)
    (in_grad,) = conv(ids, p_above, pre_grad, p_below, [w1_all], width)
    shape = (owned, 3, 3, c)
    return in_grad.reshape(inputs.shape), first.reshape(shape), second.reshape(shape)


def solution(mesh):
    return jax.shard_map(
        per_device,
        mesh=mesh,
        in_specs=(
            P("dp", "space", None, None),
            P("dp", "space", None, None),
            P("dp", "space", None, None),
            P("dp", None, None, None),
            P("dp", None, None, None),
        ),
        out_specs=(
            P("dp", "space", None, None),
            P("dp", None, None, None),
            P("dp", None, None, None),
        ),
        check_vma=False,
    )
```

time: 363 us -> 212 us (0.58)
  waiting for transfers between devices: 245 us -> 103 us
  local copies, waits for them, and re-layouts: 61.2 us -> 13.9 us
  starting transfers between devices: 13.4 us -> 50.3 us
  matrix products: 22.4 us -> 0 us
  Pallas kernels: 0 us -> 16.6 us
  between operations: 14.2 us -> 21.8 us
    reduce_scatter x2 -> x0, waiting for transfers between devices: 117 us -> none  [per_device(): lax.psum_scatter(term.reshape(owned * lax.axis_size('dp'), 3, 3, channels...]
    ppermute x4 -> x37, waiting for transfers between devices: 4.81 us -> 103 us  [the longest x33 98.2 us: swap(): return lax.ppermute(value, axis, xor_pairs(lax.axis_size(axis), k))]
    psum x1 -> x0, waiting for transfers between devices: 93.1 us -> none  [per_device(): first_grad, second_grad = lax.psum((first_part, second_part), 'space')]
    ppermute x4 -> x37, starting transfers between devices: 13 us -> 50.3 us  [the longest x33 39.5 us: swap(): return lax.ppermute(value, axis, xor_pairs(lax.axis_size(axis), k))]
    all_gather x2 -> x1, waiting for transfers between devices: 28.8 us -> 0.01 us  [per_device(): w1_all = lax.all_gather(w1, 'dp', axis=0, tiled=True)]
    dot_general x4 -> x0, matrix products: 22.4 us -> none  [the longest x2 10.8 us: apply_rows(): return jnp.dot(part, kernel, preferred_element_type=jnp.float32)]
    another operation x8 -> x1, local copies, waits for them, and re-layouts: 19.5 us -> 0.09 us  [per_device(): block = g.reshape(n, chips, c // chips)]
    unnamed x47 -> x22, local copies, waits for them, and re-layouts: 27.1 us -> 8.11 us
  transfers between devices with their start and end apart: 9 -> 38, of which waited for: 8 -> 15; matrix products, arithmetic and copies ran while one was open for 22% -> 6% of each run, Pallas kernels for 0% -> 6%
where the time goes in v1:
time: 212 us; the launch traced here: 211 us
  waiting for transfers between devices  103 us (49%)
  starting transfers between devices  50.3 us (24%)
  between operations  21.8 us (10%)
  Pallas kernels  16.6 us (8%)
  local copies, waits for them, and re-layouts  13.9 us (7%)
  other arithmetic  5.44 us (3%)
    ppermute x33, waiting for transfers between devices, swap(): return lax.ppermute(value, axis, xor_pairs(lax.axis_size(axis), k))  98.2 us
    ppermute x33, starting transfers between devices, swap(): return lax.ppermute(value, axis, xor_pairs(lax.axis_size(axis), k))  39.5 us
    pallas_call x2, Pallas kernels, wgrad(): pl.pallas_call(wgrad_kernel(count, width), out_shape=[half, half], in_spe...  9.13 us
    unnamed x22, local copies, waits for them, and re-layouts  8.11 us
    ppermute x2, starting transfers between devices, halos(): above = lax.ppermute(value[..., n - width:, :], 'space', down_pairs)  7.74 us
    pallas_call x2, Pallas kernels, conv(): pl.pallas_call(conv_kernel(count, width, pieces, owned, pre is not None),...  7.5 us
    ppermute x2, waiting for transfers between devices, halos(): below = lax.ppermute(value[..., :width, :], 'space', up_pairs)  4.7 us
  transfers between devices with their start and end apart: 38, of which 15 were waited for; matrix products, arithmetic and copies ran while one was open for 6% of the time, Pallas kernels for 6%

profile of v1, /device:TPU:0, one launch (start us, length us, event | category | flops | bytes accessed | tf_op | source)
XLA Modules:
  0.0 211.0 jit_solution(6428410025052033776)
XLA Ops:
  7.2 1.6 copy.14
  8.8 0.8 reshape.89.refs_4_
  9.7 0.5 collective-permute-start.2
  10.2 2.6 %collective-permute-start.3 = (bf16[64,4608]{1,0:T(8,128)(2,1)S(1)}, bf16[64,4608]{1,0:T(8,128)(2,1)}, u32[]{:S(2)}, u32[]{:S(2)}) collective-permute-start(bf16[64,4608]{1,0:T(8,128)(2,1)S(1)} %reshape.89.refs_4_), channel_id=1, source_target_pairs={{0,8},{4,12},{8,0},{12,4},{16,24},{20,28},{24,16},{28,20},{1,9},{5... | collective-permute-start | bytes 1769480 | tf_op jit(solution)/shard_map/ppermute | solution.py:21
  12.8 1.5 collective-permute-start.5
  14.3 0.5 copy.15
  14.8 1.6 reshape.91
  16.4 0.3 fusion.7
  16.7 0.7 pad_maximum_fusion.4
  17.5 4.1 %collective-permute-start = (bf16[3,48,512]{2,1,0:T(8,128)(2,1)}, bf16[3,48,512]{2,1,0:T(8,128)(2,1)}, u32[]{:S(2)}, u32[]{:S(2)}) collective-permute-start(bf16[3,48,512]{2,1,0:T(8,128)(2,1)} %get-tuple-element.31), channel_id=1, source_target_pairs={{0,1},{1,2},{2,3},{4,5},{5,6},{6,7},{8,9},{9,10},{10,11},{12,13},{... | collective-permute-start | bytes 442376 | tf_op jit(solution)/shard_map/ppermute | solution.py:214
  21.7 0.8 constant_dynamic-slice_fusion.4
  22.6 0.6 collective-permute-start.27
  23.2 0.3 fusion.3
  23.5 9.0 %collective-permute-done.27.refs_6_ = bf16[384,128]{1,0:T(8,128)(2,1)S(1)} collective-permute-done((bf16[384,128]{1,0:T(8,128)(2,1)S(1)}, bf16[384,128]{1,0:T(8,128)(2,1)S(1)}, u32[]{:S(2)}, u32[]{:S(2)}) %collective-permute-start.27) | collective-permute-done | bytes 98336 | tf_op jit(solution)/shard_map/ppermute | solution.py:21
  32.5 3.2 %collective-permute-start.7 = (bf16[64,4608]{1,0:T(8,128)(2,1)S(1)}, bf16[64,4608]{1,0:T(8,128)(2,1)S(1)}, u32[]{:S(2)}, u32[]{:S(2)}) collective-permute-start(bf16[64,4608]{1,0:T(8,128)(2,1)S(1)} %reshape.89.refs_4_), channel_id=1, source_target_pairs={{0,24},{4,28},{8,16},{12,20},{16,8},{20,12},{24,0},{28,4},{1,25},{... | collective-permute-start | bytes 1769480 | tf_op jit(solution)/shard_map/ppermute | solution.py:21
  35.7 1.5 collective-permute-start.1
  37.2 0.9 slice_bitcast_fusion.1
  38.0 4.7 %collective-permute-done.1 = bf16[3,48,512]{2,1,0:T(8,128)(2,1)S(1)} collective-permute-done((bf16[3,48,512]{2,1,0:T(8,128)(2,1)S(1)}, bf16[3,48,512]{2,1,0:T(8,128)(2,1)S(1)}, u32[]{:S(2)}, u32[]{:S(2)}) %collective-permute-start.1) | collective-permute-done | bytes 147488 | tf_op jit(solution)/shard_map/ppermute | solution.py:215
  42.7 0.7 collective-permute-start.28
  43.4 9.8 %collective-permute-done.28.refs_7_ = bf16[384,128]{1,0:T(8,128)(2,1)S(1)} collective-permute-done((bf16[384,128]{1,0:T(8,128)(2,1)S(1)}, bf16[384,128]{1,0:T(8,128)(2,1)S(1)}, u32[]{:S(2)}, u32[]{:S(2)}) %collective-permute-start.28) | collective-permute-done | bytes 98336 | tf_op jit(solution)/shard_map/ppermute | solution.py:21
  53.2 0.3 collective-permute-start.29
  53.5 7.9 %collective-permute-done.29.refs_8_ = bf16[384,128]{1,0:T(8,128)(2,1)S(1)} collective-permute-done((bf16[384,128]{1,0:T(8,128)(2,1)S(1)}, bf16[384,128]{1,0:T(8,128)(2,1)S(1)}, u32[]{:S(2)}, u32[]{:S(2)}) %collective-permute-start.29) | collective-permute-done | bytes 98336 | tf_op jit(solution)/shard_map/ppermute | solution.py:21
  61.4 0.6 collective-permute-start.24
  62.0 0.5 collective-permute-start.25
  62.7 2.4 %collective-permute-start.26 = (bf16[480,512]{1,0:T(8,128)(2,1)S(1)}, bf16[480,512]{1,0:T(8,128)(2,1)S(1)}, u32[]{:S(2)}, u32[]{:S(2)}) collective-permute-start(bf16[480,512]{1,0:T(8,128)(2,1)S(1)} %pad_maximum_fusion.3.refs_1_), channel_id=1, source_target_pairs={{0,24},{4,28},{8,16},{12,20},{16,8},{20,12},{24,0},{28,4},{1,25},{... | collective-permute-start | bytes 1474568 | tf_op jit(solution)/shard_map/ppermute | solution.py:21
  65.1 10.4 %collective-permute-done.24.refs_2_ = bf16[480,512]{1,0:T(8,128)(2,1)S(1)} collective-permute-done((bf16[480,512]{1,0:T(8,128)(2,1)S(1)}, bf16[480,512]{1,0:T(8,128)(2,1)S(1)}, u32[]{:S(2)}, u32[]{:S(2)}) %collective-permute-start.24) | collective-permute-done | bytes 491552 | tf_op jit(solution)/shard_map/ppermute | solution.py:21
  75.6 11.3 %collective-permute-done.25.refs_3_ = bf16[480,512]{1,0:T(8,128)(2,1)S(1)} collective-permute-done((bf16[480,512]{1,0:T(8,128)(2,1)S(1)}, bf16[480,512]{1,0:T(8,128)(2,1)S(1)}, u32[]{:S(2)}, u32[]{:S(2)}) %collective-permute-start.25) | collective-permute-done | bytes 491552 | tf_op jit(solution)/shard_map/ppermute | solution.py:21
  86.9 1.5 collective-permute-start.11
  88.4 0.8 collective-permute-start.12
  89.2 4.6 %wgrad.3 = (f32[64,4608]{1,0:T(8,128)S(1)}, f32[64,4608]{1,0:T(8,128)}) custom-call(s32[1]{0:T(128)} %bitcast.refs_0_, bf16[480,512]{1,0:T(8,128)(2,1)S(1)} %pad_maximum_fusion.3.refs_1_, bf16[480,512]{1,0:T(8,128)(2,1)S(1)} %collective-permute-done.24.refs_2_, bf16[480,512]{1,0:T(8,128)(2,1)S(1)} %collective-permute-done.25.refs_3_, ...), custom_call_target="tpu_custom_call" | custom-call | tf_op jit(solution)/shard_map/wgrad/pallas_call | solution.py:156
  93.8 1.3 collective-permute-start.13
  95.1 0.8 copy-done.4
  95.9 4.0 %conv_gated.1 = (bf16[384,512]{1,0:T(8,128)(2,1)S(1)}, bf16[384,128]{1,0:T(8,128)(2,1)S(1)}, bf16[384,128]{1,0:T(8,128)(2,1)S(1)}, bf16[384,128]{1,0:T(8,128)(2,1)S(1)}, bf16[384,128]{1,0:T(8,128)(2,1)S(1)}) custom-call(s32[1]{0:T(128)} %bitcast.refs_0_, bf16[48,512]{1,0:T(8,128)(2,1)S(1)} %get-tuple-element.48.refs_1_, bf16[384,512]{1,0:T(8,128)(2,1)S(1)} %bitcast.81, ...), custom_call_target="tpu_custom_call" | custom-call | tf_op jit(solution)/shard_map/conv_gated/pallas_call | solution.py:106
  99.8 1.6 collective-permute-start.14
  101.4 0.8 collective-permute-start.15
  102.2 11.2 %collective-permute-done.12.refs_3_ = bf16[480,512]{1,0:T(8,128)(2,1)S(1)} collective-permute-done((bf16[480,512]{1,0:T(8,128)(2,1)S(1)}, bf16[480,512]{1,0:T(8,128)(2,1)S(1)}, u32[]{:S(2)}, u32[]{:S(2)}) %collective-permute-start.12) | collective-permute-done | bytes 491552 | tf_op jit(solution)/shard_map/ppermute | solution.py:21
  113.4 0.3 collective-permute-done.14.refs_6_
  113.7 1.2 collective-permute-done.15.refs_7_
  114.9 4.0 %collective-permute-done.16.refs_8_ = bf16[384,128]{1,0:T(8,128)(2,1)S(1)} collective-permute-done((bf16[384,128]{1,0:T(8,128)(2,1)S(1)}, bf16[384,128]{1,0:T(8,128)(2,1)S(1)}, u32[]{:S(2)}, u32[]{:S(2)}) %collective-permute-start.16) | collective-permute-done | bytes 98336 | tf_op jit(solution)/shard_map/ppermute | solution.py:21
  118.9 4.6 %wgrad.2 = (f32[64,4608]{1,0:T(8,128)S(1)}, f32[64,4608]{1,0:T(8,128)}) custom-call(s32[1]{0:T(128)} %bitcast.refs_0_, bf16[480,512]{1,0:T(8,128)(2,1)S(1)} %pad_maximum_fusion.2.refs_1_, bf16[480,512]{1,0:T(8,128)(2,1)S(1)} %collective-permute-done.11.refs_2_, bf16[480,512]{1,0:T(8,128)(2,1)S(1)} %collective-permute-done.12.refs_3_, ...), custom_call_target="tpu_custom_call" | custom-call | tf_op jit(solution)/shard_map/wgrad/pallas_call | solution.py:156
  123.4 0.6 fusion.21
  131.4 3.6 %collective-permute-start.9 = (bf16[48,512]{1,0:T(8,128)(2,1)S(1)}, bf16[48,512]{1,0:T(8,128)(2,1)S(1)}, u32[]{:S(2)}, u32[]{:S(2)}) collective-permute-start(bf16[48,512]{1,0:T(8,128)(2,1)S(1)} %get-tuple-element.45), channel_id=1, source_target_pairs={{0,1},{1,2},{2,3},{4,5},{5,6},{6,7},{8,9},{9,10},{10,11},{12,13},{... | collective-permute-start | bytes 147464 | tf_op jit(solution)/shard_map/ppermute | solution.py:214
  135.0 1.5 collective-permute-start.10
  136.6 1.4 add.101
  138.0 4.0 %collective-permute-start.33 = (bf16[16,4608]{1,0:T(8,128)(2,1)S(1)}, bf16[16,4608]{1,0:T(8,128)(2,1)S(1)}, u32[]{:S(2)}, u32[]{:S(2)}) collective-permute-start(bf16[16,4608]{1,0:T(8,128)(2,1)S(1)} %get-tuple-element.25), channel_id=1, source_target_pairs={{0,3},{1,2},{2,1},{3,0},{4,7},{5,6},{6,5},{7,4},{8,11},{9,10},{10,... | collective-permute-start | bytes 442376 | tf_op jit(solution)/shard_map/ppermute | solution.py:21
  142.2 0.5 collective-permute-start.31
  142.7 1.4 add.84
  144.2 2.7 %collective-permute-done.33 = bf16[16,4608]{1,0:T(8,128)(2,1)S(1)} collective-permute-done((bf16[16,4608]{1,0:T(8,128)(2,1)S(1)}, bf16[16,4608]{1,0:T(8,128)(2,1)S(1)}, u32[]{:S(2)}, u32[]{:S(2)}) %collective-permute-start.33) | collective-permute-done | bytes 147488 | tf_op jit(solution)/shard_map/ppermute | solution.py:21
  146.8 3.9 %collective-permute-start.20 = (bf16[16,4608]{1,0:T(8,128)(2,1)S(1)}, bf16[16,4608]{1,0:T(8,128)(2,1)S(1)}, u32[]{:S(2)}, u32[]{:S(2)}) collective-permute-start(bf16[16,4608]{1,0:T(8,128)(2,1)S(1)} %get-tuple-element.28), channel_id=1, source_target_pairs={{0,3},{1,2},{2,1},{3,0},{4,7},{5,6},{6,5},{7,4},{8,11},{9,10},{10,... | collective-permute-start | bytes 442376 | tf_op jit(solution)/shard_map/ppermute | solution.py:21
  150.7 8.1 %collective-permute-done.32 = bf16[16,4608]{1,0:T(8,128)(2,1)S(1)} collective-permute-done((bf16[16,4608]{1,0:T(8,128)(2,1)S(1)}, bf16[16,4608]{1,0:T(8,128)(2,1)S(1)}, u32[]{:S(2)}, u32[]{:S(2)}) %collective-permute-start.32) | collective-permute-done | bytes 147488 | tf_op jit(solution)/shard_map/ppermute | solution.py:21
  158.8 3.5 %collective-permute-start.18 = (bf16[16,4608]{1,0:T(8,128)(2,1)S(1)}, bf16[16,4608]{1,0:T(8,128)(2,1)S(1)}, u32[]{:S(2)}, u32[]{:S(2)}) collective-permute-start(bf16[16,4608]{1,0:T(8,128)(2,1)S(1)} %get-tuple-element.27), channel_id=1, source_target_pairs={{0,1},{1,0},{2,3},{3,2},{4,5},{5,4},{6,7},{7,6},{8,9},{9,8},{10,11... | collective-permute-start | bytes 442376 | tf_op jit(solution)/shard_map/ppermute | solution.py:21
  162.3 1.0 collective-permute-start.36
  163.3 8.1 %collective-permute-done.19 = bf16[16,4608]{1,0:T(8,128)(2,1)S(1)} collective-permute-done((bf16[16,4608]{1,0:T(8,128)(2,1)S(1)}, bf16[16,4608]{1,0:T(8,128)(2,1)S(1)}, u32[]{:S(2)}, u32[]{:S(2)}) %collective-permute-start.19) | collective-permute-done | bytes 147488 | tf_op jit(solution)/shard_map/ppermute | solution.py:21
  171.4 3.1 %collective-permute-start.34 = (bf16[16,4608]{1,0:T(8,128)(2,1)S(1)}, bf16[16,4608]{1,0:T(8,128)(2,1)S(1)}, u32[]{:S(2)}, u32[]{:S(2)}) collective-permute-start(bf16[16,4608]{1,0:T(8,128)(2,1)S(1)} %fusion.10), channel_id=1, source_target_pairs={{0,1},{1,0},{2,3},{3,2},{4,5},{5,4},{6,7},{7,6},{8,9},{9,8},{10,11... | collective-permute-start | bytes 442376 | tf_op jit(solution)/shard_map/ppermute | solution.py:21
  174.6 1.4 collective-permute-start.23
  176.0 8.1 %collective-permute-done.35 = bf16[16,4608]{1,0:T(8,128)(2,1)S(1)} collective-permute-done((bf16[16,4608]{1,0:T(8,128)(2,1)S(1)}, bf16[16,4608]{1,0:T(8,128)(2,1)S(1)}, u32[]{:S(2)}, u32[]{:S(2)}) %collective-permute-start.35) | collective-permute-done | bytes 147488 | tf_op jit(solution)/shard_map/ppermute | solution.py:21
  184.1 3.1 %collective-permute-start.21 = (bf16[16,4608]{1,0:T(8,128)(2,1)S(1)}, bf16[16,4608]{1,0:T(8,128)(2,1)S(1)}, u32[]{:S(2)}, u32[]{:S(2)}) collective-permute-start(bf16[16,4608]{1,0:T(8,128)(2,1)S(1)} %fusion.13), channel_id=1, source_target_pairs={{0,1},{1,0},{2,3},{3,2},{4,5},{5,4},{6,7},{7,6},{8,9},{9,8},{10,11... | collective-permute-start | bytes 442376 | tf_op jit(solution)/shard_map/ppermute | solution.py:21
  187.2 6.2 %collective-permute-done.22 = bf16[16,4608]{1,0:T(8,128)(2,1)S(1)} collective-permute-done((bf16[16,4608]{1,0:T(8,128)(2,1)S(1)}, bf16[16,4608]{1,0:T(8,128)(2,1)S(1)}, u32[]{:S(2)}, u32[]{:S(2)}) %collective-permute-start.22) | collective-permute-done | bytes 147488 | tf_op jit(solution)/shard_map/ppermute | solution.py:21
  194.5 0.5 maximum_convert_fusion
  195.0 0.5 maximum_convert_fusion.1
  195.5 1.4 copy.20
  196.9 1.4 copy.21
  198.3 2.3 %copy-done = bf16[512,4608]{1,0:T(8,128)(2,1)S(1)} copy-done((bf16[512,4608]{1,0:T(8,128)(2,1)S(1)}, bf16[512,4608]{1,0:T(8,128)(2,1)}, u32[]{:S(2)}) %copy-start) | copy-done | bytes 4718616
  200.6 3.5 %conv_plain.1 = f32[384,512]{1,0:T(8,128)} custom-call(s32[1]{0:T(128)} %bitcast.refs_0_, bf16[48,512]{1,0:T(8,128)(2,1)S(1)} %collective-permute-done.9.refs_1_, bf16[384,512]{1,0:T(8,128)(2,1)S(1)} %get-tuple-element.12.refs_2_, bf16[48,512]{1,0:T(8,128)(2,1)S(1)} %collective-permute-done.10.refs_3_, bf16[512,4608]{1,0:T(8,128)(2,1)S(1)} %copy-done), custom_call_target="tpu_custom_call" | custom-call | tf_op jit(solution)/shard_map/conv_plain/pallas_call | solution.py:106
  (72 shorter events, 2.0 us)
Async XLA Ops:
  7.2 7.1 %copy-start.5 = (bf16[64,3,3,512]{3,0,2,1:T(8,128)(2,1)S(1)}, bf16[64,3,3,512]{3,0,2,1:T(8,128)(2,1)}, u32[]{:S(2)}) copy-start(bf16[64,3,3,512]{3,0,2,1:T(8,128)(2,1)} %param.8) | copy-start | bytes 1769476
  7.2 191.1 %all-gather.2.cloned.1.call-start = ((), (), s32[]{:S(2)}) async-start(), calls=%async_computation | async-start | bytes 5308416 | tf_op jit(solution)/shard_map/all_gather | solution.py:207
  9.7 52.3 %collective-permute-start.2 = (bf16[64,4608]{1,0:T(8,128)(2,1)S(1)}, bf16[64,4608]{1,0:T(8,128)(2,1)S(1)}, u32[]{:S(2)}, u32[]{:S(2)}) collective-permute-start(bf16[64,4608]{1,0:T(8,128)(2,1)S(1)} %reshape.89.refs_4_), channel_id=1, source_target_pairs={{0,4},{4,0},{8,12},{12,8},{16,20},{20,16},{24,28},{28,24},{1,5},{5... | collective-permute-start | bytes 1769480 | tf_op jit(solution)/shard_map/ppermute | solution.py:21
  10.2 51.8 %collective-permute-start.3 = (bf16[64,4608]{1,0:T(8,128)(2,1)S(1)}, bf16[64,4608]{1,0:T(8,128)(2,1)}, u32[]{:S(2)}, u32[]{:S(2)}) collective-permute-start(bf16[64,4608]{1,0:T(8,128)(2,1)S(1)} %reshape.89.refs_4_), channel_id=1, source_target_pairs={{0,8},{4,12},{8,0},{12,4},{16,24},{20,28},{24,16},{28,20},{1,9},{5... | collective-permute-start | bytes 1769480 | tf_op jit(solution)/shard_map/ppermute | solution.py:21
  12.8 49.8 %collective-permute-start.5 = (bf16[64,4608]{1,0:T(8,128)(2,1)S(1)}, bf16[64,4608]{1,0:T(8,128)(2,1)}, u32[]{:S(2)}, u32[]{:S(2)}) collective-permute-start(bf16[64,4608]{1,0:T(8,128)(2,1)S(1)} %reshape.89.refs_4_), channel_id=1, source_target_pairs={{0,16},{4,20},{8,24},{12,28},{16,0},{20,4},{24,8},{28,12},{1,17},{... | collective-permute-start | bytes 1769480 | tf_op jit(solution)/shard_map/ppermute | solution.py:21
  14.8 1.6 copy-start.1
  14.8 1.9 copy-start.2
  14.8 1.9 copy-start.3
  17.5 18.3 %collective-permute-start = (bf16[3,48,512]{2,1,0:T(8,128)(2,1)}, bf16[3,48,512]{2,1,0:T(8,128)(2,1)}, u32[]{:S(2)}, u32[]{:S(2)}) collective-permute-start(bf16[3,48,512]{2,1,0:T(8,128)(2,1)} %get-tuple-element.31), channel_id=1, source_target_pairs={{0,1},{1,2},{2,3},{4,5},{5,6},{6,7},{8,9},{9,10},{10,11},{12,13},{... | collective-permute-start | bytes 442376 | tf_op jit(solution)/shard_map/ppermute | solution.py:214
  22.5 13.2 %copy-start.6 = (bf16[3,48,512]{2,1,0:T(8,128)(2,1)S(1)}, bf16[3,48,512]{2,1,0:T(8,128)(2,1)}, u32[]{:S(2)}) copy-start(bf16[3,48,512]{2,1,0:T(8,128)(2,1)} %get-tuple-element.30) | copy-start | bytes 442372
  22.6 9.9 %collective-permute-start.27 = (bf16[384,128]{1,0:T(8,128)(2,1)S(1)}, bf16[384,128]{1,0:T(8,128)(2,1)S(1)}, u32[]{:S(2)}, u32[]{:S(2)}) collective-permute-start(bf16[384,128]{1,0:T(8,128)(2,1)S(1)} %bitcast.100), channel_id=1, source_target_pairs={{0,8},{4,12},{8,0},{12,4},{16,24},{20,28},{24,16},{28,20},{1,9},{5... | collective-permute-start | bytes 294920 | tf_op jit(solution)/shard_map/ppermute | solution.py:21
  32.5 30.3 %collective-permute-start.7 = (bf16[64,4608]{1,0:T(8,128)(2,1)S(1)}, bf16[64,4608]{1,0:T(8,128)(2,1)S(1)}, u32[]{:S(2)}, u32[]{:S(2)}) collective-permute-start(bf16[64,4608]{1,0:T(8,128)(2,1)S(1)} %reshape.89.refs_4_), channel_id=1, source_target_pairs={{0,24},{4,28},{8,16},{12,20},{16,8},{20,12},{24,0},{28,4},{1,25},{... | collective-permute-start | bytes 1769480 | tf_op jit(solution)/shard_map/ppermute | solution.py:21
  35.7 7.0 %collective-permute-start.1 = (bf16[3,48,512]{2,1,0:T(8,128)(2,1)S(1)}, bf16[3,48,512]{2,1,0:T(8,128)(2,1)S(1)}, u32[]{:S(2)}, u32[]{:S(2)}) collective-permute-start(bf16[3,48,512]{2,1,0:T(8,128)(2,1)S(1)} %copy-done.6), channel_id=1, source_target_pairs={{1,0},{2,1},{3,2},{5,4},{6,5},{7,6},{9,8},{10,9},{11,10},{13,12},{... | collective-permute-start | bytes 442376 | tf_op jit(solution)/shard_map/ppermute | solution.py:215
  42.7 10.5 %collective-permute-start.28 = (bf16[384,128]{1,0:T(8,128)(2,1)S(1)}, bf16[384,128]{1,0:T(8,128)(2,1)S(1)}, u32[]{:S(2)}, u32[]{:S(2)}) collective-permute-start(bf16[384,128]{1,0:T(8,128)(2,1)S(1)} %bitcast.99), channel_id=1, source_target_pairs={{0,16},{4,20},{8,24},{12,28},{16,0},{20,4},{24,8},{28,12},{1,17},{... | collective-permute-start | bytes 294920 | tf_op jit(solution)/shard_map/ppermute | solution.py:21
  53.2 8.2 %collective-permute-start.29 = (bf16[384,128]{1,0:T(8,128)(2,1)S(1)}, bf16[384,128]{1,0:T(8,128)(2,1)S(1)}, u32[]{:S(2)}, u32[]{:S(2)}) collective-permute-start(bf16[384,128]{1,0:T(8,128)(2,1)S(1)} %bitcast.98), channel_id=1, source_target_pairs={{0,24},{4,28},{8,16},{12,20},{16,8},{20,12},{24,0},{28,4},{1,25},{... | collective-permute-start | bytes 294920 | tf_op jit(solution)/shard_map/ppermute | solution.py:21
  61.4 14.2 %collective-permute-start.24 = (bf16[480,512]{1,0:T(8,128)(2,1)S(1)}, bf16[480,512]{1,0:T(8,128)(2,1)S(1)}, u32[]{:S(2)}, u32[]{:S(2)}) collective-permute-start(bf16[480,512]{1,0:T(8,128)(2,1)S(1)} %pad_maximum_fusion.3.refs_1_), channel_id=1, source_target_pairs={{0,8},{4,12},{8,0},{12,4},{16,24},{20,28},{24,16},{28,20},{1,9},{5... | collective-permute-start | bytes 1474568 | tf_op jit(solution)/shard_map/ppermute | solution.py:21
  62.0 31.8 %collective-permute-start.4 = (bf16[64,4608]{1,0:T(8,128)(2,1)}, bf16[64,4608]{1,0:T(8,128)(2,1)S(1)}, u32[]{:S(2)}, u32[]{:S(2)}) collective-permute-start(bf16[64,4608]{1,0:T(8,128)(2,1)} %collective-permute-done.3.refs_6_), channel_id=1, source_target_pairs={{0,4},{4,0},{8,12},{12,8},{16,20},{20,16},{24,28},{28,24},{1,5},{5... | collective-permute-start | bytes 1769480 | tf_op jit(solution)/shard_map/ppermute | solution.py:21
  62.0 24.9 %collective-permute-start.25 = (bf16[480,512]{1,0:T(8,128)(2,1)S(1)}, bf16[480,512]{1,0:T(8,128)(2,1)S(1)}, u32[]{:S(2)}, u32[]{:S(2)}) collective-permute-start(bf16[480,512]{1,0:T(8,128)(2,1)S(1)} %pad_maximum_fusion.3.refs_1_), channel_id=1, source_target_pairs={{0,16},{4,20},{8,24},{12,28},{16,0},{20,4},{24,8},{28,12},{1,17},{... | collective-permute-start | bytes 1474568 | tf_op jit(solution)/shard_map/ppermute | solution.py:21
  62.6 31.2 %collective-permute-start.6 = (bf16[64,4608]{1,0:T(8,128)(2,1)}, bf16[64,4608]{1,0:T(8,128)(2,1)S(1)}, u32[]{:S(2)}, u32[]{:S(2)}) collective-permute-start(bf16[64,4608]{1,0:T(8,128)(2,1)} %collective-permute-done.5.refs_8_), channel_id=1, source_target_pairs={{0,4},{4,0},{8,12},{12,8},{16,20},{20,16},{24,28},{28,24},{1,5},{5... | collective-permute-start | bytes 1769480 | tf_op jit(solution)/shard_map/ppermute | solution.py:21
  62.7 25.7 %collective-permute-start.26 = (bf16[480,512]{1,0:T(8,128)(2,1)S(1)}, bf16[480,512]{1,0:T(8,128)(2,1)S(1)}, u32[]{:S(2)}, u32[]{:S(2)}) collective-permute-start(bf16[480,512]{1,0:T(8,128)(2,1)S(1)} %pad_maximum_fusion.3.refs_1_), channel_id=1, source_target_pairs={{0,24},{4,28},{8,16},{12,20},{16,8},{20,12},{24,0},{28,4},{1,25},{... | collective-permute-start | bytes 1474568 | tf_op jit(solution)/shard_map/ppermute | solution.py:21
  75.6 19.5 %collective-permute-start.8 = (bf16[64,4608]{1,0:T(8,128)(2,1)S(1)}, bf16[64,4608]{1,0:T(8,128)(2,1)S(1)}, u32[]{:S(2)}, u32[]{:S(2)}) collective-permute-start(bf16[64,4608]{1,0:T(8,128)(2,1)S(1)} %collective-permute-done.7.refs_10_), channel_id=1, source_target_pairs={{0,4},{4,0},{8,12},{12,8},{16,20},{20,16},{24,28},{28,24},{1,5},{5... | collective-permute-start | bytes 1769480 | tf_op jit(solution)/shard_map/ppermute | solution.py:21
  86.9 14.5 %collective-permute-start.11 = (bf16[480,512]{1,0:T(8,128)(2,1)S(1)}, bf16[480,512]{1,0:T(8,128)(2,1)S(1)}, u32[]{:S(2)}, u32[]{:S(2)}) collective-permute-start(bf16[480,512]{1,0:T(8,128)(2,1)S(1)} %pad_maximum_fusion.2.refs_1_), channel_id=1, source_target_pairs={{0,8},{4,12},{8,0},{12,4},{16,24},{20,28},{24,16},{28,20},{1,9},{5... | collective-permute-start | bytes 1474568 | tf_op jit(solution)/shard_map/ppermute | solution.py:21
  88.4 25.0 %collective-permute-start.12 = (bf16[480,512]{1,0:T(8,128)(2,1)S(1)}, bf16[480,512]{1,0:T(8,128)(2,1)S(1)}, u32[]{:S(2)}, u32[]{:S(2)}) collective-permute-start(bf16[480,512]{1,0:T(8,128)(2,1)S(1)} %pad_maximum_fusion.2.refs_1_), channel_id=1, source_target_pairs={{0,16},{4,20},{8,24},{12,28},{16,0},{20,4},{24,8},{28,12},{1,17},{... | collective-permute-start | bytes 1474568 | tf_op jit(solution)/shard_map/ppermute | solution.py:21
  93.8 42.8 %collective-permute-start.30 = (f32[64,4608]{1,0:T(8,128)}, f32[64,4608]{1,0:T(8,128)}, u32[]{:S(2)}, u32[]{:S(2)}) collective-permute-start(f32[64,4608]{1,0:T(8,128)} %get-tuple-element.20), channel_id=1, source_target_pairs={{0,4},{4,0},{8,12},{12,8},{16,20},{20,16},{24,28},{28,24},{1,5},{5... | collective-permute-start | bytes 3538952 | tf_op jit(solution)/shard_map/ppermute | solution.py:21
  93.8 19.6 %collective-permute-start.13 = (bf16[480,512]{1,0:T(8,128)(2,1)S(1)}, bf16[480,512]{1,0:T(8,128)(2,1)S(1)}, u32[]{:S(2)}, u32[]{:S(2)}) collective-permute-start(bf16[480,512]{1,0:T(8,128)(2,1)S(1)} %pad_maximum_fusion.2.refs_1_), channel_id=1, source_target_pairs={{0,24},{4,28},{8,16},{12,20},{16,8},{20,12},{24,0},{28,4},{1,25},{... | collective-permute-start | bytes 1474568 | tf_op jit(solution)/shard_map/ppermute | solution.py:21
  95.1 0.8 copy-start.4
  99.8 13.8 %collective-permute-start.14 = (bf16[384,128]{1,0:T(8,128)(2,1)S(1)}, bf16[384,128]{1,0:T(8,128)(2,1)S(1)}, u32[]{:S(2)}, u32[]{:S(2)}) collective-permute-start(bf16[384,128]{1,0:T(8,128)(2,1)S(1)} %get-tuple-element.14), channel_id=1, source_target_pairs={{0,8},{4,12},{8,0},{12,4},{16,24},{20,28},{24,16},{28,20},{1,9},{5... | collective-permute-start | bytes 294920 | tf_op jit(solution)/shard_map/ppermute | solution.py:21
  101.4 13.5 %collective-permute-start.15 = (bf16[384,128]{1,0:T(8,128)(2,1)S(1)}, bf16[384,128]{1,0:T(8,128)(2,1)S(1)}, u32[]{:S(2)}, u32[]{:S(2)}) collective-permute-start(bf16[384,128]{1,0:T(8,128)(2,1)S(1)} %get-tuple-element.15), channel_id=1, source_target_pairs={{0,16},{4,20},{8,24},{12,28},{16,0},{20,4},{24,8},{28,12},{1,17},{... | collective-permute-start | bytes 294920 | tf_op jit(solution)/shard_map/ppermute | solution.py:21
  113.4 5.5 %collective-permute-start.16 = (bf16[384,128]{1,0:T(8,128)(2,1)S(1)}, bf16[384,128]{1,0:T(8,128)(2,1)S(1)}, u32[]{:S(2)}, u32[]{:S(2)}) collective-permute-start(bf16[384,128]{1,0:T(8,128)(2,1)S(1)} %get-tuple-element.16), channel_id=1, source_target_pairs={{0,24},{4,28},{8,16},{12,20},{16,8},{20,12},{24,0},{28,4},{1,25},{... | collective-permute-start | bytes 294920 | tf_op jit(solution)/shard_map/ppermute | solution.py:21
  123.4 18.8 %collective-permute-start.17 = (f32[64,4608]{1,0:T(8,128)}, f32[64,4608]{1,0:T(8,128)}, u32[]{:S(2)}, u32[]{:S(2)}) collective-permute-start(f32[64,4608]{1,0:T(8,128)} %get-tuple-element.18), channel_id=1, source_target_pairs={{0,4},{4,0},{8,12},{12,8},{16,20},{20,16},{24,28},{28,24},{1,5},{5... | collective-permute-start | bytes 3538952 | tf_op jit(solution)/shard_map/ppermute | solution.py:21
  131.4 66.8 %collective-permute-start.9 = (bf16[48,512]{1,0:T(8,128)(2,1)S(1)}, bf16[48,512]{1,0:T(8,128)(2,1)S(1)}, u32[]{:S(2)}, u32[]{:S(2)}) collective-permute-start(bf16[48,512]{1,0:T(8,128)(2,1)S(1)} %get-tuple-element.45), channel_id=1, source_target_pairs={{0,1},{1,2},{2,3},{4,5},{5,6},{6,7},{8,9},{9,10},{10,11},{12,13},{... | collective-permute-start | bytes 147464 | tf_op jit(solution)/shard_map/ppermute | solution.py:214
  135.0 63.2 %collective-permute-start.10 = (bf16[48,512]{1,0:T(8,128)(2,1)S(1)}, bf16[48,512]{1,0:T(8,128)(2,1)S(1)}, u32[]{:S(2)}, u32[]{:S(2)}) collective-permute-start(bf16[48,512]{1,0:T(8,128)(2,1)S(1)} %get-tuple-element.44), channel_id=1, source_target_pairs={{1,0},{2,1},{3,2},{5,4},{6,5},{7,6},{9,8},{10,9},{11,10},{13,12},{... | collective-permute-start | bytes 147464 | tf_op jit(solution)/shard_map/ppermute | solution.py:215
  138.0 8.8 %collective-permute-start.33 = (bf16[16,4608]{1,0:T(8,128)(2,1)S(1)}, bf16[16,4608]{1,0:T(8,128)(2,1)S(1)}, u32[]{:S(2)}, u32[]{:S(2)}) collective-permute-start(bf16[16,4608]{1,0:T(8,128)(2,1)S(1)} %get-tuple-element.25), channel_id=1, source_target_pairs={{0,3},{1,2},{2,1},{3,0},{4,7},{5,6},{6,5},{7,4},{8,11},{9,10},{10,... | collective-permute-start | bytes 442376 | tf_op jit(solution)/shard_map/ppermute | solution.py:21
  142.1 16.7 %collective-permute-start.32 = (bf16[16,4608]{1,0:T(8,128)(2,1)S(1)}, bf16[16,4608]{1,0:T(8,128)(2,1)S(1)}, u32[]{:S(2)}, u32[]{:S(2)}) collective-permute-start(bf16[16,4608]{1,0:T(8,128)(2,1)S(1)} %get-tuple-element.26), channel_id=1, source_target_pairs={{0,2},{1,3},{2,0},{3,1},{4,6},{5,7},{6,4},{7,5},{8,10},{9,11},{10,... | collective-permute-start | bytes 442376 | tf_op jit(solution)/shard_map/ppermute | solution.py:21
  142.2 16.6 %collective-permute-start.31 = (bf16[16,4608]{1,0:T(8,128)(2,1)S(1)}, bf16[16,4608]{1,0:T(8,128)(2,1)S(1)}, u32[]{:S(2)}, u32[]{:S(2)}) collective-permute-start(bf16[16,4608]{1,0:T(8,128)(2,1)S(1)} %get-tuple-element.24), channel_id=1, source_target_pairs={{0,1},{1,0},{2,3},{3,2},{4,5},{5,4},{6,7},{7,6},{8,9},{9,8},{10,11... | collective-permute-start | bytes 442376 | tf_op jit(solution)/shard_map/ppermute | solution.py:21
  146.8 15.5 %collective-permute-start.20 = (bf16[16,4608]{1,0:T(8,128)(2,1)S(1)}, bf16[16,4608]{1,0:T(8,128)(2,1)S(1)}, u32[]{:S(2)}, u32[]{:S(2)}) collective-permute-start(bf16[16,4608]{1,0:T(8,128)(2,1)S(1)} %get-tuple-element.28), channel_id=1, source_target_pairs={{0,3},{1,2},{2,1},{3,0},{4,7},{5,6},{6,5},{7,4},{8,11},{9,10},{10,... | collective-permute-start | bytes 442376 | tf_op jit(solution)/shard_map/ppermute | solution.py:21
  158.8 12.6 %collective-permute-start.19 = (bf16[16,4608]{1,0:T(8,128)(2,1)S(1)}, bf16[16,4608]{1,0:T(8,128)(2,1)S(1)}, u32[]{:S(2)}, u32[]{:S(2)}) collective-permute-start(bf16[16,4608]{1,0:T(8,128)(2,1)S(1)} %get-tuple-element.29), channel_id=1, source_target_pairs={{0,2},{1,3},{2,0},{3,1},{4,6},{5,7},{6,4},{7,5},{8,10},{9,11},{10,... | collective-permute-start | bytes 442376 | tf_op jit(solution)/shard_map/ppermute | solution.py:21
  158.8 12.7 %collective-permute-start.18 = (bf16[16,4608]{1,0:T(8,128)(2,1)S(1)}, bf16[16,4608]{1,0:T(8,128)(2,1)S(1)}, u32[]{:S(2)}, u32[]{:S(2)}) collective-permute-start(bf16[16,4608]{1,0:T(8,128)(2,1)S(1)} %get-tuple-element.27), channel_id=1, source_target_pairs={{0,1},{1,0},{2,3},{3,2},{4,5},{5,4},{6,7},{7,6},{8,9},{9,8},{10,11... | collective-permute-start | bytes 442376 | tf_op jit(solution)/shard_map/ppermute | solution.py:21
  162.3 12.2 %collective-permute-start.36 = (bf16[16,4608]{1,0:T(8,128)(2,1)S(1)}, bf16[16,4608]{1,0:T(8,128)(2,1)S(1)}, u32[]{:S(2)}, u32[]{:S(2)}) collective-permute-start(bf16[16,4608]{1,0:T(8,128)(2,1)S(1)} %fusion.10), channel_id=1, source_target_pairs={{0,3},{1,2},{2,1},{3,0},{4,7},{5,6},{6,5},{7,4},{8,11},{9,10},{10,... | collective-permute-start | bytes 442376 | tf_op jit(solution)/shard_map/ppermute | solution.py:21
  171.4 12.6 %collective-permute-start.35 = (bf16[16,4608]{1,0:T(8,128)(2,1)S(1)}, bf16[16,4608]{1,0:T(8,128)(2,1)S(1)}, u32[]{:S(2)}, u32[]{:S(2)}) collective-permute-start(bf16[16,4608]{1,0:T(8,128)(2,1)S(1)} %fusion.10), channel_id=1, source_target_pairs={{0,2},{1,3},{2,0},{3,1},{4,6},{5,7},{6,4},{7,5},{8,10},{9,11},{10,... | collective-permute-start | bytes 442376 | tf_op jit(solution)/shard_map/ppermute | solution.py:21
  171.4 12.6 %collective-permute-start.34 = (bf16[16,4608]{1,0:T(8,128)(2,1)S(1)}, bf16[16,4608]{1,0:T(8,128)(2,1)S(1)}, u32[]{:S(2)}, u32[]{:S(2)}) collective-permute-start(bf16[16,4608]{1,0:T(8,128)(2,1)S(1)} %fusion.10), channel_id=1, source_target_pairs={{0,1},{1,0},{2,3},{3,2},{4,5},{5,4},{6,7},{7,6},{8,9},{9,8},{10,11... | collective-permute-start | bytes 442376 | tf_op jit(solution)/shard_map/ppermute | solution.py:21
  174.6 12.6 %collective-permute-start.23 = (bf16[16,4608]{1,0:T(8,128)(2,1)S(1)}, bf16[16,4608]{1,0:T(8,128)(2,1)S(1)}, u32[]{:S(2)}, u32[]{:S(2)}) collective-permute-start(bf16[16,4608]{1,0:T(8,128)(2,1)S(1)} %fusion.13), channel_id=1, source_target_pairs={{0,3},{1,2},{2,1},{3,0},{4,7},{5,6},{6,5},{7,4},{8,11},{9,10},{10,... | collective-permute-start | bytes 442376 | tf_op jit(solution)/shard_map/ppermute | solution.py:21
  184.1 9.3 %collective-permute-start.22 = (bf16[16,4608]{1,0:T(8,128)(2,1)S(1)}, bf16[16,4608]{1,0:T(8,128)(2,1)S(1)}, u32[]{:S(2)}, u32[]{:S(2)}) collective-permute-start(bf16[16,4608]{1,0:T(8,128)(2,1)S(1)} %fusion.13), channel_id=1, source_target_pairs={{0,2},{1,3},{2,0},{3,1},{4,6},{5,7},{6,4},{7,5},{8,10},{9,11},{10,... | collective-permute-start | bytes 442376 | tf_op jit(solution)/shard_map/ppermute | solution.py:21
  184.1 9.4 %collective-permute-start.21 = (bf16[16,4608]{1,0:T(8,128)(2,1)S(1)}, bf16[16,4608]{1,0:T(8,128)(2,1)S(1)}, u32[]{:S(2)}, u32[]{:S(2)}) collective-permute-start(bf16[16,4608]{1,0:T(8,128)(2,1)S(1)} %fusion.13), channel_id=1, source_target_pairs={{0,1},{1,0},{2,3},{3,2},{4,5},{5,4},{6,7},{7,6},{8,9},{9,8},{10,11... | collective-permute-start | bytes 442376 | tf_op jit(solution)/shard_map/ppermute | solution.py:21
  198.3 2.3 %copy-start = (bf16[512,4608]{1,0:T(8,128)(2,1)S(1)}, bf16[512,4608]{1,0:T(8,128)(2,1)}, u32[]{:S(2)}) copy-start(bf16[512,4608]{1,0:T(8,128)(2,1)} %all-gather.2.cloned.1.call-done.refs_4_) | copy-start | bytes 14155780
Sparse Core Ops, SparseCore 0:
  16.6 51.5 all-gather.1

commit v2 on v1

v2 whole, which is shorter than its diff:
```python
import jax
import jax.numpy as jnp
from jax import lax
from jax.experimental import pallas as pl
from jax.experimental.pallas import tpu as pltpu
from jax.sharding import PartitionSpec as P

BF = jnp.bfloat16
F32 = jnp.float32
PARAMS = pltpu.CompilerParams(vmem_limit_bytes=48 * 1024 * 1024)
ANY = pl.BlockSpec(memory_space=pl.ANY)
VM = pl.BlockSpec(memory_space=pltpu.VMEM)
SM = pl.BlockSpec(memory_space=pltpu.SMEM)


def xor_pairs(count, k):
    return [(i, i ^ k) for i in range(count)]


def swap(value, axis, k):
    return lax.ppermute(value, axis, xor_pairs(lax.axis_size(axis), k))


def shifted(flat, width):
    rows = flat.shape[0]
    wide = flat.astype(F32)
    col = lax.broadcasted_iota(jnp.int32, wide.shape, 0) % width
    left = jnp.where(col == 0, 0.0, pltpu.roll(wide, 1, 0)).astype(BF)
    right = jnp.where(col == width - 1, 0.0, pltpu.roll(wide, rows - 1, 0)).astype(BF)
    return left, flat, right


def products(field, kernel, n, c, width):
    acc = None
    for r in range(3):
        for s in range(3):
            tap = 3 * r + s
            lhs = field[s, (2 - r) * width : (2 - r) * width + n, :]
            part = jnp.dot(lhs, kernel[:, tap * c : (tap + 1) * c], preferred_element_type=F32)
            acc = part if acc is None else acc + part
    return acc


def gated_kernel(count, width, pieces):
    def body(*refs):
        ids, gup, g, gdown, hup, h, hdown = refs[:7]
        weights = refs[7 : 7 + count]
        out, parts, field, kernel, sems = refs[7 + count :]
        copies = []
        for k in range(count):
            rows = weights[k].shape[0]
            start = pl.multiple_of((ids[0] ^ k) * rows, rows)
            copies.append(
                pltpu.make_async_copy(weights[k], kernel.at[pl.ds(start, rows)], sems.at[k])
            )
            copies[-1].start()
        left, same, right = shifted(
            jnp.concatenate([gup[...], g[...], gdown[...]], axis=0), width
        )
        field[0] = right
        field[1] = same
        field[2] = left
        for copy in copies:
            copy.wait()
        n, c = out.shape
        acc = products(field, kernel, n, c, width)
        hf = jnp.concatenate([hup[...], h[...], hdown[...]], axis=0).astype(F32)
        sig = jax.nn.sigmoid(hf)
        acc = acc * (sig * (1.0 + hf * (1.0 - sig)))
        row = lax.broadcasted_iota(jnp.int32, acc.shape, 0)
        inside = jnp.logical_and(
            jnp.logical_or(row >= width, ids[1] > 0),
            jnp.logical_or(row < n - width, ids[2] > 0),
        )
        res = jnp.where(inside, acc, 0.0).astype(BF)
        out[...] = res
        w = c // pieces
        for t in range(pieces):
            parts[t] = res[:, t * w : (t + 1) * w]

    return body


def gated(ids, gup, g, gdown, hup, h, hdown, weights, width, pieces):
    n, c = h.shape
    count = len(weights)
    rows = n + 2 * width
    return pl.pallas_call(
        gated_kernel(count, width, pieces),
        out_shape=[
            jax.ShapeDtypeStruct((rows, c), BF),
            jax.ShapeDtypeStruct((pieces, rows, c // pieces), BF),
        ],
        in_specs=[SM] + [VM] * 6 + [ANY] * count,
        out_specs=[VM, VM],
        scratch_shapes=[
            pltpu.VMEM((3, rows + 2 * width, c), BF),
            pltpu.VMEM((weights[0].shape[0] * count, weights[0].shape[1]), BF),
            pltpu.SemaphoreType.DMA((count,)),
        ],
        compiler_params=PARAMS,
        name="gated",
    )(ids, gup, g, gdown, hup, h, hdown, *weights)


def plain_kernel(width):
    def body(ext, weight, out, field):
        left, same, right = shifted(ext[...], width)
        field[0] = right
        field[1] = same
        field[2] = left
        n, c = out.shape
        out[...] = products(field, weight, n, c, width)

    return body


def plain(ext, weight, width):
    rows, c = ext.shape
    return pl.pallas_call(
        plain_kernel(width),
        out_shape=jax.ShapeDtypeStruct((rows - 2 * width, c), F32),
        in_specs=[VM, VM],
        out_specs=VM,
        scratch_shapes=[pltpu.VMEM((3, rows, c), BF)],
        compiler_params=PARAMS,
        name="plain",
    )(ext, weight)


def wgrad_kernel(width):
    def body(ids, fields, cots, keep, send, lhs, acc):
        count, rows, w = cots.shape
        n = rows - 2 * width
        for i in range(count):
            left, same, right = shifted(cots[i], width)
            for s, part in enumerate((right, same, left)):
                for r in range(3):
                    tap = 3 * r + s
                    lhs[tap * w : (tap + 1) * w, i * n : (i + 1) * n] = part[
                        (2 - r) * width : (2 - r) * width + n, :
                    ].T
        for tap in range(9):
            acc[tap] = jnp.dot(
                lhs[tap * w : (tap + 1) * w, :], fields[...], preferred_element_type=F32
            )
        half = w // 2
        mine = ids[0] & 1
        keep[...] = acc[:, pl.ds(pl.multiple_of(mine * half, half), half), :]
        send[...] = acc[:, pl.ds(pl.multiple_of((1 - mine) * half, half), half), :]

    return body


def wgrad(ids, fields, cots, width):
    count, _, w = cots.shape
    n, c = fields.shape
    half = jax.ShapeDtypeStruct((9, w // 2, c), F32)
    return pl.pallas_call(
        wgrad_kernel(width),
        out_shape=[half, half],
        in_specs=[SM, VM, VM],
        out_specs=[VM, VM],
        scratch_shapes=[pltpu.VMEM((9 * w, n), BF), pltpu.VMEM((9, w, c), F32)],
        compiler_params=PARAMS,
        name="wgrad",
    )(ids, fields, cots)


def reduced(keep, send):
    total = keep + swap(send, "dp", 1)
    owned, c = total.shape[1:]
    count = lax.axis_size("space")
    at = lax.axis_index("space")
    blocks = total.reshape(count, 9 * owned // count, c)
    got = lax.all_to_all(blocks.astype(BF), "space", 0, 0)
    own = (jnp.arange(count) == at)[:, None, None]
    mine = jnp.sum(jnp.where(own, blocks, got.astype(F32)), axis=0).astype(BF)
    whole = lax.all_to_all(jnp.broadcast_to(mine, (count,) + mine.shape), "space", 0, 0)
    whole = whole.reshape(3, 3, owned, c).transpose(2, 0, 1, 3)
    return whole.astype(F32)


def after(value, *others):
    return lax.optimization_barrier((value,) + others)[0]


def per_device(inputs, pre_act, grad_out, w_first, w_second):
    _, height, width, c = inputs.shape
    n = height * width
    dp = lax.axis_size("dp")
    chips = dp // 2
    owned = w_first.shape[0]
    me = lax.axis_index("dp")
    strips = lax.axis_size("space")
    at = lax.axis_index("space")
    ids = jnp.stack([me, at, strips - 1 - at]).astype(jnp.int32)
    same_core = [[2 * q + k for q in range(chips)] for k in range(2)]

    def exchange(blocks):
        return lax.all_to_all(blocks, "dp", 0, 0, axis_index_groups=same_core)

    x = inputs.reshape(n, c)
    h = pre_act.reshape(n, c)
    g = grad_out.reshape(n, c)
    hf = h.astype(F32)
    act = (hf * jax.nn.sigmoid(hf)).astype(BF)

    acts = lax.all_gather(act, "dp", axis=0, tiled=True, axis_index_groups=same_core)
    w1 = after(w_first.reshape(owned, 9 * c), acts)
    w1_all = lax.all_gather(w1, "dp", axis=0, tiled=True)

    down_pairs = [(i, i + 1) for i in range(strips - 1)]
    up_pairs = [(i + 1, i) for i in range(strips - 1)]
    tail = jnp.concatenate([g[n - 2 * width :], h[n - width :]], axis=0)
    head = jnp.concatenate([g[: 2 * width], h[:width]], axis=0)
    above = lax.ppermute(tail, "space", down_pairs)
    below = lax.ppermute(head, "space", up_pairs)
    gup, hup = above[: 2 * width], above[2 * width :]
    gdown, hdown = below[: 2 * width], below[2 * width :]

    w2 = w_second.reshape(owned, 9 * c)
    shards = [w2] + [None] * (dp - 1)
    for k in range(2, dp, 2):
        shards[k] = swap(w2, "dp", k)
    for k in range(0, dp, 2):
        shards[k + 1] = swap(shards[k], "dp", 1)

    g_ext = jnp.concatenate([gup[width:], g, gdown[:width]], axis=0)
    g_cots = exchange(g_ext.reshape(n + 2 * width, chips, c // chips).transpose(1, 0, 2))
    second = reduced(*wgrad(ids, acts, g_cots, width))

    x_late = after(x, *shards[2::2])
    xs = exchange(jnp.broadcast_to(x_late, (chips, n, c))).reshape(chips * n, c)

    pre_ext, pieces = gated(ids, gup, g, gdown, hup, h, hdown, shards, width, chips)
    first = reduced(*wgrad(ids, xs, exchange(pieces), width))

    in_grad = plain(pre_ext, w1_all, width)
    return in_grad.reshape(inputs.shape), first, second


def solution(mesh):
    return jax.shard_map(
        per_device,
        mesh=mesh,
        in_specs=(
            P("dp", "space", None, None),
            P("dp", "space", None, None),
            P("dp", "space", None, None),
            P("dp", None, None, None),
            P("dp", None, None, None),
        ),
        out_specs=(
            P("dp", "space", None, None),
            P("dp", None, None, None),
            P("dp", None, None, None),
        ),
        check_vma=False,
    )
```

time: 212 us -> 247 us (1.17)
  blocking collectives: 0 us -> 52 us
  starting transfers between devices: 50.3 us -> 24.2 us
  waiting for transfers between devices: 103 us -> 117 us
  between operations: 21.8 us -> 14.4 us
  other arithmetic: 5.44 us -> 11.5 us
  local copies, waits for them, and re-layouts: 13.9 us -> 10.6 us
    ppermute x33 -> x9, waiting for transfers between devices: 98.2 us -> 27.3 us  [swap(): return lax.ppermute(value, axis, xor_pairs(lax.axis_size(axis), k))]
    all_to_all x0 -> x4, waiting for transfers between devices: none -> 56.2 us  [the longest x2 28.9 us: reduced(): got = lax.all_to_all(blocks.astype(BF), 'space', 0, 0)]
    all_to_all x0 -> x3, blocking collectives: none -> 52 us  [the longest x2 34.2 us: exchange(): return lax.all_to_all(blocks, 'dp', 0, 0, axis_index_groups=same_core)]
    ppermute x33 -> x9, starting transfers between devices: 39.5 us -> 3.57 us  [swap(): return lax.ppermute(value, axis, xor_pairs(lax.axis_size(axis), k))]
    all_gather x0 -> x1, waiting for transfers between devices: none -> 32.7 us  [per_device(): lax.all_gather(act, 'dp', axis=0, tiled=True, axis_index_groups=same_core)]
    all_to_all x0 -> x4, starting transfers between devices: none -> 15.8 us  [the longest x2 8.76 us: reduced(): got = lax.all_to_all(blocks.astype(BF), 'space', 0, 0)]
    ppermute x4 -> x2, starting transfers between devices: 10.7 us -> 4.68 us  [the longest x1 3.4 us: per_device(): above = lax.ppermute(tail, 'space', down_pairs)]
    ppermute x4 -> x2, waiting for transfers between devices: 4.7 us -> 0.69 us  [the longest x1 0.69 us: per_device(): above = lax.ppermute(tail, 'space', down_pairs)]
  transfers between devices with their start and end apart: 38 -> 17, of which waited for: 15 -> 10; matrix products, arithmetic and copies ran while one was open for 6% -> 6% of each run, Pallas kernels for 6% -> 6%
where the time goes in v2:
time: 247 us; the launch traced here: 246 us
  waiting for transfers between devices  117 us (47%)
  blocking collectives  52 us (21%)
  starting transfers between devices  24.2 us (10%)
  Pallas kernels  16.5 us (7%)
  between operations  14.4 us (6%)
  other arithmetic  11.5 us (5%)
  local copies, waits for them, and re-layouts  10.6 us (4%)
    all_to_all x2, blocking collectives, exchange(): return lax.all_to_all(blocks, 'dp', 0, 0, axis_index_groups=same_core)  34.2 us
    all_gather x1, waiting for transfers between devices, per_device(): lax.all_gather(act, 'dp', axis=0, tiled=True, axis_index_groups=same_core)  32.7 us
    all_to_all x2, waiting for transfers between devices, reduced(): got = lax.all_to_all(blocks.astype(BF), 'space', 0, 0)  28.9 us
    ppermute x9, waiting for transfers between devices, swap(): return lax.ppermute(value, axis, xor_pairs(lax.axis_size(axis), k))  27.3 us
    all_to_all x1, blocking collectives, reduced(): lax.all_to_all(jnp.broadcast_to(mine, (count,) + mine.shape), 'space', 0, 0)  17.8 us
    all_to_all x1, waiting for transfers between devices, reduced(): lax.all_to_all(jnp.broadcast_to(mine, (count,) + mine.shape), 'space', 0, 0)  13.9 us
    all_to_all x1, waiting for transfers between devices, exchange(): return lax.all_to_all(blocks, 'dp', 0, 0, axis_index_groups=same_core)  13.4 us
    all_to_all x2, starting transfers between devices, reduced(): got = lax.all_to_all(blocks.astype(BF), 'space', 0, 0)  8.76 us
  transfers between devices with their start and end apart: 17, of which 10 were waited for; matrix products, arithmetic and copies ran while one was open for 6% of the time, Pallas kernels for 6%

profile of v2, /device:TPU:0, one launch (start us, length us, event | category | flops | bytes accessed | tf_op | source)
XLA Modules:
  0.0 246.2 jit_solution(10515499528828158470)
XLA Ops:
  7.2 0.0 all-gather.3.cloned.1.call-start
  7.2 2.0 fusion.3
  9.2 0.0 all-gather.3.cloned.1.call-update
  9.3 0.0 all-gather.5.cloned.1.call-start
  9.3 0.5 copy.11
  9.8 0.0 copy-start.12
  9.9 1.5 reshape.55
  11.4 32.7 %all-gather.3.cloned.1.call-done.fields = bf16[1536,512]{1,0:T(8,128)(2,1)} async-done(((bf16[384,512]{1,0:T(8,128)(2,1)}), bf16[1536,512]{1,0:T(8,128)(2,1)}) %all-gather.3.cloned.1.call-update) | async-done | bytes 1572880 | tf_op jit(solution)/shard_map/all_gather | solution.py:209
  44.1 0.0 all-gather.5.cloned.1.call-update
  44.2 0.0 copy-start.2
  44.2 0.0 copy-start.1
  44.2 0.5 copy.10
  44.7 0.8 reshape.54.refs_7_
  45.5 1.5 collective-permute-start.3
  47.1 0.6 collective-permute-start.5
  47.6 1.5 collective-permute-start.7
  49.2 3.4 %collective-permute-start = (bf16[144,512]{1,0:T(8,128)(2,1)S(1)}, bf16[144,512]{1,0:T(8,128)(2,1)S(1)}, u32[]{:S(2)}, u32[]{:S(2)}) collective-permute-start(bf16[144,512]{1,0:T(8,128)(2,1)S(1)} %pad_maximum_fusion), channel_id=1, source_target_pairs={{0,1},{1,2},{2,3},{4,5},{5,6},{6,7},{8,9},{9,10},{10,11},{12,13},{... | collective-permute-start | bytes 442376 | tf_op jit(solution)/shard_map/ppermute | solution.py:217
  52.6 0.7 pad_maximum_fusion.1
  53.2 1.3 collective-permute-start.1
  54.5 0.7 collective-permute-done
  55.2 0.0 collective-permute-start.2
  55.2 11.6 %collective-permute-done.3.refs_9_ = bf16[64,4608]{1,0:T(8,128)(2,1)S(1)} collective-permute-done((bf16[64,4608]{1,0:T(8,128)(2,1)S(1)}, bf16[64,4608]{1,0:T(8,128)(2,1)S(1)}, u32[]{:S(2)}, u32[]{:S(2)}) %collective-permute-start.3) | collective-permute-done | bytes 589856 | tf_op jit(solution)/shard_map/ppermute | solution.py:21
  66.8 0.0 collective-permute-start.4
  66.8 3.8 %collective-permute-done.5.refs_11_ = bf16[64,4608]{1,0:T(8,128)(2,1)S(1)} collective-permute-done((bf16[64,4608]{1,0:T(8,128)(2,1)S(1)}, bf16[64,4608]{1,0:T(8,128)(2,1)S(1)}, u32[]{:S(2)}, u32[]{:S(2)}) %collective-permute-start.5) | collective-permute-done | bytes 589856 | tf_op jit(solution)/shard_map/ppermute | solution.py:21
  70.6 0.0 collective-permute-start.6
  70.6 10.0 %collective-permute-done.7.refs_13_ = bf16[64,4608]{1,0:T(8,128)(2,1)S(1)} collective-permute-done((bf16[64,4608]{1,0:T(8,128)(2,1)S(1)}, bf16[64,4608]{1,0:T(8,128)(2,1)S(1)}, u32[]{:S(2)}, u32[]{:S(2)}) %collective-permute-start.7) | collective-permute-done | bytes 589856 | tf_op jit(solution)/shard_map/ppermute | solution.py:21
  80.6 0.0 collective-permute-start.8
  80.6 0.1 pad_add_fusion.refs_0_.ids
  80.7 0.0 collective-permute-done.2.refs_8_
  80.8 0.0 collective-permute-done.4.refs_10_
  80.8 2.0 collective-permute-done.8.refs_14_
  82.7 5.0 %gated.1 = (bf16[480,512]{1,0:T(8,128)(2,1)S(1)}, bf16[4,480,128]{2,1,0:T(8,128)(2,1)S(1)}) custom-call(s32[3]{0:T(128)S(1)} %pad_add_fusion.refs_0_.ids, bf16[96,512]{1,0:T(8,128)(2,1)S(1)} %slice.58.refs_1_, bf16[384,512]{1,0:T(8,128)(2,1)S(1)} %bitcast.38, bf16[96,512]{1,0:T(8,128)(2,1)S(1)} %slice.59.refs_3_, ...), custom_call_target="tpu_custom_call" | custom-call | tf_op jit(solution)/shard_map/gated/pallas_call | solution.py:88
  87.8 0.8 copy-done.4
  88.6 0.8 copy-done.6
  89.4 3.6 %all-to-all-start.1 = ((bf16[4,480,128]{2,1,0:T(8,128)(2,1)}), bf16[4,480,128]{2,1,0:T(8,128)(2,1)S(1)}, u32[]{:S(2)}, u32[]{:S(2)}) async-start(bf16[4,480,128]{2,1,0:T(8,128)(2,1)} %copy-done.6), calls=%async_computation.1 | async-start | bytes 983040 | tf_op jit(solution)/shard_map/all_to_all | solution.py:201
  93.0 13.4 %all-to-all-done.1.cots = bf16[4,480,128]{2,1,0:T(8,128)(2,1)S(1)} async-done(((bf16[4,480,128]{2,1,0:T(8,128)(2,1)}), bf16[4,480,128]{2,1,0:T(8,128)(2,1)S(1)}, u32[]{:S(2)}, u32[]{:S(2)}) %all-to-all-start.1) | async-done | bytes 491552 | tf_op jit(solution)/shard_map/all_to_all | solution.py:201
  106.4 0.1 broadcast_in_dim.23
  106.5 22.5 %all_to_all.35 = bf16[4,384,512]{2,1,0:T(8,128)(2,1)S(1)} all-to-all(bf16[4,384,512]{2,1,0:T(8,128)(2,1)S(1)} %broadcast_in_dim.23), channel_id=1, replica_groups={{0,8,16,24},{4,12,20,28},{1,9,17,25},{5,13,21,29},{2,10,18,26},{6,14,22..., dimensions={0} | all-to-all | bytes 3145728 | tf_op jit(solution)/shard_map/all_to_all | solution.py:201
  129.0 4.3 %wgrad.2 = (f32[9,64,512]{2,1,0:T(8,128)S(1)}, f32[9,64,512]{2,1,0:T(8,128)}) custom-call(s32[3]{0:T(128)S(1)} %pad_add_fusion.refs_0_.ids, bf16[1536,512]{1,0:T(8,128)(2,1)S(1)} %bitcast.37, bf16[4,480,128]{2,1,0:T(8,128)(2,1)S(1)} %all-to-all-done.1.cots), custom_call_target="tpu_custom_call" | custom-call | tf_op jit(solution)/shard_map/wgrad/pallas_call | solution.py:159
  133.3 0.1 concatenate.19
  133.4 0.1 copy.13
  133.5 11.7 %all_to_all.36.cots = bf16[4,480,128]{2,1,0:T(8,128)(2,1)S(1)} all-to-all(bf16[4,480,128]{2,1,0:T(8,128)(2,1)S(1)} %maximum_bitcast_fusion), channel_id=1, replica_groups={{0,8,16,24},{4,12,20,28},{1,9,17,25},{5,13,21,29},{2,10,18,26},{6,14,22..., dimensions={0} | all-to-all | bytes 983040 | tf_op jit(solution)/shard_map/all_to_all | solution.py:201
  145.3 4.3 %wgrad.3 = (f32[9,64,512]{2,1,0:T(8,128)S(1)}, f32[9,64,512]{2,1,0:T(8,128)}) custom-call(s32[3]{0:T(128)S(1)} %pad_add_fusion.refs_0_.ids, bf16[1536,512]{1,0:T(8,128)(2,1)S(1)} %copy-done.3, bf16[4,480,128]{2,1,0:T(8,128)(2,1)S(1)} %all_to_all.36.cots), custom_call_target="tpu_custom_call" | custom-call | tf_op jit(solution)/shard_map/wgrad/pallas_call | solution.py:159
  149.6 1.5 add.10
  151.1 0.0 copy-start.7
  151.1 1.0 copy-done.7
  152.1 0.9 convert_element_type.44
  153.0 4.6 %all-to-all-start.2 = ((bf16[4,144,512]{2,1,0:T(8,128)(2,1)}), bf16[4,144,512]{2,1,0:T(8,128)(2,1)S(1)}, u32[]{:S(2)}, u32[]{:S(2)}) async-start(bf16[4,144,512]{2,1,0:T(8,128)(2,1)} %convert_element_type.44), calls=%async_computation.2 | async-start | bytes 1179648 | tf_op jit(solution)/shard_map/all_to_all | solution.py:176
  157.7 1.5 add.11
  159.2 0.0 copy-start.9
  159.2 1.0 copy-done.9
  160.2 0.9 convert_element_type.50
  161.1 13.1 %all-to-all-done.2 = bf16[4,144,512]{2,1,0:T(8,128)(2,1)S(1)} async-done(((bf16[4,144,512]{2,1,0:T(8,128)(2,1)}), bf16[4,144,512]{2,1,0:T(8,128)(2,1)S(1)}, u32[]{:S(2)}, u32[]{:S(2)}) %all-to-all-start.2) | async-done | bytes 589856 | tf_op jit(solution)/shard_map/all_to_all | solution.py:176
  174.2 4.2 %all-to-all-start.5 = ((bf16[4,144,512]{2,1,0:T(8,128)(2,1)}), bf16[4,144,512]{2,1,0:T(8,128)(2,1)}, u32[]{:S(2)}, u32[]{:S(2)}) async-start(bf16[4,144,512]{2,1,0:T(8,128)(2,1)} %convert_element_type.50), calls=%async_computation.5 | async-start | bytes 1179648 | tf_op jit(solution)/shard_map/all_to_all | solution.py:176
  178.4 15.8 %all-to-all-done.5 = bf16[4,144,512]{2,1,0:T(8,128)(2,1)} async-done(((bf16[4,144,512]{2,1,0:T(8,128)(2,1)}), bf16[4,144,512]{2,1,0:T(8,128)(2,1)}, u32[]{:S(2)}, u32[]{:S(2)}) %all-to-all-start.5) | async-done | bytes 589856 | tf_op jit(solution)/shard_map/all_to_all | solution.py:176
  194.2 1.5 select_reduce_fusion
  195.7 17.8 %all_to_all.37 = bf16[4,144,512]{2,1,0:T(8,128)(2,1)S(1)} all-to-all(bf16[4,144,512]{2,1,0:T(8,128)(2,1)S(1)} %broadcast_in_dim.25), channel_id=1, replica_groups=mesh['dp'=8,'space'=4] {'space'}, dimensions={0} | all-to-all | bytes 1179648 | tf_op jit(solution)/shard_map/all_to_all | solution.py:179
  213.5 0.9 broadcast_in_dim.24
  214.4 3.5 %all-to-all-start.3 = ((bf16[4,144,512]{2,1,0:T(8,128)(2,1)}), bf16[4,144,512]{2,1,0:T(8,128)(2,1)S(1)}, u32[]{:S(2)}, u32[]{:S(2)}) async-start(bf16[4,144,512]{2,1,0:T(8,128)(2,1)} %broadcast_in_dim.24), calls=%async_computation.3 | async-start | bytes 1179648 | tf_op jit(solution)/shard_map/all_to_all | solution.py:179
  217.8 1.2 convert_bitcast_fusion
  219.0 13.9 %all-to-all-done.3 = bf16[4,144,512]{2,1,0:T(8,128)(2,1)S(1)} async-done(((bf16[4,144,512]{2,1,0:T(8,128)(2,1)}), bf16[4,144,512]{2,1,0:T(8,128)(2,1)S(1)}, u32[]{:S(2)}, u32[]{:S(2)}) %all-to-all-start.3) | async-done | bytes 589856 | tf_op jit(solution)/shard_map/all_to_all | solution.py:179
  232.9 1.2 convert_bitcast_fusion.1
  234.1 2.3 copy-done
  236.4 2.9 %plain.1 = f32[384,512]{1,0:T(8,128)} custom-call(bf16[480,512]{1,0:T(8,128)(2,1)S(1)} %copy-done.5, bf16[512,4608]{1,0:T(8,128)(2,1)S(1)} %copy-done), custom_call_target="tpu_custom_call" | custom-call | tf_op jit(solution)/shard_map/plain/pallas_call | solution.py:120
  (36 shorter events, 0.2 us)
Async XLA Ops:
  7.2 2.2 copy-start.11
  7.2 37.0 %all-gather.3.cloned.1.call-start = ((), (), s32[]{:S(2)}) async-start(), calls=%async_computation.7 | async-start | bytes 1966080 | tf_op jit(solution)/shard_map/all_gather | solution.py:209
  9.3 224.8 %all-gather.5.cloned.1.call-start = ((), (), s32[]{:S(2)}) async-start(), calls=%async_computation.8 | async-start | bytes 5308416 | tf_op jit(solution)/shard_map/all_gather | solution.py:211
  9.8 34.3 %copy-start.12 = (bf16[64,3,3,512]{3,0,2,1:T(8,128)(2,1)S(1)}, bf16[64,3,3,512]{3,0,2,1:T(8,128)(2,1)}, u32[]{:S(2)}) copy-start(bf16[64,3,3,512]{3,0,2,1:T(8,128)(2,1)} %param.9) | copy-start | bytes 1769476
  44.2 4.9 %copy-start.2 = (bf16[1,8,48,512]{3,2,1,0:T(8,128)(2,1)S(1)}, bf16[1,8,48,512]{3,2,1,0:T(8,128)(2,1)}, u32[]{:S(2)}) copy-start(bf16[1,8,48,512]{3,2,1,0:T(8,128)(2,1)} %param.6) | copy-start | bytes 1179652
  44.2 4.9 %copy-start.1 = (bf16[1,8,48,512]{3,2,1,0:T(8,128)(2,1)S(1)}, bf16[1,8,48,512]{3,2,1,0:T(8,128)(2,1)}, u32[]{:S(2)}) copy-start(bf16[1,8,48,512]{3,2,1,0:T(8,128)(2,1)} %param.7) | copy-start | bytes 1179652
  45.5 21.3 %collective-permute-start.3 = (bf16[64,4608]{1,0:T(8,128)(2,1)S(1)}, bf16[64,4608]{1,0:T(8,128)(2,1)S(1)}, u32[]{:S(2)}, u32[]{:S(2)}) collective-permute-start(bf16[64,4608]{1,0:T(8,128)(2,1)S(1)} %reshape.54.refs_7_), channel_id=1, source_target_pairs={{0,8},{4,12},{8,0},{12,4},{16,24},{20,28},{24,16},{28,20},{1,9},{5... | collective-permute-start | bytes 1769480 | tf_op jit(solution)/shard_map/ppermute | solution.py:21
  47.1 23.6 %collective-permute-start.5 = (bf16[64,4608]{1,0:T(8,128)(2,1)S(1)}, bf16[64,4608]{1,0:T(8,128)(2,1)S(1)}, u32[]{:S(2)}, u32[]{:S(2)}) collective-permute-start(bf16[64,4608]{1,0:T(8,128)(2,1)S(1)} %reshape.54.refs_7_), channel_id=1, source_target_pairs={{0,16},{4,20},{8,24},{12,28},{16,0},{20,4},{24,8},{28,12},{1,17},{... | collective-permute-start | bytes 1769480 | tf_op jit(solution)/shard_map/ppermute | solution.py:21
  47.6 33.0 %collective-permute-start.7 = (bf16[64,4608]{1,0:T(8,128)(2,1)S(1)}, bf16[64,4608]{1,0:T(8,128)(2,1)S(1)}, u32[]{:S(2)}, u32[]{:S(2)}) collective-permute-start(bf16[64,4608]{1,0:T(8,128)(2,1)S(1)} %reshape.54.refs_7_), channel_id=1, source_target_pairs={{0,24},{4,28},{8,16},{12,20},{16,8},{20,12},{24,0},{28,4},{1,25},{... | collective-permute-start | bytes 1769480 | tf_op jit(solution)/shard_map/ppermute | solution.py:21
  49.2 6.1 %collective-permute-start = (bf16[144,512]{1,0:T(8,128)(2,1)S(1)}, bf16[144,512]{1,0:T(8,128)(2,1)S(1)}, u32[]{:S(2)}, u32[]{:S(2)}) collective-permute-start(bf16[144,512]{1,0:T(8,128)(2,1)S(1)} %pad_maximum_fusion), channel_id=1, source_target_pairs={{0,1},{1,2},{2,3},{4,5},{5,6},{6,7},{8,9},{9,10},{10,11},{12,13},{... | collective-permute-start | bytes 442376 | tf_op jit(solution)/shard_map/ppermute | solution.py:217
  53.2 27.4 %collective-permute-start.1 = (bf16[144,512]{1,0:T(8,128)(2,1)}, bf16[144,512]{1,0:T(8,128)(2,1)S(1)}, u32[]{:S(2)}, u32[]{:S(2)}) collective-permute-start(bf16[144,512]{1,0:T(8,128)(2,1)} %pad_maximum_fusion.1), channel_id=1, source_target_pairs={{1,0},{2,1},{3,2},{5,4},{6,5},{7,6},{9,8},{10,9},{11,10},{13,12},{... | collective-permute-start | bytes 442376 | tf_op jit(solution)/shard_map/ppermute | solution.py:218
  55.2 25.5 %collective-permute-start.2 = (bf16[64,4608]{1,0:T(8,128)(2,1)S(1)}, bf16[64,4608]{1,0:T(8,128)(2,1)}, u32[]{:S(2)}, u32[]{:S(2)}) collective-permute-start(bf16[64,4608]{1,0:T(8,128)(2,1)S(1)} %reshape.54.refs_7_), channel_id=1, source_target_pairs={{0,4},{4,0},{8,12},{12,8},{16,20},{20,16},{24,28},{28,24},{1,5},{5... | collective-permute-start | bytes 1769480 | tf_op jit(solution)/shard_map/ppermute | solution.py:21
  66.8 14.0 %collective-permute-start.4 = (bf16[64,4608]{1,0:T(8,128)(2,1)S(1)}, bf16[64,4608]{1,0:T(8,128)(2,1)}, u32[]{:S(2)}, u32[]{:S(2)}) collective-permute-start(bf16[64,4608]{1,0:T(8,128)(2,1)S(1)} %collective-permute-done.3.refs_9_), channel_id=1, source_target_pairs={{0,4},{4,0},{8,12},{12,8},{16,20},{20,16},{24,28},{28,24},{1,5},{5... | collective-permute-start | bytes 1769480 | tf_op jit(solution)/shard_map/ppermute | solution.py:21
  70.6 10.1 %collective-permute-start.6 = (bf16[64,4608]{1,0:T(8,128)(2,1)S(1)}, bf16[64,4608]{1,0:T(8,128)(2,1)}, u32[]{:S(2)}, u32[]{:S(2)}) collective-permute-start(bf16[64,4608]{1,0:T(8,128)(2,1)S(1)} %collective-permute-done.5.refs_11_), channel_id=1, source_target_pairs={{0,4},{4,0},{8,12},{12,8},{16,20},{20,16},{24,28},{28,24},{1,5},{5... | collective-permute-start | bytes 1769480 | tf_op jit(solution)/shard_map/ppermute | solution.py:21
  80.6 2.1 collective-permute-start.8
  87.7 0.8 copy-start.4
  88.6 0.8 copy-start.6
  89.4 17.0 %copy-start.13 = (bf16[1,8,48,512]{3,2,1,0:T(8,128)(2,1)S(1)}, bf16[1,8,48,512]{3,2,1,0:T(8,128)(2,1)}, u32[]{:S(2)}) copy-start(bf16[1,8,48,512]{3,2,1,0:T(8,128)(2,1)} %param.5) | copy-start | bytes 1179652
  89.4 17.0 %all-to-all-start.1 = ((bf16[4,480,128]{2,1,0:T(8,128)(2,1)}), bf16[4,480,128]{2,1,0:T(8,128)(2,1)S(1)}, u32[]{:S(2)}, u32[]{:S(2)}) async-start(bf16[4,480,128]{2,1,0:T(8,128)(2,1)} %copy-done.6), calls=%async_computation.1 | async-start | bytes 983040 | tf_op jit(solution)/shard_map/all_to_all | solution.py:201
  133.3 16.3 %collective-permute-start.9 = (f32[9,64,512]{2,1,0:T(8,128)}, f32[9,64,512]{2,1,0:T(8,128)}, u32[]{:S(2)}, u32[]{:S(2)}) collective-permute-start(f32[9,64,512]{2,1,0:T(8,128)} %get-tuple-element.16), channel_id=1, source_target_pairs={{0,4},{4,0},{8,12},{12,8},{16,20},{20,16},{24,28},{28,24},{1,5},{5... | collective-permute-start | bytes 3538952 | tf_op jit(solution)/shard_map/ppermute | solution.py:21
  133.5 11.8 %copy-start.3 = (bf16[1536,512]{1,0:T(8,128)(2,1)S(1)}, bf16[1536,512]{1,0:T(8,128)(2,1)}, u32[]{:S(2)}) copy-start(bf16[1536,512]{1,0:T(8,128)(2,1)} %all-gather.3.cloned.1.call-done.fields) | copy-start | bytes 4718596
  149.6 8.0 %collective-permute-start.10 = (f32[9,64,512]{2,1,0:T(8,128)}, f32[9,64,512]{2,1,0:T(8,128)}, u32[]{:S(2)}, u32[]{:S(2)}) collective-permute-start(f32[9,64,512]{2,1,0:T(8,128)} %get-tuple-element.18), channel_id=1, source_target_pairs={{0,4},{4,0},{8,12},{12,8},{16,20},{20,16},{24,28},{28,24},{1,5},{5... | collective-permute-start | bytes 3538952 | tf_op jit(solution)/shard_map/ppermute | solution.py:21
  151.1 1.0 copy-start.7
  153.0 21.2 %all-to-all-start.2 = ((bf16[4,144,512]{2,1,0:T(8,128)(2,1)}), bf16[4,144,512]{2,1,0:T(8,128)(2,1)S(1)}, u32[]{:S(2)}, u32[]{:S(2)}) async-start(bf16[4,144,512]{2,1,0:T(8,128)(2,1)} %convert_element_type.44), calls=%async_computation.2 | async-start | bytes 1179648 | tf_op jit(solution)/shard_map/all_to_all | solution.py:176
  159.2 1.0 copy-start.9
  160.2 34.0 %copy-start.8 = (f32[9,64,512]{2,1,0:T(8,128)S(1)}, f32[9,64,512]{2,1,0:T(8,128)}, u32[]{:S(2)}) copy-start(f32[9,64,512]{2,1,0:T(8,128)} %copy-done.7) | copy-start | bytes 3538948
  161.1 33.1 %copy-start.10 = (f32[9,64,512]{2,1,0:T(8,128)S(1)}, f32[9,64,512]{2,1,0:T(8,128)}, u32[]{:S(2)}) copy-start(f32[9,64,512]{2,1,0:T(8,128)} %copy-done.9) | copy-start | bytes 3538948
  174.2 20.0 %all-to-all-start.5 = ((bf16[4,144,512]{2,1,0:T(8,128)(2,1)}), bf16[4,144,512]{2,1,0:T(8,128)(2,1)}, u32[]{:S(2)}, u32[]{:S(2)}) async-start(bf16[4,144,512]{2,1,0:T(8,128)(2,1)} %convert_element_type.50), calls=%async_computation.5 | async-start | bytes 1179648 | tf_op jit(solution)/shard_map/all_to_all | solution.py:176
  214.4 18.6 %all-to-all-start.3 = ((bf16[4,144,512]{2,1,0:T(8,128)(2,1)}), bf16[4,144,512]{2,1,0:T(8,128)(2,1)S(1)}, u32[]{:S(2)}, u32[]{:S(2)}) async-start(bf16[4,144,512]{2,1,0:T(8,128)(2,1)} %broadcast_in_dim.24), calls=%async_computation.3 | async-start | bytes 1179648 | tf_op jit(solution)/shard_map/all_to_all | solution.py:179
  219.0 15.1 %copy-start.5 = (bf16[480,512]{1,0:T(8,128)(2,1)S(1)}, bf16[480,512]{1,0:T(8,128)(2,1)}, u32[]{:S(2)}) copy-start(bf16[480,512]{1,0:T(8,128)(2,1)} %copy-done.4) | copy-start | bytes 1474564
  234.1 2.3 copy-start
Sparse Core Ops, SparseCore 0:
  10.4 33.6 all-gather.2
  46.6 61.4 all-gather.4

commit v3 on v2

v3 whole, which is shorter than its diff:
```python
import jax
import jax.numpy as jnp
from jax import lax
from jax.experimental import pallas as pl
from jax.experimental.pallas import tpu as pltpu
from jax.sharding import PartitionSpec as P

BF = jnp.bfloat16
F32 = jnp.float32
PARAMS = pltpu.CompilerParams(vmem_limit_bytes=48 * 1024 * 1024)
ANY = pl.BlockSpec(memory_space=pl.ANY)
VM = pl.BlockSpec(memory_space=pltpu.VMEM)
SM = pl.BlockSpec(memory_space=pltpu.SMEM)


def xor_pairs(count, k):
    return [(i, i ^ k) for i in range(count)]


def swap(value, axis, k):
    return lax.ppermute(value, axis, xor_pairs(lax.axis_size(axis), k))


def shifted(flat, width):
    rows = flat.shape[0]
    wide = flat.astype(F32)
    col = lax.broadcasted_iota(jnp.int32, wide.shape, 0) % width
    left = jnp.where(col == 0, 0.0, pltpu.roll(wide, 1, 0)).astype(BF)
    right = jnp.where(col == width - 1, 0.0, pltpu.roll(wide, rows - 1, 0)).astype(BF)
    return left, flat, right


def products(field, kernel, n, c, width):
    acc = None
    for r in range(3):
        for s in range(3):
            tap = 3 * r + s
            lhs = field[s, (2 - r) * width : (2 - r) * width + n, :]
            part = jnp.dot(lhs, kernel[:, tap * c : (tap + 1) * c], preferred_element_type=F32)
            acc = part if acc is None else acc + part
    return acc


def weight_copies(ids, weights, kernel, sems):
    copies = []
    for k, weight in enumerate(weights):
        rows = weight.shape[0]
        start = pl.multiple_of((ids[0] ^ k) * rows, rows)
        copies.append(pltpu.make_async_copy(weight, kernel.at[pl.ds(start, rows)], sems.at[k]))
        copies[-1].start()
    return copies


def gated_kernel(count, width):
    def body(*refs):
        ids, gup, g, gdown, hup, h, hdown = refs[:7]
        weights = refs[7 : 7 + count]
        out, parts, field, kernel, sems = refs[7 + count :]
        copies = weight_copies(ids, weights, kernel, sems)
        left, same, right = shifted(
            jnp.concatenate([gup[...], g[...], gdown[...]], axis=0), width
        )
        field[0] = right
        field[1] = same
        field[2] = left
        for copy in copies:
            copy.wait()
        n, c = out.shape
        acc = products(field, kernel, n, c, width)
        hf = jnp.concatenate([hup[...], h[...], hdown[...]], axis=0).astype(F32)
        sig = jax.nn.sigmoid(hf)
        acc = acc * (sig * (1.0 + hf * (1.0 - sig)))
        row = lax.broadcasted_iota(jnp.int32, acc.shape, 0)
        inside = jnp.logical_and(
            jnp.logical_or(row >= width, ids[1] > 0),
            jnp.logical_or(row < n - width, ids[2] > 0),
        )
        res = jnp.where(inside, acc, 0.0).astype(BF)
        out[...] = res
        strips = parts.shape[0]
        each = c // (strips * count)
        src = lax.broadcasted_iota(jnp.int32, (c, c), 0)
        dst = lax.broadcasted_iota(jnp.int32, (c, c), 1)
        owner, rest = src // (strips * each), src % (strips * each)
        goes = (rest // each) * (count * each) + owner * each + rest % each
        moved = jnp.dot(
            res[width : n - width], (goes == dst).astype(BF), preferred_element_type=F32
        ).astype(BF)
        w = c // strips
        for t in range(strips):
            parts[t] = moved[:, t * w : (t + 1) * w]

    return body


def gated(ids, gup, g, gdown, hup, h, hdown, weights, width, pieces):
    n, c = h.shape
    count = len(weights)
    rows = n + 2 * width
    return pl.pallas_call(
        gated_kernel(count, width),
        out_shape=[
            jax.ShapeDtypeStruct((rows, c), BF),
            jax.ShapeDtypeStruct((pieces, n, c // pieces), BF),
        ],
        in_specs=[SM] + [VM] * 6 + [ANY] * count,
        out_specs=[VM, VM],
        scratch_shapes=[
            pltpu.VMEM((3, rows + 2 * width, c), BF),
            pltpu.VMEM((weights[0].shape[0] * count, weights[0].shape[1]), BF),
            pltpu.SemaphoreType.DMA((count,)),
        ],
        compiler_params=PARAMS,
        name="gated",
    )(ids, gup, g, gdown, hup, h, hdown, *weights)


def plain_kernel(count, width):
    def body(*refs):
        ids, ext = refs[:2]
        weights = refs[2 : 2 + count]
        out, field, kernel, sems = refs[2 + count :]
        copies = weight_copies(ids, weights, kernel, sems)
        left, same, right = shifted(ext[...], width)
        field[0] = right
        field[1] = same
        field[2] = left
        for copy in copies:
            copy.wait()
        n, c = out.shape
        out[...] = products(field, kernel, n, c, width)

    return body


def plain(ids, ext, weights, width):
    rows, c = ext.shape
    count = len(weights)
    return pl.pallas_call(
        plain_kernel(count, width),
        out_shape=jax.ShapeDtypeStruct((rows - 2 * width, c), F32),
        in_specs=[SM, VM] + [ANY] * count,
        out_specs=VM,
        scratch_shapes=[
            pltpu.VMEM((3, rows, c), BF),
            pltpu.VMEM((weights[0].shape[0] * count, weights[0].shape[1]), BF),
            pltpu.SemaphoreType.DMA((count,)),
        ],
        compiler_params=PARAMS,
        name="plain",
    )(ids, ext, *weights)


def wgrad_products(lhs, cots, fields, acc, width):
    w = cots[0].shape[1]
    n = cots[0].shape[0] - 2 * width
    for i, cot in enumerate(cots):
        left, same, right = shifted(cot, width)
        for s, part in enumerate((right, same, left)):
            for r in range(3):
                tap = 3 * r + s
                lhs[tap * w : (tap + 1) * w, i * n : (i + 1) * n] = part[
                    (2 - r) * width : (2 - r) * width + n, :
                ].T
    for tap in range(9):
        total = None
        for i, field in enumerate(fields):
            part = jnp.dot(
                lhs[tap * w : (tap + 1) * w, i * n : (i + 1) * n],
                field[...],
                preferred_element_type=F32,
            )
            total = part if total is None else total + part
        acc[tap] = total


def strip_kernel(count, width):
    def body(*refs):
        ids = refs[0]
        fields = refs[1 : 1 + count]
        cots = refs[1 + count : 1 + 2 * count]
        keep, send, lhs, acc = refs[1 + 2 * count :]
        wgrad_products(lhs, [cot[...] for cot in cots], fields, acc, width)
        half = keep.shape[1]
        mine = ids[0] & 1
        keep[...] = acc[:, pl.ds(pl.multiple_of(mine * half, half), half), :]
        send[...] = acc[:, pl.ds(pl.multiple_of((1 - mine) * half, half), half), :]

    return body


def strip_wgrad(ids, fields, cots, width):
    count = len(fields)
    n, c = fields[0].shape
    w = cots[0].shape[1]
    half = jax.ShapeDtypeStruct((9, w // 2, c), F32)
    return pl.pallas_call(
        strip_kernel(count, width),
        out_shape=[half, half],
        in_specs=[SM] + [VM] * (2 * count),
        out_specs=[VM, VM],
        scratch_shapes=[pltpu.VMEM((9 * w, count * n), BF), pltpu.VMEM((9, w, c), F32)],
        compiler_params=PARAMS,
        name="strip_wgrad",
    )(ids, *fields, *cots)


def image_kernel(width):
    def body(ids, field, cots, own, parts, lhs, acc):
        count, n, w = cots.shape
        zero = jnp.zeros((width, w), BF)
        cot = jnp.concatenate([zero] + [cots[t] for t in range(count)] + [zero], axis=0)
        wgrad_products(lhs, [cot], [field], acc, width)
        owners, _, each, _ = parts.shape
        for d in range(owners):
            block = acc[:, d * each : (d + 1) * each, :]
            parts[d] = block.astype(BF)

            @pl.when(ids[0] == d)
            def _():
                own[...] = block

    return body


def image_wgrad(ids, field, cots, owners, width):
    n, c = field.shape
    w = cots.shape[2]
    each = w // owners
    return pl.pallas_call(
        image_kernel(width),
        out_shape=[
            jax.ShapeDtypeStruct((9, each, c), F32),
            jax.ShapeDtypeStruct((owners, 9, each, c), BF),
        ],
        in_specs=[SM, VM, VM],
        out_specs=[VM, VM],
        scratch_shapes=[pltpu.VMEM((9 * w, n), BF), pltpu.VMEM((9, w, c), F32)],
        compiler_params=PARAMS,
        name="image_wgrad",
    )(ids, field, cots)


def strips_summed(keep, send):
    total = keep + swap(send, "dp", 1)
    owned, c = total.shape[1:]
    count = lax.axis_size("space")
    at = lax.axis_index("space")
    blocks = total.reshape(count, 9 * owned // count, c)
    mine = lax.dynamic_index_in_dim(blocks, at, 0, keepdims=False)
    for k in range(1, count):
        sent = lax.dynamic_index_in_dim(blocks, at ^ k, 0, keepdims=False).astype(BF)
        mine = mine + swap(sent, "space", k).astype(F32)
    mine = mine.astype(BF)
    got = jnp.stack([mine] + [swap(mine, "space", k) for k in range(1, count)])
    whole = jnp.concatenate(
        [lax.dynamic_index_in_dim(got, at ^ j, 0, keepdims=False) for j in range(count)], axis=0
    )
    whole = whole.reshape(3, 3, owned, c).transpose(2, 0, 1, 3)
    return whole.astype(F32)


def images_summed(own, parts):
    owners = parts.shape[0]
    got = lax.all_to_all(parts, "dp", 0, 0)
    here = (jnp.arange(owners) == lax.axis_index("dp"))[:, None, None, None]
    return jnp.sum(jnp.where(here, own, got.astype(F32)), axis=0).astype(BF)


def strips_shared(mine):
    count = lax.axis_size("space")
    whole = lax.all_to_all(jnp.broadcast_to(mine, (count,) + mine.shape), "space", 0, 0)
    _, taps, each, c = whole.shape
    whole = whole.transpose(0, 2, 1, 3).reshape(count * each, 3, 3, c)
    return whole.astype(F32)


def after(value, *others):
    return lax.optimization_barrier((value,) + others)[0]


def per_device(inputs, pre_act, grad_out, w_first, w_second):
    _, height, width, c = inputs.shape
    n = height * width
    dp = lax.axis_size("dp")
    chips = dp // 2
    owned = w_first.shape[0]
    me = lax.axis_index("dp")
    strips = lax.axis_size("space")
    at = lax.axis_index("space")
    ids = jnp.stack([me, at, strips - 1 - at]).astype(jnp.int32)

    def sent_to_chips(rows):
        return [swap(rows, "dp", k) for k in range(2, dp, 2)]

    def sent_to_pair(shards):
        return [shard for own in shards for shard in (own, swap(own, "dp", 1))]

    x = inputs.reshape(n, c)
    h = pre_act.reshape(n, c)
    g = grad_out.reshape(n, c)
    hf = h.astype(F32)
    act = (hf * jax.nn.sigmoid(hf)).astype(BF)

    w2 = w_second.reshape(owned, 9 * c)
    w2_shards = [w2] + sent_to_chips(w2)
    shards = sent_to_pair(w2_shards)

    down_pairs = [(i, i + 1) for i in range(strips - 1)]
    up_pairs = [(i + 1, i) for i in range(strips - 1)]
    tail = jnp.concatenate([g[n - 2 * width :], h[n - width :]], axis=0)
    head = jnp.concatenate([g[: 2 * width], h[:width]], axis=0)
    above = lax.ppermute(tail, "space", down_pairs)
    below = lax.ppermute(head, "space", up_pairs)
    gup, hup = above[: 2 * width], above[2 * width :]
    gdown, hdown = below[: 2 * width], below[2 * width :]

    x_late = after(x, above, below)
    image = lax.all_to_all(jnp.broadcast_to(x_late, (strips, n, c)), "space", 0, 0)
    image = image.reshape(strips * n, c)

    pre_ext, pieces = gated(ids, gup, g, gdown, hup, h, hdown, shards, width, strips)
    pieces = after(pieces, image)
    p_cots = lax.all_to_all(pieces, "space", 0, 0)

    g_ext = jnp.concatenate([gup[width:], g, gdown[:width]], axis=0)
    blocks = g_ext.reshape(n + 2 * width, chips, c // chips).transpose(1, 0, 2)
    act_late, blocks_late = after((act, blocks), *w2_shards[1:])
    acts, g_cots = [act], [lax.dynamic_index_in_dim(blocks, me >> 1, 0, keepdims=False)]
    for k in range(1, chips):
        acts.append(swap(act_late, "dp", 2 * k))
        part = lax.dynamic_index_in_dim(blocks_late, (me >> 1) ^ k, 0, keepdims=False)
        g_cots.append(swap(part, "dp", 2 * k))

    w1 = w_first.reshape(owned, 9 * c)
    w1_shards = [w1] + sent_to_chips(after(w1, *acts[1:], *g_cots[1:]))

    share = images_summed(*image_wgrad(ids, image, p_cots, dp, width))
    w1_shards = sent_to_pair(after(w1_shards, share))
    first = strips_shared(share)
    second = strips_summed(*strip_wgrad(ids, acts, g_cots, width))
    in_grad = plain(ids, pre_ext, w1_shards, width)
    return in_grad.reshape(inputs.shape), first, second


def solution(mesh):
    return jax.shard_map(
        per_device,
        mesh=mesh,
        in_specs=(
            P("dp", "space", None, None),
            P("dp", "space", None, None),
            P("dp", "space", None, None),
            P("dp", None, None, None),
            P("dp", None, None, None),
        ),
        out_specs=(
            P("dp", "space", None, None),
            P("dp", None, None, None),
            P("dp", None, None, None),
        ),
        check_vma=False,
    )
```

time: 247 us -> 160 us (0.65)
  waiting for transfers between devices: 117 us -> 56.2 us
  blocking collectives: 52 us -> 0 us
  starting transfers between devices: 24.2 us -> 54 us
  between operations: 14.4 us -> 0.99 us
  local copies, waits for them, and re-layouts: 10.6 us -> 20.6 us
  other arithmetic: 11.5 us -> 6.99 us
  Pallas kernels: 16.5 us -> 20 us
    all_to_all x4, waiting for transfers between devices: 56.2 us -> 0.95 us  [the longest x1 0.95 us: images_summed(): got = lax.all_to_all(parts, 'dp', 0, 0)]
    all_to_all x3 -> x0, blocking collectives: 52 us -> none  [the longest x2 34.2 us: exchange(): return lax.all_to_all(blocks, 'dp', 0, 0, axis_index_groups=same_core)]
    all_gather x2 -> x0, waiting for transfers between devices: 32.7 us -> none  [the longest x1 32.7 us: per_device(): lax.all_gather(act, 'dp', axis=0, tiled=True, axis_index_groups=same_core)]
    ppermute x9 -> x27, starting transfers between devices: 3.57 us -> 29 us  [swap(): return lax.ppermute(value, axis, xor_pairs(lax.axis_size(axis), k))]
    ppermute x9 -> x27, waiting for transfers between devices: 27.3 us -> 49.3 us  [swap(): return lax.ppermute(value, axis, xor_pairs(lax.axis_size(axis), k))]
    ppermute x1, waiting for transfers between devices: 0.01 us -> 4.25 us  [per_device(): below = lax.ppermute(head, 'space', up_pairs)]
    pallas_call x4, Pallas kernels: 16.5 us -> 20 us  [the longest x1 5.53 us: strip_wgrad(): pl.pallas_call(strip_kernel(count, width), out_shape=[half, half], in_spe...]
    all_to_all x4, starting transfers between devices: 15.8 us -> 18.7 us  [the longest x1 5.11 us: strips_shared(): lax.all_to_all(jnp.broadcast_to(mine, (count,) + mine.shape), 'space', 0, 0)]
  transfers between devices with their start and end apart: 17 -> 33, of which waited for: 10 -> 10; matrix products, arithmetic and copies ran while one was open for 6% -> 10% of each run, Pallas kernels for 6% -> 13%
where the time goes in v3:
time: 160 us; the launch traced here: 159 us
  waiting for transfers between devices  56.2 us (35%)
  starting transfers between devices  54 us (34%)
  local copies, waits for them, and re-layouts  20.6 us (13%)
  Pallas kernels  20 us (12%)
  other arithmetic  6.99 us (4%)
    ppermute x27, waiting for transfers between devices, swap(): return lax.ppermute(value, axis, xor_pairs(lax.axis_size(axis), k))  49.3 us
    ppermute x27, starting transfers between devices, swap(): return lax.ppermute(value, axis, xor_pairs(lax.axis_size(axis), k))  29 us
    unnamed x46, local copies, waits for them, and re-layouts  9.64 us
    pallas_call x1, Pallas kernels, strip_wgrad(): pl.pallas_call(strip_kernel(count, width), out_shape=[half, half], in_spe...  5.53 us
    pallas_call x1, Pallas kernels, gated(): pl.pallas_call(gated_kernel(count, width), out_shape=[jax.ShapeDtypeStruc...  5.47 us
    all_to_all x1, starting transfers between devices, strips_shared(): lax.all_to_all(jnp.broadcast_to(mine, (count,) + mine.shape), 'space', 0, 0)  5.11 us
    all_to_all x1, starting transfers between devices, per_device(): p_cots = lax.all_to_all(pieces, 'space', 0, 0)  5.09 us
    ppermute x1, starting transfers between devices, per_device(): above = lax.ppermute(tail, 'space', down_pairs)  4.94 us
  transfers between devices with their start and end apart: 33, of which 10 were waited for; matrix products, arithmetic and copies ran while one was open for 10% of the time, Pallas kernels for 13%

profile of v3, /device:TPU:0, one launch (start us, length us, event | category | flops | bytes accessed | tf_op | source)
XLA Modules:
  0.0 158.8 jit_solution(2717978594287849564)
XLA Ops:
  0.6 0.9 slice_bitcast_fusion.2
  1.5 1.0 fusion.10
  2.5 4.9 %collective-permute-start = (bf16[144,512]{1,0:T(8,128)(2,1)S(1)}, bf16[144,512]{1,0:T(8,128)(2,1)S(1)}, u32[]{:S(2)}, u32[]{:S(2)}) collective-permute-start(bf16[144,512]{1,0:T(8,128)(2,1)S(1)} %pad_maximum_fusion.2), channel_id=1, source_target_pairs={{0,1},{1,2},{2,3},{4,5},{5,6},{6,7},{8,9},{9,10},{10,11},{12,13},{... | collective-permute-start | bytes 442376 | tf_op jit(solution)/shard_map/ppermute | solution.py:313
  7.5 1.3 collective-permute-start.1
  8.8 1.8 %collective-permute-done = bf16[144,512]{1,0:T(8,128)(2,1)S(1)} collective-permute-done((bf16[144,512]{1,0:T(8,128)(2,1)S(1)}, bf16[144,512]{1,0:T(8,128)(2,1)S(1)}, u32[]{:S(2)}, u32[]{:S(2)}) %collective-permute-start) | collective-permute-done | bytes 147488 | tf_op jit(solution)/shard_map/ppermute | solution.py:313
  10.5 4.2 %collective-permute-done.1 = bf16[144,512]{1,0:T(8,128)(2,1)} collective-permute-done((bf16[144,512]{1,0:T(8,128)(2,1)S(1)}, bf16[144,512]{1,0:T(8,128)(2,1)}, u32[]{:S(2)}, u32[]{:S(2)}) %collective-permute-start.1) | collective-permute-done | bytes 147488 | tf_op jit(solution)/shard_map/ppermute | solution.py:314
  14.8 1.3 broadcast_in_dim.20
  16.1 4.0 %all-to-all-start = ((bf16[4,384,512]{2,1,0:T(8,128)(2,1)}), bf16[4,384,512]{2,1,0:T(8,128)(2,1)S(1)}, u32[]{:S(2)}, u32[]{:S(2)}) async-start(bf16[4,384,512]{2,1,0:T(8,128)(2,1)} %broadcast_in_dim.20), calls=%async_computation | async-start | bytes 3145728 | tf_op jit(solution)/shard_map/all_to_all | solution.py:319
  20.1 1.4 copy.23
  21.5 1.9 %reshape.56.refs_7_ = bf16[64,4608]{1,0:T(8,128)(2,1)S(1)} reshape(bf16[64,3,3,512]{3,2,1,0:T(4,128)(2,1)} %copy.23) | data formatting | bytes 1179648 | tf_op jit(solution)/shard_map/reshape | solution.py:305
  23.4 1.6 collective-permute-start.3
  25.0 1.5 collective-permute-start.5
  26.5 0.5 collective-permute-start.7
  27.0 0.8 concatenate.22
  28.1 11.6 %collective-permute-done.3.refs_9_ = bf16[64,4608]{1,0:T(8,128)(2,1)} collective-permute-done((bf16[64,4608]{1,0:T(8,128)(2,1)S(1)}, bf16[64,4608]{1,0:T(8,128)(2,1)}, u32[]{:S(2)}, u32[]{:S(2)}) %collective-permute-start.3) | collective-permute-done | bytes 589856 | tf_op jit(solution)/shard_map/ppermute | solution.py:21
  39.7 13.4 %collective-permute-done.5.refs_11_ = bf16[64,4608]{1,0:T(8,128)(2,1)} collective-permute-done((bf16[64,4608]{1,0:T(8,128)(2,1)S(1)}, bf16[64,4608]{1,0:T(8,128)(2,1)}, u32[]{:S(2)}, u32[]{:S(2)}) %collective-permute-start.5) | collective-permute-done | bytes 589856 | tf_op jit(solution)/shard_map/ppermute | solution.py:21
  53.2 0.6 collective-permute-start.8
  53.8 0.8 slice_bitcast_fusion
  54.7 0.6 collective-permute-start.9
  55.3 1.5 collective-permute-start.10
  56.8 1.4 collective-permute-start.11
  58.2 0.8 dynamic-slice_bitcast_fusion.5
  59.0 0.6 collective-permute-start.12
  59.7 0.9 slice.59.refs_3_
  60.6 0.8 copy-done.14
  61.4 5.5 %gated.1 = (bf16[480,512]{1,0:T(8,128)(2,1)S(1)}, bf16[4,384,128]{2,1,0:T(8,128)(2,1)S(1)}) custom-call(s32[3]{0:T(128)S(1)} %pad_add_fusion.refs_0_.ids, bf16[96,512]{1,0:T(8,128)(2,1)S(1)} %slice.58.refs_1_, bf16[384,512]{1,0:T(8,128)(2,1)S(1)} %bitcast.69, bf16[96,512]{1,0:T(8,128)(2,1)S(1)} %slice.59.refs_3_, ...), custom_call_target="tpu_custom_call" | custom-call | tf_op jit(solution)/shard_map/gated/pallas_call | solution.py:100
  66.9 0.8 copy-done.4
  67.6 0.7 copy-done.6
  68.4 5.1 %all-to-all-start.1 = ((bf16[4,384,128]{2,1,0:T(8,128)(2,1)}), bf16[4,384,128]{2,1,0:T(8,128)(2,1)S(1)}, u32[]{:S(2)}, u32[]{:S(2)}) async-start(bf16[4,384,128]{2,1,0:T(8,128)(2,1)} %copy-done.6), calls=%async_computation.1 | async-start | bytes 786432 | tf_op jit(solution)/shard_map/all_to_all | solution.py:324
  73.5 1.5 collective-permute-start.13
  75.0 1.9 %collective-permute-done.12.refs_6_ = bf16[480,128]{1,0:T(8,128)(2,1)S(1)} collective-permute-done((bf16[480,128]{1,0:T(8,128)(2,1)}, bf16[480,128]{1,0:T(8,128)(2,1)S(1)}, u32[]{:S(2)}, u32[]{:S(2)}) %collective-permute-start.12) | collective-permute-done | bytes 122912 | tf_op jit(solution)/shard_map/ppermute | solution.py:21
  76.9 1.5 collective-permute-start.14
  78.4 0.9 dynamic-slice_bitcast_fusion.4.refs_5_
  79.3 0.6 copy-done.7
  79.9 2.9 %collective-permute-done.14.refs_8_ = bf16[480,128]{1,0:T(8,128)(2,1)S(1)} collective-permute-done((bf16[480,128]{1,0:T(8,128)(2,1)}, bf16[480,128]{1,0:T(8,128)(2,1)S(1)}, u32[]{:S(2)}, u32[]{:S(2)}) %collective-permute-start.14) | collective-permute-done | bytes 122912 | tf_op jit(solution)/shard_map/ppermute | solution.py:21
  82.9 0.6 copy-done.9
  83.5 0.9 copy-done.8
  84.4 0.9 copy-done.10
  85.3 5.5 %strip_wgrad.1 = (f32[9,64,512]{2,1,0:T(8,128)S(1)}, f32[9,64,512]{2,1,0:T(8,128)}) custom-call(s32[3]{0:T(128)S(1)} %pad_add_fusion.refs_0_.ids, bf16[384,512]{1,0:T(8,128)(2,1)S(1)} %fusion.3.refs_1_, bf16[384,512]{1,0:T(8,128)(2,1)} %collective-permute-done.9.refs_2_, bf16[384,512]{1,0:T(8,128)(2,1)} %collective-permute-done.10.refs_3_, ...), custom_call_target="tpu_custom_call" | custom-call | tf_op jit(solution)/shard_map/strip_wgrad/pallas_call | solution.py:197
  90.9 1.0 copy-done.2
  91.9 4.1 %image_wgrad.1 = (f32[9,16,512]{2,1,0:T(8,128)S(1)}, bf16[8,9,16,512]{3,2,1,0:T(8,128)(2,1)}) custom-call(s32[3]{0:T(128)S(1)} %pad_add_fusion.refs_0_.ids, bf16[1536,512]{1,0:T(8,128)(2,1)S(1)} %bitcast.68, bf16[4,384,128]{2,1,0:T(8,128)(2,1)S(1)} %all-to-all-done.1.cots), custom_call_target="tpu_custom_call" | custom-call | tf_op jit(solution)/shard_map/image_wgrad/pallas_call | solution.py:230
  96.1 4.6 %all-to-all-start.2 = ((bf16[8,9,16,512]{3,2,1,0:T(8,128)(2,1)}), bf16[8,9,16,512]{3,2,1,0:T(8,128)(2,1)}, u32[]{:S(2)}, u32[]{:S(2)}) async-start(bf16[8,9,16,512]{3,2,1,0:T(8,128)(2,1)} %get-tuple-element.26), calls=%async_computation.2 | async-start | bytes 2359296 | tf_op jit(solution)/shard_map/all_to_all | solution.py:265
  100.7 1.5 add.51
  102.2 0.7 fusion.7
  103.3 3.8 %collective-permute-start.25 = (bf16[144,512]{1,0:T(8,128)(2,1)S(1)}, bf16[144,512]{1,0:T(8,128)(2,1)S(1)}, u32[]{:S(2)}, u32[]{:S(2)}) collective-permute-start(bf16[144,512]{1,0:T(8,128)(2,1)S(1)} %get-tuple-element.34), channel_id=1, source_target_pairs={{0,3},{1,2},{2,1},{3,0},{4,7},{5,6},{6,5},{7,4},{8,11},{9,10},{10,... | collective-permute-start | bytes 442376 | tf_op jit(solution)/shard_map/ppermute | solution.py:21
  107.1 0.5 copy.24
  107.6 0.8 reshape.57.refs_2_
  108.5 1.8 %collective-permute-start.15 = (bf16[64,4608]{1,0:T(8,128)(2,1)S(1)}, bf16[64,4608]{1,0:T(8,128)(2,1)S(1)}, u32[]{:S(2)}, u32[]{:S(2)}) collective-permute-start(bf16[64,4608]{1,0:T(8,128)(2,1)S(1)} %reshape.57.refs_2_), channel_id=1, source_target_pairs={{0,8},{4,12},{8,0},{12,4},{16,24},{20,28},{24,16},{28,20},{1,9},{5... | collective-permute-start | bytes 1769480 | tf_op jit(solution)/shard_map/ppermute | solution.py:21
  110.2 1.5 collective-permute-start.16
  112.0 4.8 %collective-permute-start.23 = (bf16[144,512]{1,0:T(8,128)(2,1)S(1)}, bf16[144,512]{1,0:T(8,128)(2,1)S(1)}, u32[]{:S(2)}, u32[]{:S(2)}) collective-permute-start(bf16[144,512]{1,0:T(8,128)(2,1)S(1)} %get-tuple-element.33), channel_id=1, source_target_pairs={{0,1},{1,0},{2,3},{3,2},{4,5},{5,4},{6,7},{7,6},{8,9},{9,8},{10,11... | collective-permute-start | bytes 442376 | tf_op jit(solution)/shard_map/ppermute | solution.py:21
  116.8 0.9 all-to-all-done.2
  117.8 1.6 %select_reduce_fusion = bf16[9,16,512]{2,1,0:T(8,128)(2,1)S(1)} fusion(bf16[8,9,16,512]{3,2,1,0:T(8,128)(2,1)} %all-to-all-done.2, f32[9,16,512]{2,1,0:T(8,128)S(1)} %get-tuple-element.25, pred[8]{0:T(512)(128)(4,1)S(1)} %iota_compare_fusion), kind=kLoop, calls=%fused_computation | loop fusion | flops 1695744 | bytes 1622024 | tf_op jit(solution)/shard_map/reduce_sum | solution.py:267
  119.4 0.9 broadcast_in_dim.22
  120.3 5.1 %all-to-all-start.3 = ((bf16[4,9,16,512]{3,2,1,0:T(8,128)(2,1)}), bf16[4,9,16,512]{3,2,1,0:T(8,128)(2,1)S(1)}, u32[]{:S(2)}, u32[]{:S(2)}) async-start(bf16[4,9,16,512]{3,2,1,0:T(8,128)(2,1)} %broadcast_in_dim.22), calls=%async_computation.3 | async-start | bytes 1179648 | tf_op jit(solution)/shard_map/all_to_all | solution.py:272
  125.4 1.0 fusion.6
  126.4 3.9 %collective-permute-start.28 = (bf16[144,512]{1,0:T(8,128)(2,1)S(1)}, bf16[144,512]{1,0:T(8,128)(2,1)S(1)}, u32[]{:S(2)}, u32[]{:S(2)}) collective-permute-start(bf16[144,512]{1,0:T(8,128)(2,1)S(1)} %fusion.6), channel_id=1, source_target_pairs={{0,3},{1,2},{2,1},{3,0},{4,7},{5,6},{6,5},{7,4},{8,11},{9,10},{10,... | collective-permute-start | bytes 442376 | tf_op jit(solution)/shard_map/ppermute | solution.py:21
  130.3 1.1 collective-permute-start.26
  131.4 11.0 %collective-permute-done.17.refs_8_ = bf16[64,4608]{1,0:T(8,128)(2,1)S(1)} collective-permute-done((bf16[64,4608]{1,0:T(8,128)(2,1)S(1)}, bf16[64,4608]{1,0:T(8,128)(2,1)S(1)}, u32[]{:S(2)}, u32[]{:S(2)}) %collective-permute-start.17) | collective-permute-done | bytes 589856 | tf_op jit(solution)/shard_map/ppermute | solution.py:21
  142.5 0.5 collective-permute-start.19
  143.0 7.8 %collective-permute-done.27 = bf16[144,512]{1,0:T(8,128)(2,1)S(1)} collective-permute-done((bf16[144,512]{1,0:T(8,128)(2,1)S(1)}, bf16[144,512]{1,0:T(8,128)(2,1)S(1)}, u32[]{:S(2)}, u32[]{:S(2)}) %collective-permute-start.27) | collective-permute-done | bytes 147488 | tf_op jit(solution)/shard_map/ppermute | solution.py:21
  151.0 1.2 convert_bitcast_fusion
  152.2 0.6 collective-permute-done.21.refs_9_
  152.8 4.9 %plain.1 = f32[384,512]{1,0:T(8,128)} custom-call(s32[3]{0:T(128)S(1)} %pad_add_fusion.refs_0_.ids, bf16[480,512]{1,0:T(8,128)(2,1)S(1)} %copy-done.5, bf16[64,4608]{1,0:T(8,128)(2,1)S(1)} %reshape.57.refs_2_, bf16[64,4608]{1,0:T(8,128)(2,1)S(1)} %collective-permute-done.18.refs_3_, bf16[64,4608]{1,0:T(8,128)(2,1)S(1)} %collective-permute-done.15.refs_4_, ...), custom_call_target="tpu_custom_call" | custom-call | tf_op jit(solution)/shard_map/plain/pallas_call | solution.py:139
  157.7 1.2 copy_convert_fusion
  (78 shorter events, 1.5 us)
Async XLA Ops:
  0.6 14.1 %copy-start.17 = (bf16[1,8,48,512]{3,2,1,0:T(8,128)(2,1)S(1)}, bf16[1,8,48,512]{3,2,1,0:T(8,128)(2,1)}, u32[]{:S(2)}) copy-start(bf16[1,8,48,512]{3,2,1,0:T(8,128)(2,1)} %param.5) | copy-start | bytes 1179652
  2.5 8.0 %collective-permute-start = (bf16[144,512]{1,0:T(8,128)(2,1)S(1)}, bf16[144,512]{1,0:T(8,128)(2,1)S(1)}, u32[]{:S(2)}, u32[]{:S(2)}) collective-permute-start(bf16[144,512]{1,0:T(8,128)(2,1)S(1)} %pad_maximum_fusion.2), channel_id=1, source_target_pairs={{0,1},{1,2},{2,3},{4,5},{5,6},{6,7},{8,9},{9,10},{10,11},{12,13},{... | collective-permute-start | bytes 442376 | tf_op jit(solution)/shard_map/ppermute | solution.py:313
  7.5 7.3 %collective-permute-start.1 = (bf16[144,512]{1,0:T(8,128)(2,1)S(1)}, bf16[144,512]{1,0:T(8,128)(2,1)}, u32[]{:S(2)}, u32[]{:S(2)}) collective-permute-start(bf16[144,512]{1,0:T(8,128)(2,1)S(1)} %pad_maximum_fusion.3), channel_id=1, source_target_pairs={{1,0},{2,1},{3,2},{5,4},{6,5},{7,6},{9,8},{10,9},{11,10},{13,12},{... | collective-permute-start | bytes 442376 | tf_op jit(solution)/shard_map/ppermute | solution.py:314
  10.5 17.6 %copy-start.18 = (bf16[144,512]{1,0:T(8,128)(2,1)}, bf16[144,512]{1,0:T(8,128)(2,1)S(1)}, u32[]{:S(2)}) copy-start(bf16[144,512]{1,0:T(8,128)(2,1)S(1)} %collective-permute-done) | copy-start | bytes 442372
  16.1 4.0 %copy-start.15 = (bf16[64,3,3,512]{3,0,2,1:T(8,128)(2,1)S(1)}, bf16[64,3,3,512]{3,0,2,1:T(8,128)(2,1)}, u32[]{:S(2)}) copy-start(bf16[64,3,3,512]{3,0,2,1:T(8,128)(2,1)} %param.9) | copy-start | bytes 1769476
  16.1 52.3 %all-to-all-start = ((bf16[4,384,512]{2,1,0:T(8,128)(2,1)}), bf16[4,384,512]{2,1,0:T(8,128)(2,1)S(1)}, u32[]{:S(2)}, u32[]{:S(2)}) async-start(bf16[4,384,512]{2,1,0:T(8,128)(2,1)} %broadcast_in_dim.20), calls=%async_computation | async-start | bytes 3145728 | tf_op jit(solution)/shard_map/all_to_all | solution.py:319
  20.1 6.9 %copy-start = (bf16[1,8,48,512]{3,2,1,0:T(8,128)(2,1)S(1)}, bf16[1,8,48,512]{3,2,1,0:T(8,128)(2,1)}, u32[]{:S(2)}) copy-start(bf16[1,8,48,512]{3,2,1,0:T(8,128)(2,1)} %param.7) | copy-start | bytes 1179652
  21.5 6.4 %copy-start.1 = (bf16[1,8,48,512]{3,2,1,0:T(8,128)(2,1)S(1)}, bf16[1,8,48,512]{3,2,1,0:T(8,128)(2,1)}, u32[]{:S(2)}) copy-start(bf16[1,8,48,512]{3,2,1,0:T(8,128)(2,1)} %param.6) | copy-start | bytes 1179652
  23.3 31.9 %collective-permute-start.2 = (bf16[64,4608]{1,0:T(8,128)(2,1)S(1)}, bf16[64,4608]{1,0:T(8,128)(2,1)}, u32[]{:S(2)}, u32[]{:S(2)}) collective-permute-start(bf16[64,4608]{1,0:T(8,128)(2,1)S(1)} %reshape.56.refs_7_), channel_id=1, source_target_pairs={{0,4},{4,0},{8,12},{12,8},{16,20},{20,16},{24,28},{28,24},{1,5},{5... | collective-permute-start | bytes 1769480 | tf_op jit(solution)/shard_map/ppermute | solution.py:21
  23.4 16.3 %collective-permute-start.3 = (bf16[64,4608]{1,0:T(8,128)(2,1)S(1)}, bf16[64,4608]{1,0:T(8,128)(2,1)}, u32[]{:S(2)}, u32[]{:S(2)}) collective-permute-start(bf16[64,4608]{1,0:T(8,128)(2,1)S(1)} %reshape.56.refs_7_), channel_id=1, source_target_pairs={{0,8},{4,12},{8,0},{12,4},{16,24},{20,28},{24,16},{28,20},{1,9},{5... | collective-permute-start | bytes 1769480 | tf_op jit(solution)/shard_map/ppermute | solution.py:21
  25.0 28.1 %collective-permute-start.5 = (bf16[64,4608]{1,0:T(8,128)(2,1)S(1)}, bf16[64,4608]{1,0:T(8,128)(2,1)}, u32[]{:S(2)}, u32[]{:S(2)}) collective-permute-start(bf16[64,4608]{1,0:T(8,128)(2,1)S(1)} %reshape.56.refs_7_), channel_id=1, source_target_pairs={{0,16},{4,20},{8,24},{12,28},{16,0},{20,4},{24,8},{28,12},{1,17},{... | collective-permute-start | bytes 1769480 | tf_op jit(solution)/shard_map/ppermute | solution.py:21
  26.5 26.7 %collective-permute-start.7 = (bf16[64,4608]{1,0:T(8,128)(2,1)S(1)}, bf16[64,4608]{1,0:T(8,128)(2,1)}, u32[]{:S(2)}, u32[]{:S(2)}) collective-permute-start(bf16[64,4608]{1,0:T(8,128)(2,1)S(1)} %reshape.56.refs_7_), channel_id=1, source_target_pairs={{0,24},{4,28},{8,16},{12,20},{16,8},{20,12},{24,0},{28,4},{1,25},{... | collective-permute-start | bytes 1769480 | tf_op jit(solution)/shard_map/ppermute | solution.py:21
  27.8 25.3 %copy-start.12 = (bf16[384,4,128]{2,1,0:T(4,128)(2,1)S(1)}, bf16[384,4,128]{2,1,0:T(4,128)(2,1)}, u32[]{:S(2)}) copy-start(bf16[384,4,128]{2,1,0:T(4,128)(2,1)} %concatenate.22) | copy-start | bytes 1179652
  28.1 31.5 %copy-start.19 = (bf16[144,512]{1,0:T(8,128)(2,1)S(1)}, bf16[144,512]{1,0:T(8,128)(2,1)}, u32[]{:S(2)}) copy-start(bf16[144,512]{1,0:T(8,128)(2,1)} %copy-done.18) | copy-start | bytes 442372
  39.7 17.1 %collective-permute-start.4 = (bf16[64,4608]{1,0:T(8,128)(2,1)}, bf16[64,4608]{1,0:T(8,128)(2,1)S(1)}, u32[]{:S(2)}, u32[]{:S(2)}) collective-permute-start(bf16[64,4608]{1,0:T(8,128)(2,1)} %collective-permute-done.3.refs_9_), channel_id=1, source_target_pairs={{0,4},{4,0},{8,12},{12,8},{16,20},{20,16},{24,28},{28,24},{1,5},{5... | collective-permute-start | bytes 1769480 | tf_op jit(solution)/shard_map/ppermute | solution.py:21
  53.1 5.9 %collective-permute-start.6 = (bf16[64,4608]{1,0:T(8,128)(2,1)}, bf16[64,4608]{1,0:T(8,128)(2,1)S(1)}, u32[]{:S(2)}, u32[]{:S(2)}) collective-permute-start(bf16[64,4608]{1,0:T(8,128)(2,1)} %collective-permute-done.5.refs_11_), channel_id=1, source_target_pairs={{0,4},{4,0},{8,12},{12,8},{16,20},{20,16},{24,28},{28,24},{1,5},{5... | collective-permute-start | bytes 1769480 | tf_op jit(solution)/shard_map/ppermute | solution.py:21
  53.2 7.3 %collective-permute-start.8 = (bf16[64,4608]{1,0:T(8,128)(2,1)}, bf16[64,4608]{1,0:T(8,128)(2,1)S(1)}, u32[]{:S(2)}, u32[]{:S(2)}) collective-permute-start(bf16[64,4608]{1,0:T(8,128)(2,1)} %collective-permute-done.7.refs_13_), channel_id=1, source_target_pairs={{0,4},{4,0},{8,12},{12,8},{16,20},{20,16},{24,28},{28,24},{1,5},{5... | collective-permute-start | bytes 1769480 | tf_op jit(solution)/shard_map/ppermute | solution.py:21
  54.7 5.9 %copy-start.13 = (bf16[480,4,128]{2,0,1:T(8,128)(2,1)}, bf16[480,4,128]{2,0,1:T(8,128)(2,1)S(1)}, u32[]{:S(2)}) copy-start(bf16[480,4,128]{2,0,1:T(8,128)(2,1)S(1)} %bitcast_dynamic-update-slice_fusion) | copy-start | bytes 1474564
  54.7 28.8 %collective-permute-start.9 = (bf16[384,512]{1,0:T(8,128)(2,1)S(1)}, bf16[384,512]{1,0:T(8,128)(2,1)}, u32[]{:S(2)}, u32[]{:S(2)}) collective-permute-start(bf16[384,512]{1,0:T(8,128)(2,1)S(1)} %fusion.3.refs_1_), channel_id=1, source_target_pairs={{0,8},{4,12},{8,0},{12,4},{16,24},{20,28},{24,16},{28,20},{1,9},{5... | collective-permute-start | bytes 1179656 | tf_op jit(solution)/shard_map/ppermute | solution.py:21
  55.3 28.2 %collective-permute-start.10 = (bf16[384,512]{1,0:T(8,128)(2,1)S(1)}, bf16[384,512]{1,0:T(8,128)(2,1)}, u32[]{:S(2)}, u32[]{:S(2)}) collective-permute-start(bf16[384,512]{1,0:T(8,128)(2,1)S(1)} %fusion.3.refs_1_), channel_id=1, source_target_pairs={{0,16},{4,20},{8,24},{12,28},{16,0},{20,4},{24,8},{28,12},{1,17},{... | collective-permute-start | bytes 1179656 | tf_op jit(solution)/shard_map/ppermute | solution.py:21
  56.8 26.7 %collective-permute-start.11 = (bf16[384,512]{1,0:T(8,128)(2,1)S(1)}, bf16[384,512]{1,0:T(8,128)(2,1)}, u32[]{:S(2)}, u32[]{:S(2)}) collective-permute-start(bf16[384,512]{1,0:T(8,128)(2,1)S(1)} %fusion.3.refs_1_), channel_id=1, source_target_pairs={{0,24},{4,28},{8,16},{12,20},{16,8},{20,12},{24,0},{28,4},{1,25},{... | collective-permute-start | bytes 1179656 | tf_op jit(solution)/shard_map/ppermute | solution.py:21
  59.0 17.9 %collective-permute-start.12 = (bf16[480,128]{1,0:T(8,128)(2,1)}, bf16[480,128]{1,0:T(8,128)(2,1)S(1)}, u32[]{:S(2)}, u32[]{:S(2)}) collective-permute-start(bf16[480,128]{1,0:T(8,128)(2,1)} %get-tuple-element.42), channel_id=1, source_target_pairs={{0,8},{4,12},{8,0},{12,4},{16,24},{20,28},{24,16},{28,20},{1,9},{5... | collective-permute-start | bytes 368648 | tf_op jit(solution)/shard_map/ppermute | solution.py:21
  60.6 0.8 copy-start.14
  66.9 0.8 copy-start.4
  67.6 0.8 copy-start.6
  68.4 23.5 %all-to-all-start.1 = ((bf16[4,384,128]{2,1,0:T(8,128)(2,1)}), bf16[4,384,128]{2,1,0:T(8,128)(2,1)S(1)}, u32[]{:S(2)}, u32[]{:S(2)}) async-start(bf16[4,384,128]{2,1,0:T(8,128)(2,1)} %copy-done.6), calls=%async_computation.1 | async-start | bytes 786432 | tf_op jit(solution)/shard_map/all_to_all | solution.py:324
  73.5 5.8 %collective-permute-start.13 = (bf16[480,128]{1,0:T(8,128)(2,1)}, bf16[480,128]{1,0:T(8,128)(2,1)S(1)}, u32[]{:S(2)}, u32[]{:S(2)}) collective-permute-start(bf16[480,128]{1,0:T(8,128)(2,1)} %get-tuple-element.41), channel_id=1, source_target_pairs={{0,16},{4,20},{8,24},{12,28},{16,0},{20,4},{24,8},{28,12},{1,17},{... | collective-permute-start | bytes 368648 | tf_op jit(solution)/shard_map/ppermute | solution.py:21
  76.9 6.0 %collective-permute-start.14 = (bf16[480,128]{1,0:T(8,128)(2,1)}, bf16[480,128]{1,0:T(8,128)(2,1)S(1)}, u32[]{:S(2)}, u32[]{:S(2)}) collective-permute-start(bf16[480,128]{1,0:T(8,128)(2,1)} %get-tuple-element.40), channel_id=1, source_target_pairs={{0,24},{4,28},{8,16},{12,20},{16,8},{20,12},{24,0},{28,4},{1,25},{... | collective-permute-start | bytes 368648 | tf_op jit(solution)/shard_map/ppermute | solution.py:21
  79.3 0.7 copy-start.7
  82.9 0.6 copy-start.9
  83.5 0.9 copy-start.8
  84.4 0.9 copy-start.10
  90.9 1.0 copy-start.2
  91.9 8.7 %collective-permute-start.22 = (f32[9,64,512]{2,1,0:T(8,128)}, f32[9,64,512]{2,1,0:T(8,128)}, u32[]{:S(2)}, u32[]{:S(2)}) collective-permute-start(f32[9,64,512]{2,1,0:T(8,128)} %get-tuple-element.32), channel_id=1, source_target_pairs={{0,4},{4,0},{8,12},{12,8},{16,20},{20,16},{24,28},{28,24},{1,5},{5... | collective-permute-start | bytes 3538952 | tf_op jit(solution)/shard_map/ppermute | solution.py:21
  96.1 4.6 %copy-start.3 = (f32[9,64,512]{2,1,0:T(8,128)S(1)}, f32[9,64,512]{2,1,0:T(8,128)}, u32[]{:S(2)}) copy-start(f32[9,64,512]{2,1,0:T(8,128)} %copy-done.2) | copy-start | bytes 3538948
  96.1 21.7 %all-to-all-start.2 = ((bf16[8,9,16,512]{3,2,1,0:T(8,128)(2,1)}), bf16[8,9,16,512]{3,2,1,0:T(8,128)(2,1)}, u32[]{:S(2)}, u32[]{:S(2)}) async-start(bf16[8,9,16,512]{3,2,1,0:T(8,128)(2,1)} %get-tuple-element.26), calls=%async_computation.2 | async-start | bytes 2359296 | tf_op jit(solution)/shard_map/all_to_all | solution.py:265
  102.2 1.1 copy-start.11
  102.2 4.9 %copy-start.16 = (bf16[64,3,3,512]{3,0,2,1:T(8,128)(2,1)S(1)}, bf16[64,3,3,512]{3,0,2,1:T(8,128)(2,1)}, u32[]{:S(2)}) copy-start(bf16[64,3,3,512]{3,0,2,1:T(8,128)(2,1)} %param.8) | copy-start | bytes 1769476
  103.3 8.8 %collective-permute-start.25 = (bf16[144,512]{1,0:T(8,128)(2,1)S(1)}, bf16[144,512]{1,0:T(8,128)(2,1)S(1)}, u32[]{:S(2)}, u32[]{:S(2)}) collective-permute-start(bf16[144,512]{1,0:T(8,128)(2,1)S(1)} %get-tuple-element.34), channel_id=1, source_target_pairs={{0,3},{1,2},{2,1},{3,0},{4,7},{5,6},{6,5},{7,4},{8,11},{9,10},{10,... | collective-permute-start | bytes 442376 | tf_op jit(solution)/shard_map/ppermute | solution.py:21
  108.5 21.9 %collective-permute-start.15 = (bf16[64,4608]{1,0:T(8,128)(2,1)S(1)}, bf16[64,4608]{1,0:T(8,128)(2,1)S(1)}, u32[]{:S(2)}, u32[]{:S(2)}) collective-permute-start(bf16[64,4608]{1,0:T(8,128)(2,1)S(1)} %reshape.57.refs_2_), channel_id=1, source_target_pairs={{0,8},{4,12},{8,0},{12,4},{16,24},{20,28},{24,16},{28,20},{1,9},{5... | collective-permute-start | bytes 1769480 | tf_op jit(solution)/shard_map/ppermute | solution.py:21
  110.2 21.2 %collective-permute-start.16 = (bf16[64,4608]{1,0:T(8,128)(2,1)S(1)}, bf16[64,4608]{1,0:T(8,128)(2,1)S(1)}, u32[]{:S(2)}, u32[]{:S(2)}) collective-permute-start(bf16[64,4608]{1,0:T(8,128)(2,1)S(1)} %reshape.57.refs_2_), channel_id=1, source_target_pairs={{0,16},{4,20},{8,24},{12,28},{16,0},{20,4},{24,8},{28,12},{1,17},{... | collective-permute-start | bytes 1769480 | tf_op jit(solution)/shard_map/ppermute | solution.py:21
  111.7 30.8 %collective-permute-start.17 = (bf16[64,4608]{1,0:T(8,128)(2,1)S(1)}, bf16[64,4608]{1,0:T(8,128)(2,1)S(1)}, u32[]{:S(2)}, u32[]{:S(2)}) collective-permute-start(bf16[64,4608]{1,0:T(8,128)(2,1)S(1)} %reshape.57.refs_2_), channel_id=1, source_target_pairs={{0,24},{4,28},{8,16},{12,20},{16,8},{20,12},{24,0},{28,4},{1,25},{... | collective-permute-start | bytes 1769480 | tf_op jit(solution)/shard_map/ppermute | solution.py:21
  112.0 13.4 %collective-permute-start.24 = (bf16[144,512]{1,0:T(8,128)(2,1)}, bf16[144,512]{1,0:T(8,128)(2,1)S(1)}, u32[]{:S(2)}, u32[]{:S(2)}) collective-permute-start(bf16[144,512]{1,0:T(8,128)(2,1)} %get-tuple-element.35), channel_id=1, source_target_pairs={{0,2},{1,3},{2,0},{3,1},{4,6},{5,7},{6,4},{7,5},{8,10},{9,11},{10,... | collective-permute-start | bytes 442376 | tf_op jit(solution)/shard_map/ppermute | solution.py:21
  112.0 13.4 %collective-permute-start.23 = (bf16[144,512]{1,0:T(8,128)(2,1)S(1)}, bf16[144,512]{1,0:T(8,128)(2,1)S(1)}, u32[]{:S(2)}, u32[]{:S(2)}) collective-permute-start(bf16[144,512]{1,0:T(8,128)(2,1)S(1)} %get-tuple-element.33), channel_id=1, source_target_pairs={{0,1},{1,0},{2,3},{3,2},{4,5},{5,4},{6,7},{7,6},{8,9},{9,8},{10,11... | collective-permute-start | bytes 442376 | tf_op jit(solution)/shard_map/ppermute | solution.py:21
  120.3 37.4 %all-to-all-start.3 = ((bf16[4,9,16,512]{3,2,1,0:T(8,128)(2,1)}), bf16[4,9,16,512]{3,2,1,0:T(8,128)(2,1)S(1)}, u32[]{:S(2)}, u32[]{:S(2)}) async-start(bf16[4,9,16,512]{3,2,1,0:T(8,128)(2,1)} %broadcast_in_dim.22), calls=%async_computation.3 | async-start | bytes 1179648 | tf_op jit(solution)/shard_map/all_to_all | solution.py:272
  126.4 16.6 %collective-permute-start.28 = (bf16[144,512]{1,0:T(8,128)(2,1)S(1)}, bf16[144,512]{1,0:T(8,128)(2,1)S(1)}, u32[]{:S(2)}, u32[]{:S(2)}) collective-permute-start(bf16[144,512]{1,0:T(8,128)(2,1)S(1)} %fusion.6), channel_id=1, source_target_pairs={{0,3},{1,2},{2,1},{3,0},{4,7},{5,6},{6,5},{7,4},{8,11},{9,10},{10,... | collective-permute-start | bytes 442376 | tf_op jit(solution)/shard_map/ppermute | solution.py:21
  130.3 20.4 %collective-permute-start.27 = (bf16[144,512]{1,0:T(8,128)(2,1)S(1)}, bf16[144,512]{1,0:T(8,128)(2,1)S(1)}, u32[]{:S(2)}, u32[]{:S(2)}) collective-permute-start(bf16[144,512]{1,0:T(8,128)(2,1)S(1)} %fusion.6), channel_id=1, source_target_pairs={{0,2},{1,3},{2,0},{3,1},{4,6},{5,7},{6,4},{7,5},{8,10},{9,11},{10,... | collective-permute-start | bytes 442376 | tf_op jit(solution)/shard_map/ppermute | solution.py:21
  130.3 20.4 %collective-permute-start.26 = (bf16[144,512]{1,0:T(8,128)(2,1)S(1)}, bf16[144,512]{1,0:T(8,128)(2,1)S(1)}, u32[]{:S(2)}, u32[]{:S(2)}) collective-permute-start(bf16[144,512]{1,0:T(8,128)(2,1)S(1)} %fusion.6), channel_id=1, source_target_pairs={{0,1},{1,0},{2,3},{3,2},{4,5},{5,4},{6,7},{7,6},{8,9},{9,8},{10,11... | collective-permute-start | bytes 442376 | tf_op jit(solution)/shard_map/ppermute | solution.py:21
  142.5 9.7 %collective-permute-start.18 = (bf16[64,4608]{1,0:T(8,128)(2,1)S(1)}, bf16[64,4608]{1,0:T(8,128)(2,1)S(1)}, u32[]{:S(2)}, u32[]{:S(2)}) collective-permute-start(bf16[64,4608]{1,0:T(8,128)(2,1)S(1)} %reshape.57.refs_2_), channel_id=1, source_target_pairs={{0,4},{4,0},{8,12},{12,8},{16,20},{20,16},{24,28},{28,24},{1,5},{5... | collective-permute-start | bytes 1769480 | tf_op jit(solution)/shard_map/ppermute | solution.py:21
  142.5 9.7 %collective-permute-start.19 = (bf16[64,4608]{1,0:T(8,128)(2,1)S(1)}, bf16[64,4608]{1,0:T(8,128)(2,1)S(1)}, u32[]{:S(2)}, u32[]{:S(2)}) collective-permute-start(bf16[64,4608]{1,0:T(8,128)(2,1)S(1)} %collective-permute-done.15.refs_4_), channel_id=1, source_target_pairs={{0,4},{4,0},{8,12},{12,8},{16,20},{20,16},{24,28},{28,24},{1,5},{5... | collective-permute-start | bytes 1769480 | tf_op jit(solution)/shard_map/ppermute | solution.py:21
  143.0 9.2 %collective-permute-start.20 = (bf16[64,4608]{1,0:T(8,128)(2,1)S(1)}, bf16[64,4608]{1,0:T(8,128)(2,1)S(1)}, u32[]{:S(2)}, u32[]{:S(2)}) collective-permute-start(bf16[64,4608]{1,0:T(8,128)(2,1)S(1)} %collective-permute-done.16.refs_6_), channel_id=1, source_target_pairs={{0,4},{4,0},{8,12},{12,8},{16,20},{20,16},{24,28},{28,24},{1,5},{5... | collective-permute-start | bytes 1769480 | tf_op jit(solution)/shard_map/ppermute | solution.py:21
  150.8 2.0 %collective-permute-start.21 = (bf16[64,4608]{1,0:T(8,128)(2,1)S(1)}, bf16[64,4608]{1,0:T(8,128)(2,1)S(1)}, u32[]{:S(2)}, u32[]{:S(2)}) collective-permute-start(bf16[64,4608]{1,0:T(8,128)(2,1)S(1)} %collective-permute-done.17.refs_8_), channel_id=1, source_target_pairs={{0,4},{4,0},{8,12},{12,8},{16,20},{20,16},{24,28},{28,24},{1,5},{5... | collective-permute-start | bytes 1769480 | tf_op jit(solution)/shard_map/ppermute | solution.py:21
  151.0 1.8 %copy-start.5 = (bf16[480,512]{1,0:T(8,128)(2,1)S(1)}, bf16[480,512]{1,0:T(8,128)(2,1)}, u32[]{:S(2)}) copy-start(bf16[480,512]{1,0:T(8,128)(2,1)} %copy-done.4) | copy-start | bytes 1474564

commit v4 on v3

--- a/solution.py
+++ b/solution.py
@@ -39,6 +39,37 @@
             part = jnp.dot(lhs, kernel[:, tap * c : (tap + 1) * c], preferred_element_type=F32)
             acc = part if acc is None else acc + part
     return acc
+
+
+def prep_kernel(owners, strips):
+    def body(h, g, out):
+        n, c = h.shape
+        each = c // (strips * owners)
+        src = lax.broadcasted_iota(jnp.int32, (c, c), 0)
+        dst = lax.broadcasted_iota(jnp.int32, (c, c), 1)
+        owner, rest = src // (strips * each), src % (strips * each)
+        goes = (rest // each) * (owners * each) + owner * each + rest % each
+        moved = jnp.dot(g[...], (goes == dst).astype(BF), preferred_element_type=F32).astype(BF)
+        hf = h[...].astype(F32)
+        act = (hf * jax.nn.sigmoid(hf)).astype(BF)
+        w = c // strips
+        for t in range(strips):
+            out[t, :, :c] = act
+            out[t, :, c:] = moved[:, t * w : (t + 1) * w]
+
+    return body
+
+
+def prepared(h, g, owners, strips):
+    n, c = h.shape
+    return pl.pallas_call(
+        prep_kernel(owners, strips),
+        out_shape=jax.ShapeDtypeStruct((strips, n, c + c // strips), BF),
+        in_specs=[VM, VM],
+        out_specs=VM,
+        compiler_params=PARAMS,
+        name="prepared",
+    )(h, g)
 
 
 def weight_copies(ids, weights, kernel, sems):
@@ -77,18 +108,10 @@
         )
         res = jnp.where(inside, acc, 0.0).astype(BF)
         out[...] = res
-        strips = parts.shape[0]
-        each = c // (strips * count)
-        src = lax.broadcasted_iota(jnp.int32, (c, c), 0)
-        dst = lax.broadcasted_iota(jnp.int32, (c, c), 1)
-        owner, rest = src // (strips * each), src % (strips * each)
-        goes = (rest // each) * (count * each) + owner * each + rest % each
-        moved = jnp.dot(
-            res[width : n - width], (goes == dst).astype(BF), preferred_element_type=F32
-        ).astype(BF)
-        w = c // strips
-        for t in range(strips):
-            parts[t] = moved[:, t * w : (t + 1) * w]
+        chips = parts.shape[0]
+        w = c // chips
+        for t in range(chips):
+            parts[t] = res[:, t * w : (t + 1) * w]
 
     return body
 
@@ -101,7 +124,7 @@
         gated_kernel(count, width),
         out_shape=[
             jax.ShapeDtypeStruct((rows, c), BF),
-            jax.ShapeDtypeStruct((pieces, n, c // pieces), BF),
+            jax.ShapeDtypeStruct((pieces, rows, c // pieces), BF),
         ],
         in_specs=[SM] + [VM] * 6 + [ANY] * count,
         out_specs=[VM, VM],
@@ -206,10 +229,12 @@
 
 
 def image_kernel(width):
-    def body(ids, field, cots, own, parts, lhs, acc):
-        count, n, w = cots.shape
-        zero = jnp.zeros((width, w), BF)
-        cot = jnp.concatenate([zero] + [cots[t] for t in range(count)] + [zero], axis=0)
+    def body(ids, image, own, parts, lhs, acc):
+        count, n, _ = image.shape
+        c = own.shape[2]
+        zero = jnp.zeros((width, acc.shape[1]), BF)
+        cot = jnp.concatenate([zero] + [image[t, :, c:] for t in range(count)] + [zero], axis=0)
+        field = jnp.concatenate([image[t, :, :c] for t in range(count)], axis=0)
         wgrad_products(lhs, [cot], [field], acc, width)
         owners, _, each, _ = parts.shape
         for d in range(owners):
@@ -223,9 +248,9 @@
     return body
 
 
-def image_wgrad(ids, field, cots, owners, width):
-    n, c = field.shape
-    w = cots.shape[2]
+def image_wgrad(ids, image, c, owners, width):
+    count, n, wide = image.shape
+    w = wide - c
     each = w // owners
     return pl.pallas_call(
         image_kernel(width),
@@ -233,12 +258,12 @@
             jax.ShapeDtypeStruct((9, each, c), F32),
             jax.ShapeDtypeStruct((owners, 9, each, c), BF),
         ],
-        in_specs=[SM, VM, VM],
+        in_specs=[SM, VM],
         out_specs=[VM, VM],
-        scratch_shapes=[pltpu.VMEM((9 * w, n), BF), pltpu.VMEM((9, w, c), F32)],
+        scratch_shapes=[pltpu.VMEM((9 * w, count * n), BF), pltpu.VMEM((9, w, c), F32)],
         compiler_params=PARAMS,
         name="image_wgrad",
-    )(ids, field, cots)
+    )(ids, image)
 
 
 def strips_summed(keep, send):
@@ -246,18 +271,23 @@
     owned, c = total.shape[1:]
     count = lax.axis_size("space")
     at = lax.axis_index("space")
-    blocks = total.reshape(count, 9 * owned // count, c)
-    mine = lax.dynamic_index_in_dim(blocks, at, 0, keepdims=False)
+    blocks = total.reshape(9, count, owned // count, c)
+    mine = lax.dynamic_index_in_dim(blocks, at, 1, keepdims=False)
     for k in range(1, count):
-        sent = lax.dynamic_index_in_dim(blocks, at ^ k, 0, keepdims=False).astype(BF)
+        sent = lax.dynamic_index_in_dim(blocks, at ^ k, 1, keepdims=False).astype(BF)
         mine = mine + swap(sent, "space", k).astype(F32)
-    mine = mine.astype(BF)
+    return mine.astype(BF)
+
+
+def strips_gathered(mine):
+    count = lax.axis_size("space")
+    at = lax.axis_index("space")
+    _, each, c = mine.shape
     got = jnp.stack([mine] + [swap(mine, "space", k) for k in range(1, count)])
-    whole = jnp.concatenate(
-        [lax.dynamic_index_in_dim(got, at ^ j, 0, keepdims=False) for j in range(count)], axis=0
+    whole = jnp.stack(
+        [lax.dynamic_index_in_dim(got, at ^ j, 0, keepdims=False) for j in range(count)]
     )
-    whole = whole.reshape(3, 3, owned, c).transpose(2, 0, 1, 3)
-    return whole.astype(F32)
+    return whole.transpose(0, 2, 1, 3).reshape(count * each, 3, 3, c).astype(F32)
 
 
 def images_summed(own, parts):
@@ -290,6 +320,8 @@
     at = lax.axis_index("space")
     ids = jnp.stack([me, at, strips - 1 - at]).astype(jnp.int32)
 
+    same_core = [[2 * q + k for q in range(chips)] for k in range(2)]
+
     def sent_to_chips(rows):
         return [swap(rows, "dp", k) for k in range(2, dp, 2)]
 
@@ -299,46 +331,39 @@
     x = inputs.reshape(n, c)
     h = pre_act.reshape(n, c)
     g = grad_out.reshape(n, c)
-    hf = h.astype(F32)
-    act = (hf * jax.nn.sigmoid(hf)).astype(BF)
+
+    image = lax.all_to_all(prepared(h, g, dp, strips), "space", 0, 0)
 
     w2 = w_second.reshape(owned, 9 * c)
     w2_shards = [w2] + sent_to_chips(w2)
-    shards = sent_to_pair(w2_shards)
-
     down_pairs = [(i, i + 1) for i in range(strips - 1)]
     up_pairs = [(i + 1, i) for i in range(strips - 1)]
     tail = jnp.concatenate([g[n - 2 * width :], h[n - width :]], axis=0)
     head = jnp.concatenate([g[: 2 * width], h[:width]], axis=0)
     above = lax.ppermute(tail, "space", down_pairs)
     below = lax.ppermute(head, "space", up_pairs)
+    w2_shards, above, below = lax.optimization_barrier((w2_shards, above, below))
+    shards = sent_to_pair(w2_shards)
     gup, hup = above[: 2 * width], above[2 * width :]
     gdown, hdown = below[: 2 * width], below[2 * width :]
 
-    x_late = after(x, above, below)
-    image = lax.all_to_all(jnp.broadcast_to(x_late, (strips, n, c)), "space", 0, 0)
-    image = image.reshape(strips * n, c)
-
-    pre_ext, pieces = gated(ids, gup, g, gdown, hup, h, hdown, shards, width, strips)
-    pieces = after(pieces, image)
-    p_cots = lax.all_to_all(pieces, "space", 0, 0)
-
-    g_ext = jnp.concatenate([gup[width:], g, gdown[:width]], axis=0)
-    blocks = g_ext.reshape(n + 2 * width, chips, c // chips).transpose(1, 0, 2)
-    act_late, blocks_late = after((act, blocks), *w2_shards[1:])
-    acts, g_cots = [act], [lax.dynamic_index_in_dim(blocks, me >> 1, 0, keepdims=False)]
-    for k in range(1, chips):
-        acts.append(swap(act_late, "dp", 2 * k))
-        part = lax.dynamic_index_in_dim(blocks_late, (me >> 1) ^ k, 0, keepdims=False)
-        g_cots.append(swap(part, "dp", 2 * k))
+    xs = [x] + sent_to_chips(after(x, *w2_shards[1:]))
+
+    pre_ext, pieces = gated(ids, gup, g, gdown, hup, h, hdown, shards, width, chips)
+    pieces, image, xs = lax.optimization_barrier((pieces, image, xs))
+    p_cots = lax.all_to_all(pieces, "dp", 0, 0, axis_index_groups=same_core)
+    chip = me >> 1
+    cots = [lax.dynamic_index_in_dim(p_cots, chip ^ k, 0, keepdims=False) for k in range(chips)]
+    own, parts = image_wgrad(ids, image, c, dp, width)
+    cots, own = lax.optimization_barrier((cots, own))
+    mine = strips_summed(*strip_wgrad(ids, xs, cots, width))
+    share = images_summed(own, after(parts, p_cots))
 
     w1 = w_first.reshape(owned, 9 * c)
-    w1_shards = [w1] + sent_to_chips(after(w1, *acts[1:], *g_cots[1:]))
-
-    share = images_summed(*image_wgrad(ids, image, p_cots, dp, width))
-    w1_shards = sent_to_pair(after(w1_shards, share))
-    first = strips_shared(share)
-    second = strips_summed(*strip_wgrad(ids, acts, g_cots, width))
+    w1_shards = [w1] + sent_to_chips(after(w1, p_cots))
+    w1_shards = sent_to_pair(after(w1_shards, mine))
+    first = strips_gathered(mine)
+    second = strips_shared(share)
     in_grad = plain(ids, pre_ext, w1_shards, width)
     return in_grad.reshape(inputs.shape), first, second
 

time: 160 us -> 161 us (level)
  waiting for transfers between devices: 56.2 us -> 45 us
  starting transfers between devices: 54 us -> 64.7 us
  local copies, waits for them, and re-layouts: 20.6 us -> 22.5 us
    ppermute x27 -> x24, waiting for transfers between devices: 49.3 us -> 19.5 us  [swap(): return lax.ppermute(value, axis, xor_pairs(lax.axis_size(axis), k))]
    ppermute x1, waiting for transfers between devices: 1.76 us -> 22.8 us  [per_device(): above = lax.ppermute(tail, 'space', down_pairs)]
    ppermute x27 -> x24, starting transfers between devices: 29 us -> 36.8 us  [swap(): return lax.ppermute(value, axis, xor_pairs(lax.axis_size(axis), k))]
    unnamed x46 -> x42, local copies, waits for them, and re-layouts: 9.64 us -> 15.8 us
    ppermute x1, waiting for transfers between devices: 4.25 us -> 0.01 us  [per_device(): below = lax.ppermute(head, 'space', up_pairs)]
    all_to_all x1, starting transfers between devices: 5.11 us -> 8.07 us  [strips_shared(): lax.all_to_all(jnp.broadcast_to(mine, (count,) + mine.shape), 'space', 0, 0)]
    all_to_all x2, waiting for transfers between devices: 0.01 us -> 2.63 us  [the longest x1 2.63 us: per_device(): p_cots = lax.all_to_all(pieces, 'dp', 0, 0, axis_index_groups=same_core)]
    slice x2, local copies, waits for them, and re-layouts: 1.83 us -> 0.02 us  [per_device(): head = jnp.concatenate([g[:2 * width], h[:width]], axis=0)]
  transfers between devices with their start and end apart: 33 -> 30, of which waited for: 10 -> 6; matrix products, arithmetic and copies ran while one was open for 10% -> 10% of each run, Pallas kernels for 13% -> 6%
where the time goes in v4:
time: 161 us; the launch traced here: 160 us
  starting transfers between devices  64.7 us (40%)
  waiting for transfers between devices  45 us (28%)
  local copies, waits for them, and re-layouts  22.5 us (14%)
  Pallas kernels  19.8 us (12%)
  other arithmetic  6.77 us (4%)
    ppermute x24, starting transfers between devices, swap(): return lax.ppermute(value, axis, xor_pairs(lax.axis_size(axis), k))  36.8 us
    ppermute x1, waiting for transfers between devices, per_device(): above = lax.ppermute(tail, 'space', down_pairs)  22.8 us
    ppermute x24, waiting for transfers between devices, swap(): return lax.ppermute(value, axis, xor_pairs(lax.axis_size(axis), k))  19.5 us
    unnamed x42, local copies, waits for them, and re-layouts  15.8 us
    all_to_all x1, starting transfers between devices, strips_shared(): lax.all_to_all(jnp.broadcast_to(mine, (count,) + mine.shape), 'space', 0, 0)  8.07 us
    all_to_all x1, starting transfers between devices, per_device(): image = lax.all_to_all(prepared(h, g, dp, strips), 'space', 0, 0)  6.45 us
    pallas_call x1, Pallas kernels, plain(): pl.pallas_call(plain_kernel(count, width), out_shape=jax.ShapeDtypeStruct...  5.39 us
    pallas_call x1, Pallas kernels, gated(): pl.pallas_call(gated_kernel(count, width), out_shape=[jax.ShapeDtypeStruc...  5.12 us
  transfers between devices with their start and end apart: 30, of which 6 were waited for; matrix products, arithmetic and copies ran while one was open for 10% of the time, Pallas kernels for 6%

profile of v4, /device:TPU:0, one launch (start us, length us, event | category | flops | bytes accessed | tf_op | source)
XLA Modules:
  0.0 159.8 jit_solution(6557569160665906542)
XLA Ops:
  0.6 1.0 copy-done.1
  1.6 1.0 copy-done.3
  2.6 0.6 prepared.1
  3.2 1.3 copy-done
  4.5 6.5 %all-to-all-start = ((bf16[4,384,640]{2,1,0:T(8,128)(2,1)}), bf16[4,384,640]{2,1,0:T(8,128)(2,1)S(1)}, u32[]{:S(2)}, u32[]{:S(2)}) async-start(bf16[4,384,640]{2,1,0:T(8,128)(2,1)} %copy-done), calls=%async_computation | async-start | bytes 3932160 | tf_op jit(solution)/shard_map/all_to_all | solution.py:335
  11.0 1.4 copy.23
  12.4 1.9 %reshape.44.refs_7_ = bf16[64,4608]{1,0:T(8,128)(2,1)S(1)} reshape(bf16[64,3,3,512]{3,2,1,0:T(4,128)(2,1)} %copy.23) | data formatting | bytes 1179648 | tf_op jit(solution)/shard_map/reshape | solution.py:337
  14.2 1.6 collective-permute-start
  15.8 1.5 collective-permute-start.1
  17.3 0.5 collective-permute-start.2
  17.9 3.9 %collective-permute-start.3 = (bf16[144,512]{1,0:T(8,128)(2,1)S(1)}, bf16[144,512]{1,0:T(8,128)(2,1)S(1)}, u32[]{:S(2)}, u32[]{:S(2)}) collective-permute-start(bf16[144,512]{1,0:T(8,128)(2,1)S(1)} %pad_maximum_fusion.1), channel_id=1, source_target_pairs={{0,1},{1,2},{2,3},{4,5},{5,6},{6,7},{8,9},{9,10},{10,11},{12,13},{... | collective-permute-start | bytes 442376 | tf_op jit(solution)/shard_map/ppermute | solution.py:343
  21.8 1.3 collective-permute-start.4
  23.1 22.8 %collective-permute-done.3 = bf16[144,512]{1,0:T(8,128)(2,1)S(1)} collective-permute-done((bf16[144,512]{1,0:T(8,128)(2,1)S(1)}, bf16[144,512]{1,0:T(8,128)(2,1)S(1)}, u32[]{:S(2)}, u32[]{:S(2)}) %collective-permute-start.3) | collective-permute-done | bytes 147488 | tf_op jit(solution)/shard_map/ppermute | solution.py:343
  46.0 0.6 copy-done.19
  46.6 0.8 copy-done.5
  47.4 0.5 collective-permute-start.7
  47.9 0.8 copy-done.7
  48.7 0.5 collective-permute-start.5
  49.2 1.5 collective-permute-start.10
  50.8 0.8 copy-done.9
  51.6 1.4 collective-permute-start.11
  53.0 0.8 copy-done.11
  53.9 0.5 collective-permute-start.9
  54.5 0.9 slice.45.refs_3_
  55.4 0.8 slice.47.refs_6_
  56.2 1.1 copy-done.6
  57.3 1.1 copy-done.8
  58.3 1.1 copy-done.10
  59.4 1.1 copy-done.12
  60.5 5.1 %gated.1 = (bf16[480,512]{1,0:T(8,128)(2,1)S(1)}, bf16[4,480,128]{2,1,0:T(8,128)(2,1)S(1)}) custom-call(s32[3]{0:T(128)S(1)} %pad_add_fusion.refs_0_.ids, bf16[96,512]{1,0:T(8,128)(2,1)S(1)} %slice.44.refs_1_, bf16[384,512]{1,0:T(8,128)(2,1)S(1)} %bitcast.55, bf16[96,512]{1,0:T(8,128)(2,1)S(1)} %slice.45.refs_3_, bf16[48,512]{1,0:T(8,128)(2,1)S(1)} %slice.46.refs_4_, ...), custom_call_target="tpu_custom_call" | custom-call | tf_op jit(solution)/shard_map/gated/pallas_call | solution.py:123
  65.6 0.8 copy-done.13
  66.4 0.8 copy-done.15
  67.2 1.9 %collective-permute-done.10.refs_3_ = bf16[384,512]{1,0:T(8,128)(2,1)} collective-permute-done((bf16[384,512]{1,0:T(8,128)(2,1)}, bf16[384,512]{1,0:T(8,128)(2,1)}, u32[]{:S(2)}, u32[]{:S(2)}) %collective-permute-start.10) | collective-permute-done | bytes 393248 | tf_op jit(solution)/shard_map/ppermute | solution.py:21
  69.0 2.0 %collective-permute-done.9.refs_2_ = bf16[384,512]{1,0:T(8,128)(2,1)} collective-permute-done((bf16[384,512]{1,0:T(8,128)(2,1)}, bf16[384,512]{1,0:T(8,128)(2,1)}, u32[]{:S(2)}, u32[]{:S(2)}) %collective-permute-start.9) | collective-permute-done | bytes 393248 | tf_op jit(solution)/shard_map/ppermute | solution.py:21
  71.1 3.7 %all-to-all-start.1 = ((bf16[4,480,128]{2,1,0:T(8,128)(2,1)}), bf16[4,480,128]{2,1,0:T(8,128)(2,1)S(1)}, u32[]{:S(2)}, u32[]{:S(2)}) async-start(bf16[4,480,128]{2,1,0:T(8,128)(2,1)} %copy-done.15), calls=%async_computation.1 | async-start | bytes 983040 | tf_op jit(solution)/shard_map/all_to_all | solution.py:354
  74.8 4.1 %image_wgrad.1 = (f32[9,16,512]{2,1,0:T(8,128)S(1)}, bf16[8,9,16,512]{3,2,1,0:T(8,128)(2,1)}) custom-call(s32[3]{0:T(128)S(1)} %pad_add_fusion.refs_0_.ids, bf16[4,384,640]{2,1,0:T(8,128)(2,1)S(1)} %all-to-all-done.image), custom_call_target="tpu_custom_call" | custom-call | tf_op jit(solution)/shard_map/image_wgrad/pallas_call | solution.py:255
  78.9 2.6 %all-to-all-done.1 = bf16[4,480,128]{2,1,0:T(8,128)(2,1)S(1)} async-done(((bf16[4,480,128]{2,1,0:T(8,128)(2,1)}), bf16[4,480,128]{2,1,0:T(8,128)(2,1)S(1)}, u32[]{:S(2)}, u32[]{:S(2)}) %all-to-all-start.1) | async-done | bytes 491552 | tf_op jit(solution)/shard_map/all_to_all | solution.py:354
  81.6 4.6 %strip_wgrad.1 = (f32[9,64,512]{2,1,0:T(8,128)S(1)}, f32[9,64,512]{2,1,0:T(8,128)S(1)}) custom-call(s32[3]{0:T(128)S(1)} %pad_add_fusion.refs_0_.ids, bf16[384,512]{1,0:T(8,128)(2,1)} %bitcast.9.refs_1_, bf16[384,512]{1,0:T(8,128)(2,1)} %collective-permute-done.9.refs_2_, bf16[384,512]{1,0:T(8,128)(2,1)} %collective-permute-done.10.refs_3_, ...), custom_call_target="tpu_custom_call" | custom-call | tf_op jit(solution)/shard_map/strip_wgrad/pallas_call | solution.py:220
  86.3 4.5 %all-to-all-start.2 = ((bf16[8,9,16,512]{3,2,1,0:T(8,128)(2,1)}), bf16[8,9,16,512]{3,2,1,0:T(8,128)(2,1)}, u32[]{:S(2)}, u32[]{:S(2)}) async-start(bf16[8,9,16,512]{3,2,1,0:T(8,128)(2,1)} %get-tuple-element.62), calls=%async_computation.2 | async-start | bytes 2359296 | tf_op jit(solution)/shard_map/all_to_all | solution.py:295
  90.8 1.5 add.47
  92.4 0.9 copy-done.16
  93.3 14.2 %collective-permute-start.16 = (bf16[9,16,512]{2,1,0:T(8,128)(2,1)S(1)}, bf16[9,16,512]{2,1,0:T(8,128)(2,1)S(1)}, u32[]{:S(2)}, u32[]{:S(2)}) collective-permute-start(bf16[9,16,512]{2,1,0:T(8,128)(2,1)S(1)} %get-tuple-element.63), channel_id=1, source_target_pairs={{0,1},{1,0},{2,3},{3,2},{4,5},{5,4},{6,7},{7,6},{8,9},{9,8},{10,11... | collective-permute-start | bytes 442376 | tf_op jit(solution)/shard_map/ppermute | solution.py:21
  107.5 0.5 copy.24
  108.0 0.8 reshape.47.refs_2_
  108.8 1.8 %collective-permute-start.12 = (bf16[64,4608]{1,0:T(8,128)(2,1)S(1)}, bf16[64,4608]{1,0:T(8,128)(2,1)S(1)}, u32[]{:S(2)}, u32[]{:S(2)}) collective-permute-start(bf16[64,4608]{1,0:T(8,128)(2,1)S(1)} %reshape.47.refs_2_), channel_id=1, source_target_pairs={{0,8},{4,12},{8,0},{12,4},{16,24},{20,28},{24,16},{28,20},{1,9},{5... | collective-permute-start | bytes 1769480 | tf_op jit(solution)/shard_map/ppermute | solution.py:21
  110.6 1.5 collective-permute-start.13
  112.1 0.3 collective-permute-start.14
  112.4 0.5 collective-permute-start.17
  112.9 2.4 %collective-permute-start.18 = (bf16[9,16,512]{2,1,0:T(8,128)(2,1)S(1)}, bf16[9,16,512]{2,1,0:T(8,128)(2,1)S(1)}, u32[]{:S(2)}, u32[]{:S(2)}) collective-permute-start(bf16[9,16,512]{2,1,0:T(8,128)(2,1)S(1)} %get-tuple-element.64), channel_id=1, source_target_pairs={{0,3},{1,2},{2,1},{3,0},{4,7},{5,6},{6,5},{7,4},{8,11},{9,10},{10,... | collective-permute-start | bytes 442376 | tf_op jit(solution)/shard_map/ppermute | solution.py:21
  115.3 1.6 select_reduce_fusion
  116.8 0.9 broadcast_in_dim.18
  117.7 8.1 %all-to-all-start.3 = ((bf16[4,9,16,512]{3,2,1,0:T(8,128)(2,1)}), bf16[4,9,16,512]{3,2,1,0:T(8,128)(2,1)}, u32[]{:S(2)}, u32[]{:S(2)}) async-start(bf16[4,9,16,512]{3,2,1,0:T(8,128)(2,1)} %broadcast_in_dim.18), calls=%async_computation.3 | async-start | bytes 1179648 | tf_op jit(solution)/shard_map/all_to_all | solution.py:302
  125.8 1.1 fusion.2
  126.9 4.5 %collective-permute-start.23 = (bf16[9,16,512]{2,1,0:T(8,128)(2,1)S(1)}, bf16[9,16,512]{2,1,0:T(8,128)(2,1)S(1)}, u32[]{:S(2)}, u32[]{:S(2)}) collective-permute-start(bf16[9,16,512]{2,1,0:T(8,128)(2,1)S(1)} %fusion.2), channel_id=1, source_target_pairs={{0,1},{1,0},{2,3},{3,2},{4,5},{5,4},{6,7},{7,6},{8,9},{9,8},{10,11... | collective-permute-start | bytes 442376 | tf_op jit(solution)/shard_map/ppermute | solution.py:21
  131.4 1.7 %collective-permute-start.24 = (bf16[9,16,512]{2,1,0:T(8,128)(2,1)S(1)}, bf16[9,16,512]{2,1,0:T(8,128)(2,1)S(1)}, u32[]{:S(2)}, u32[]{:S(2)}) collective-permute-start(bf16[9,16,512]{2,1,0:T(8,128)(2,1)S(1)} %fusion.2), channel_id=1, source_target_pairs={{0,2},{1,3},{2,0},{3,1},{4,6},{5,7},{6,4},{7,5},{8,10},{9,11},{10,... | collective-permute-start | bytes 442376 | tf_op jit(solution)/shard_map/ppermute | solution.py:21
  133.1 1.4 collective-permute-start.25
  134.5 3.6 %collective-permute-done.13.refs_6_ = bf16[64,4608]{1,0:T(8,128)(2,1)S(1)} collective-permute-done((bf16[64,4608]{1,0:T(8,128)(2,1)S(1)}, bf16[64,4608]{1,0:T(8,128)(2,1)S(1)}, u32[]{:S(2)}, u32[]{:S(2)}) %collective-permute-start.13) | collective-permute-done | bytes 589856 | tf_op jit(solution)/shard_map/ppermute | solution.py:21
  138.1 0.5 collective-permute-start.20
  138.6 11.9 %collective-permute-done.24 = bf16[9,16,512]{2,1,0:T(8,128)(2,1)S(1)} collective-permute-done((bf16[9,16,512]{2,1,0:T(8,128)(2,1)S(1)}, bf16[9,16,512]{2,1,0:T(8,128)(2,1)S(1)}, u32[]{:S(2)}, u32[]{:S(2)}) %collective-permute-start.24) | collective-permute-done | bytes 147488 | tf_op jit(solution)/shard_map/ppermute | solution.py:21
  150.5 0.1 pad_maximum_fusion
  150.7 0.1 convert_bitcast_fusion
  150.8 1.2 copy.27
  152.0 2.3 %copy_convert_fusion = f32[4,9,16,512]{3,2,0,1:T(8,128)} fusion(bf16[4,9,16,512]{3,2,1,0:T(8,128)(2,1)} %all-to-all-done.3), kind=kLoop, calls=%fused_computation.3 | loop fusion | flops 294912 | bytes 1769472 | tf_op jit(solution)/shard_map/convert_element_type | solution.py:305
  154.3 5.4 %plain.1 = f32[384,512]{1,0:T(8,128)} custom-call(s32[3]{0:T(128)S(1)} %pad_add_fusion.refs_0_.ids, bf16[480,512]{1,0:T(8,128)(2,1)S(1)} %copy-done.14, bf16[64,4608]{1,0:T(8,128)(2,1)S(1)} %reshape.47.refs_2_, bf16[64,4608]{1,0:T(8,128)(2,1)S(1)} %collective-permute-done.19.refs_3_, bf16[64,4608]{1,0:T(8,128)(2,1)S(1)} %collective-permute-done.12.refs_4_, ...), custom_call_target="tpu_custom_call" | custom-call | tf_op jit(solution)/shard_map/plain/pallas_call | solution.py:162
  (66 shorter events, 0.5 us)
Async XLA Ops:
  0.6 1.0 copy-start.1
  1.6 1.0 copy-start.3
  3.2 1.3 copy-start
  4.5 6.5 %copy-start.17 = (bf16[64,3,3,512]{3,0,2,1:T(8,128)(2,1)S(1)}, bf16[64,3,3,512]{3,0,2,1:T(8,128)(2,1)}, u32[]{:S(2)}) copy-start(bf16[64,3,3,512]{3,0,2,1:T(8,128)(2,1)} %param.9) | copy-start | bytes 1769476
  4.5 66.5 %all-to-all-start = ((bf16[4,384,640]{2,1,0:T(8,128)(2,1)}), bf16[4,384,640]{2,1,0:T(8,128)(2,1)S(1)}, u32[]{:S(2)}, u32[]{:S(2)}) async-start(bf16[4,384,640]{2,1,0:T(8,128)(2,1)} %copy-done), calls=%async_computation | async-start | bytes 3932160 | tf_op jit(solution)/shard_map/all_to_all | solution.py:335
  11.0 6.8 %copy-start.2 = (bf16[1,8,48,512]{3,2,1,0:T(8,128)(2,1)S(1)}, bf16[1,8,48,512]{3,2,1,0:T(8,128)(2,1)}, u32[]{:S(2)}) copy-start(bf16[1,8,48,512]{3,2,1,0:T(8,128)(2,1)} %param.7) | copy-start | bytes 1179652
  12.4 5.5 %copy-start.4 = (bf16[1,8,48,512]{3,2,1,0:T(8,128)(2,1)S(1)}, bf16[1,8,48,512]{3,2,1,0:T(8,128)(2,1)}, u32[]{:S(2)}) copy-start(bf16[1,8,48,512]{3,2,1,0:T(8,128)(2,1)} %param.6) | copy-start | bytes 1179652
  14.2 31.7 %collective-permute-start = (bf16[64,4608]{1,0:T(8,128)(2,1)S(1)}, bf16[64,4608]{1,0:T(8,128)(2,1)S(1)}, u32[]{:S(2)}, u32[]{:S(2)}) collective-permute-start(bf16[64,4608]{1,0:T(8,128)(2,1)S(1)} %reshape.44.refs_7_), channel_id=1, source_target_pairs={{0,8},{4,12},{8,0},{12,4},{16,24},{20,28},{24,16},{28,20},{1,9},{5... | collective-permute-start | bytes 1769480 | tf_op jit(solution)/shard_map/ppermute | solution.py:21
  15.8 30.1 %collective-permute-start.1 = (bf16[64,4608]{1,0:T(8,128)(2,1)S(1)}, bf16[64,4608]{1,0:T(8,128)(2,1)S(1)}, u32[]{:S(2)}, u32[]{:S(2)}) collective-permute-start(bf16[64,4608]{1,0:T(8,128)(2,1)S(1)} %reshape.44.refs_7_), channel_id=1, source_target_pairs={{0,16},{4,20},{8,24},{12,28},{16,0},{20,4},{24,8},{28,12},{1,17},{... | collective-permute-start | bytes 1769480 | tf_op jit(solution)/shard_map/ppermute | solution.py:21
  17.3 28.6 %collective-permute-start.2 = (bf16[64,4608]{1,0:T(8,128)(2,1)S(1)}, bf16[64,4608]{1,0:T(8,128)(2,1)}, u32[]{:S(2)}, u32[]{:S(2)}) collective-permute-start(bf16[64,4608]{1,0:T(8,128)(2,1)S(1)} %reshape.44.refs_7_), channel_id=1, source_target_pairs={{0,24},{4,28},{8,16},{12,20},{16,8},{20,12},{24,0},{28,4},{1,25},{... | collective-permute-start | bytes 1769480 | tf_op jit(solution)/shard_map/ppermute | solution.py:21
  17.9 28.1 %collective-permute-start.3 = (bf16[144,512]{1,0:T(8,128)(2,1)S(1)}, bf16[144,512]{1,0:T(8,128)(2,1)S(1)}, u32[]{:S(2)}, u32[]{:S(2)}) collective-permute-start(bf16[144,512]{1,0:T(8,128)(2,1)S(1)} %pad_maximum_fusion.1), channel_id=1, source_target_pairs={{0,1},{1,2},{2,3},{4,5},{5,6},{6,7},{8,9},{9,10},{10,11},{12,13},{... | collective-permute-start | bytes 442376 | tf_op jit(solution)/shard_map/ppermute | solution.py:343
  21.8 24.1 %collective-permute-start.4 = (bf16[144,512]{1,0:T(8,128)(2,1)S(1)}, bf16[144,512]{1,0:T(8,128)(2,1)S(1)}, u32[]{:S(2)}, u32[]{:S(2)}) collective-permute-start(bf16[144,512]{1,0:T(8,128)(2,1)S(1)} %pad_maximum_fusion.2), channel_id=1, source_target_pairs={{1,0},{2,1},{3,2},{5,4},{6,5},{7,6},{9,8},{10,9},{11,10},{13,12},{... | collective-permute-start | bytes 442376 | tf_op jit(solution)/shard_map/ppermute | solution.py:344
  45.9 0.7 copy-start.19
  46.6 4.2 %collective-permute-start.6 = (bf16[64,4608]{1,0:T(8,128)(2,1)S(1)}, bf16[64,4608]{1,0:T(8,128)(2,1)S(1)}, u32[]{:S(2)}, u32[]{:S(2)}) collective-permute-start(bf16[64,4608]{1,0:T(8,128)(2,1)S(1)} %collective-permute-done.refs_9_), channel_id=1, source_target_pairs={{0,4},{4,0},{8,12},{12,8},{16,20},{20,16},{24,28},{28,24},{1,5},{5... | collective-permute-start | bytes 1769480 | tf_op jit(solution)/shard_map/ppermute | solution.py:21
  46.6 0.8 copy-start.5
  47.4 5.6 %collective-permute-start.7 = (bf16[64,4608]{1,0:T(8,128)(2,1)S(1)}, bf16[64,4608]{1,0:T(8,128)(2,1)S(1)}, u32[]{:S(2)}, u32[]{:S(2)}) collective-permute-start(bf16[64,4608]{1,0:T(8,128)(2,1)S(1)} %collective-permute-done.1.refs_11_), channel_id=1, source_target_pairs={{0,4},{4,0},{8,12},{12,8},{16,20},{20,16},{24,28},{28,24},{1,5},{5... | collective-permute-start | bytes 1769480 | tf_op jit(solution)/shard_map/ppermute | solution.py:21
  47.9 0.8 copy-start.7
  48.7 7.5 %collective-permute-start.8 = (bf16[64,4608]{1,0:T(8,128)(2,1)}, bf16[64,4608]{1,0:T(8,128)(2,1)}, u32[]{:S(2)}, u32[]{:S(2)}) collective-permute-start(bf16[64,4608]{1,0:T(8,128)(2,1)} %collective-permute-done.2.refs_13_), channel_id=1, source_target_pairs={{0,4},{4,0},{8,12},{12,8},{16,20},{20,16},{24,28},{28,24},{1,5},{5... | collective-permute-start | bytes 1769480 | tf_op jit(solution)/shard_map/ppermute | solution.py:21
  48.7 7.5 %collective-permute-start.5 = (bf16[64,4608]{1,0:T(8,128)(2,1)S(1)}, bf16[64,4608]{1,0:T(8,128)(2,1)}, u32[]{:S(2)}, u32[]{:S(2)}) collective-permute-start(bf16[64,4608]{1,0:T(8,128)(2,1)S(1)} %reshape.44.refs_7_), channel_id=1, source_target_pairs={{0,4},{4,0},{8,12},{12,8},{16,20},{20,16},{24,28},{28,24},{1,5},{5... | collective-permute-start | bytes 1769480 | tf_op jit(solution)/shard_map/ppermute | solution.py:21
  49.2 19.8 %collective-permute-start.10 = (bf16[384,512]{1,0:T(8,128)(2,1)}, bf16[384,512]{1,0:T(8,128)(2,1)}, u32[]{:S(2)}, u32[]{:S(2)}) collective-permute-start(bf16[384,512]{1,0:T(8,128)(2,1)} %bitcast.9.refs_1_), channel_id=1, source_target_pairs={{0,16},{4,20},{8,24},{12,28},{16,0},{20,4},{24,8},{28,12},{1,17},{... | collective-permute-start | bytes 1179656 | tf_op jit(solution)/shard_map/ppermute | solution.py:21
  50.8 0.8 copy-start.9
  51.6 17.4 %collective-permute-start.11 = (bf16[384,512]{1,0:T(8,128)(2,1)}, bf16[384,512]{1,0:T(8,128)(2,1)}, u32[]{:S(2)}, u32[]{:S(2)}) collective-permute-start(bf16[384,512]{1,0:T(8,128)(2,1)} %bitcast.9.refs_1_), channel_id=1, source_target_pairs={{0,24},{4,28},{8,16},{12,20},{16,8},{20,12},{24,0},{28,4},{1,25},{... | collective-permute-start | bytes 1179656 | tf_op jit(solution)/shard_map/ppermute | solution.py:21
  53.0 0.8 copy-start.11
  53.9 17.2 %collective-permute-start.9 = (bf16[384,512]{1,0:T(8,128)(2,1)}, bf16[384,512]{1,0:T(8,128)(2,1)}, u32[]{:S(2)}, u32[]{:S(2)}) collective-permute-start(bf16[384,512]{1,0:T(8,128)(2,1)} %bitcast.9.refs_1_), channel_id=1, source_target_pairs={{0,8},{4,12},{8,0},{12,4},{16,24},{20,28},{24,16},{28,20},{1,9},{5... | collective-permute-start | bytes 1179656 | tf_op jit(solution)/shard_map/ppermute | solution.py:21
  56.2 1.1 copy-start.6
  57.3 1.1 copy-start.8
  58.3 1.1 copy-start.10
  59.4 1.1 copy-start.12
  65.6 0.8 copy-start.13
  66.4 0.8 copy-start.15
  71.1 10.5 %all-to-all-start.1 = ((bf16[4,480,128]{2,1,0:T(8,128)(2,1)}), bf16[4,480,128]{2,1,0:T(8,128)(2,1)S(1)}, u32[]{:S(2)}, u32[]{:S(2)}) async-start(bf16[4,480,128]{2,1,0:T(8,128)(2,1)} %copy-done.15), calls=%async_computation.1 | async-start | bytes 983040 | tf_op jit(solution)/shard_map/all_to_all | solution.py:354
  86.2 4.6 %collective-permute-start.15 = (f32[9,64,512]{2,1,0:T(8,128)S(1)}, f32[9,64,512]{2,1,0:T(8,128)}, u32[]{:S(2)}, u32[]{:S(2)}) collective-permute-start(f32[9,64,512]{2,1,0:T(8,128)S(1)} %get-tuple-element.55), channel_id=1, source_target_pairs={{0,4},{4,0},{8,12},{12,8},{16,20},{20,16},{24,28},{28,24},{1,5},{5... | collective-permute-start | bytes 3538952 | tf_op jit(solution)/shard_map/ppermute | solution.py:21
  86.3 29.0 %all-to-all-start.2 = ((bf16[8,9,16,512]{3,2,1,0:T(8,128)(2,1)}), bf16[8,9,16,512]{3,2,1,0:T(8,128)(2,1)}, u32[]{:S(2)}, u32[]{:S(2)}) async-start(bf16[8,9,16,512]{3,2,1,0:T(8,128)(2,1)} %get-tuple-element.62), calls=%async_computation.2 | async-start | bytes 2359296 | tf_op jit(solution)/shard_map/all_to_all | solution.py:295
  92.3 1.0 copy-start.16
  92.3 15.2 %copy-start.18 = (bf16[64,3,3,512]{3,0,2,1:T(8,128)(2,1)S(1)}, bf16[64,3,3,512]{3,0,2,1:T(8,128)(2,1)}, u32[]{:S(2)}) copy-start(bf16[64,3,3,512]{3,0,2,1:T(8,128)(2,1)} %param.8) | copy-start | bytes 1769476
  93.3 19.6 %collective-permute-start.16 = (bf16[9,16,512]{2,1,0:T(8,128)(2,1)S(1)}, bf16[9,16,512]{2,1,0:T(8,128)(2,1)S(1)}, u32[]{:S(2)}, u32[]{:S(2)}) collective-permute-start(bf16[9,16,512]{2,1,0:T(8,128)(2,1)S(1)} %get-tuple-element.63), channel_id=1, source_target_pairs={{0,1},{1,0},{2,3},{3,2},{4,5},{5,4},{6,7},{7,6},{8,9},{9,8},{10,11... | collective-permute-start | bytes 442376 | tf_op jit(solution)/shard_map/ppermute | solution.py:21
  108.8 24.2 %collective-permute-start.12 = (bf16[64,4608]{1,0:T(8,128)(2,1)S(1)}, bf16[64,4608]{1,0:T(8,128)(2,1)S(1)}, u32[]{:S(2)}, u32[]{:S(2)}) collective-permute-start(bf16[64,4608]{1,0:T(8,128)(2,1)S(1)} %reshape.47.refs_2_), channel_id=1, source_target_pairs={{0,8},{4,12},{8,0},{12,4},{16,24},{20,28},{24,16},{28,20},{1,9},{5... | collective-permute-start | bytes 1769480 | tf_op jit(solution)/shard_map/ppermute | solution.py:21
  110.6 27.5 %collective-permute-start.13 = (bf16[64,4608]{1,0:T(8,128)(2,1)S(1)}, bf16[64,4608]{1,0:T(8,128)(2,1)S(1)}, u32[]{:S(2)}, u32[]{:S(2)}) collective-permute-start(bf16[64,4608]{1,0:T(8,128)(2,1)S(1)} %reshape.47.refs_2_), channel_id=1, source_target_pairs={{0,16},{4,20},{8,24},{12,28},{16,0},{20,4},{24,8},{28,12},{1,17},{... | collective-permute-start | bytes 1769480 | tf_op jit(solution)/shard_map/ppermute | solution.py:21
  112.1 26.0 %collective-permute-start.14 = (bf16[64,4608]{1,0:T(8,128)(2,1)S(1)}, bf16[64,4608]{1,0:T(8,128)(2,1)S(1)}, u32[]{:S(2)}, u32[]{:S(2)}) collective-permute-start(bf16[64,4608]{1,0:T(8,128)(2,1)S(1)} %reshape.47.refs_2_), channel_id=1, source_target_pairs={{0,24},{4,28},{8,16},{12,20},{16,8},{20,12},{24,0},{28,4},{1,25},{... | collective-permute-start | bytes 1769480 | tf_op jit(solution)/shard_map/ppermute | solution.py:21
  112.4 13.4 %collective-permute-start.17 = (bf16[9,16,512]{2,1,0:T(8,128)(2,1)S(1)}, bf16[9,16,512]{2,1,0:T(8,128)(2,1)S(1)}, u32[]{:S(2)}, u32[]{:S(2)}) collective-permute-start(bf16[9,16,512]{2,1,0:T(8,128)(2,1)S(1)} %get-tuple-element.65), channel_id=1, source_target_pairs={{0,2},{1,3},{2,0},{3,1},{4,6},{5,7},{6,4},{7,5},{8,10},{9,11},{10,... | collective-permute-start | bytes 442376 | tf_op jit(solution)/shard_map/ppermute | solution.py:21
  112.9 12.9 %collective-permute-start.18 = (bf16[9,16,512]{2,1,0:T(8,128)(2,1)S(1)}, bf16[9,16,512]{2,1,0:T(8,128)(2,1)S(1)}, u32[]{:S(2)}, u32[]{:S(2)}) collective-permute-start(bf16[9,16,512]{2,1,0:T(8,128)(2,1)S(1)} %get-tuple-element.64), channel_id=1, source_target_pairs={{0,3},{1,2},{2,1},{3,0},{4,7},{5,6},{6,5},{7,4},{8,11},{9,10},{10,... | collective-permute-start | bytes 442376 | tf_op jit(solution)/shard_map/ppermute | solution.py:21
  117.7 34.2 %all-to-all-start.3 = ((bf16[4,9,16,512]{3,2,1,0:T(8,128)(2,1)}), bf16[4,9,16,512]{3,2,1,0:T(8,128)(2,1)}, u32[]{:S(2)}, u32[]{:S(2)}) async-start(bf16[4,9,16,512]{3,2,1,0:T(8,128)(2,1)} %broadcast_in_dim.18), calls=%async_computation.3 | async-start | bytes 1179648 | tf_op jit(solution)/shard_map/all_to_all | solution.py:302
  126.9 11.7 %collective-permute-start.23 = (bf16[9,16,512]{2,1,0:T(8,128)(2,1)S(1)}, bf16[9,16,512]{2,1,0:T(8,128)(2,1)S(1)}, u32[]{:S(2)}, u32[]{:S(2)}) collective-permute-start(bf16[9,16,512]{2,1,0:T(8,128)(2,1)S(1)} %fusion.2), channel_id=1, source_target_pairs={{0,1},{1,0},{2,3},{3,2},{4,5},{5,4},{6,7},{7,6},{8,9},{9,8},{10,11... | collective-permute-start | bytes 442376 | tf_op jit(solution)/shard_map/ppermute | solution.py:21
  131.4 19.1 %collective-permute-start.24 = (bf16[9,16,512]{2,1,0:T(8,128)(2,1)S(1)}, bf16[9,16,512]{2,1,0:T(8,128)(2,1)S(1)}, u32[]{:S(2)}, u32[]{:S(2)}) collective-permute-start(bf16[9,16,512]{2,1,0:T(8,128)(2,1)S(1)} %fusion.2), channel_id=1, source_target_pairs={{0,2},{1,3},{2,0},{3,1},{4,6},{5,7},{6,4},{7,5},{8,10},{9,11},{10,... | collective-permute-start | bytes 442376 | tf_op jit(solution)/shard_map/ppermute | solution.py:21
  133.1 17.5 %collective-permute-start.25 = (bf16[9,16,512]{2,1,0:T(8,128)(2,1)S(1)}, bf16[9,16,512]{2,1,0:T(8,128)(2,1)S(1)}, u32[]{:S(2)}, u32[]{:S(2)}) collective-permute-start(bf16[9,16,512]{2,1,0:T(8,128)(2,1)S(1)} %fusion.2), channel_id=1, source_target_pairs={{0,3},{1,2},{2,1},{3,0},{4,7},{5,6},{6,5},{7,4},{8,11},{9,10},{10,... | collective-permute-start | bytes 442376 | tf_op jit(solution)/shard_map/ppermute | solution.py:21
  138.1 16.2 %collective-permute-start.19 = (bf16[64,4608]{1,0:T(8,128)(2,1)S(1)}, bf16[64,4608]{1,0:T(8,128)(2,1)S(1)}, u32[]{:S(2)}, u32[]{:S(2)}) collective-permute-start(bf16[64,4608]{1,0:T(8,128)(2,1)S(1)} %reshape.47.refs_2_), channel_id=1, source_target_pairs={{0,4},{4,0},{8,12},{12,8},{16,20},{20,16},{24,28},{28,24},{1,5},{5... | collective-permute-start | bytes 1769480 | tf_op jit(solution)/shard_map/ppermute | solution.py:21
  138.1 16.2 %collective-permute-start.20 = (bf16[64,4608]{1,0:T(8,128)(2,1)S(1)}, bf16[64,4608]{1,0:T(8,128)(2,1)S(1)}, u32[]{:S(2)}, u32[]{:S(2)}) collective-permute-start(bf16[64,4608]{1,0:T(8,128)(2,1)S(1)} %collective-permute-done.12.refs_4_), channel_id=1, source_target_pairs={{0,4},{4,0},{8,12},{12,8},{16,20},{20,16},{24,28},{28,24},{1,5},{5... | collective-permute-start | bytes 1769480 | tf_op jit(solution)/shard_map/ppermute | solution.py:21
  138.6 15.7 %collective-permute-start.21 = (bf16[64,4608]{1,0:T(8,128)(2,1)S(1)}, bf16[64,4608]{1,0:T(8,128)(2,1)}, u32[]{:S(2)}, u32[]{:S(2)}) collective-permute-start(bf16[64,4608]{1,0:T(8,128)(2,1)S(1)} %collective-permute-done.13.refs_6_), channel_id=1, source_target_pairs={{0,4},{4,0},{8,12},{12,8},{16,20},{20,16},{24,28},{28,24},{1,5},{5... | collective-permute-start | bytes 1769480 | tf_op jit(solution)/shard_map/ppermute | solution.py:21
  150.5 3.7 %collective-permute-start.22 = (bf16[64,4608]{1,0:T(8,128)(2,1)S(1)}, bf16[64,4608]{1,0:T(8,128)(2,1)}, u32[]{:S(2)}, u32[]{:S(2)}) collective-permute-start(bf16[64,4608]{1,0:T(8,128)(2,1)S(1)} %collective-permute-done.14.refs_8_), channel_id=1, source_target_pairs={{0,4},{4,0},{8,12},{12,8},{16,20},{20,16},{24,28},{28,24},{1,5},{5... | collective-permute-start | bytes 1769480 | tf_op jit(solution)/shard_map/ppermute | solution.py:21
  151.9 2.3 %copy-start.14 = (bf16[480,512]{1,0:T(8,128)(2,1)S(1)}, bf16[480,512]{1,0:T(8,128)(2,1)}, u32[]{:S(2)}) copy-start(bf16[480,512]{1,0:T(8,128)(2,1)} %copy-done.13) | copy-start | bytes 1474564

commit v5 on v4

--- a/solution.py
+++ b/solution.py
@@ -8,7 +8,7 @@
 BF = jnp.bfloat16
 F32 = jnp.float32
 PARAMS = pltpu.CompilerParams(vmem_limit_bytes=48 * 1024 * 1024)
-ANY = pl.BlockSpec(memory_space=pl.ANY)
+ANY = pl.BlockSpec(memory_space=pltpu.HBM)
 VM = pl.BlockSpec(memory_space=pltpu.VMEM)
 SM = pl.BlockSpec(memory_space=pltpu.SMEM)
 
@@ -30,15 +30,21 @@
     return left, flat, right
 
 
-def products(field, kernel, n, c, width):
+def products(field, kernel, copies, n, c, width):
     acc = None
     for r in range(3):
+        for copy in copies[r]:
+            copy.wait()
         for s in range(3):
             tap = 3 * r + s
             lhs = field[s, (2 - r) * width : (2 - r) * width + n, :]
             part = jnp.dot(lhs, kernel[:, tap * c : (tap + 1) * c], preferred_element_type=F32)
             acc = part if acc is None else acc + part
     return acc
+
+
+def in_hbm(arrays):
+    return [pltpu.with_memory_space_constraint(array, pltpu.HBM) for array in arrays]
 
 
 def prep_kernel(owners, strips):
@@ -73,13 +79,20 @@
 
 
 def weight_copies(ids, weights, kernel, sems):
+    count = len(weights)
+    rows, wide = weights[0].shape
     copies = []
-    for k, weight in enumerate(weights):
-        rows = weight.shape[0]
-        start = pl.multiple_of((ids[0] ^ k) * rows, rows)
-        copies.append(pltpu.make_async_copy(weight, kernel.at[pl.ds(start, rows)], sems.at[k]))
-        copies[-1].start()
-    return copies
+    for r in range(3):
+        cols = pl.ds(r * (wide // 3), wide // 3)
+        for k, weight in enumerate(weights):
+            start = pl.multiple_of((ids[0] ^ k) * rows, rows)
+            copies.append(
+                pltpu.make_async_copy(
+                    weight.at[:, cols], kernel.at[pl.ds(start, rows), cols], sems.at[r * count + k]
+                )
+            )
+            copies[-1].start()
+    return [copies[r * count : (r + 1) * count] for r in range(3)]
 
 
 def gated_kernel(count, width):
@@ -94,10 +107,8 @@
         field[0] = right
         field[1] = same
         field[2] = left
-        for copy in copies:
-            copy.wait()
         n, c = out.shape
-        acc = products(field, kernel, n, c, width)
+        acc = products(field, kernel, copies, n, c, width)
         hf = jnp.concatenate([hup[...], h[...], hdown[...]], axis=0).astype(F32)
         sig = jax.nn.sigmoid(hf)
         acc = acc * (sig * (1.0 + hf * (1.0 - sig)))
@@ -131,11 +142,11 @@
         scratch_shapes=[
             pltpu.VMEM((3, rows + 2 * width, c), BF),
             pltpu.VMEM((weights[0].shape[0] * count, weights[0].shape[1]), BF),
-            pltpu.SemaphoreType.DMA((count,)),
+            pltpu.SemaphoreType.DMA((3 * count,)),
         ],
         compiler_params=PARAMS,
         name="gated",
-    )(ids, gup, g, gdown, hup, h, hdown, *weights)
+    )(ids, gup, g, gdown, hup, h, hdown, *in_hbm(weights))
 
 
 def plain_kernel(count, width):
@@ -148,10 +159,8 @@
         field[0] = right
         field[1] = same
         field[2] = left
-        for copy in copies:
-            copy.wait()
         n, c = out.shape
-        out[...] = products(field, kernel, n, c, width)
+        out[...] = products(field, kernel, copies, n, c, width)
 
     return body
 
@@ -167,11 +176,11 @@
         scratch_shapes=[
             pltpu.VMEM((3, rows, c), BF),
             pltpu.VMEM((weights[0].shape[0] * count, weights[0].shape[1]), BF),
-            pltpu.SemaphoreType.DMA((count,)),
+            pltpu.SemaphoreType.DMA((3 * count,)),
         ],
         compiler_params=PARAMS,
         name="plain",
-    )(ids, ext, *weights)
+    )(ids, ext, *in_hbm(weights))
 
 
 def wgrad_products(lhs, cots, fields, acc, width):
@@ -332,17 +341,18 @@
     h = pre_act.reshape(n, c)
     g = grad_out.reshape(n, c)
 
-    image = lax.all_to_all(prepared(h, g, dp, strips), "space", 0, 0)
-
     w2 = w_second.reshape(owned, 9 * c)
-    w2_shards = [w2] + sent_to_chips(w2)
+    ready = prepared(h, g, dp, strips)
+
     down_pairs = [(i, i + 1) for i in range(strips - 1)]
     up_pairs = [(i + 1, i) for i in range(strips - 1)]
     tail = jnp.concatenate([g[n - 2 * width :], h[n - width :]], axis=0)
     head = jnp.concatenate([g[: 2 * width], h[:width]], axis=0)
     above = lax.ppermute(tail, "space", down_pairs)
     below = lax.ppermute(head, "space", up_pairs)
-    w2_shards, above, below = lax.optimization_barrier((w2_shards, above, below))
+    w2, ready, above, below = lax.optimization_barrier((w2, ready, above, below))
+    image = lax.all_to_all(ready, "space", 0, 0)
+    w2_shards = lax.optimization_barrier([w2] + sent_to_chips(w2))
     shards = sent_to_pair(w2_shards)
     gup, hup = above[: 2 * width], above[2 * width :]
     gdown, hdown = below[: 2 * width], below[2 * width :]
@@ -350,7 +360,8 @@
     xs = [x] + sent_to_chips(after(x, *w2_shards[1:]))
 
     pre_ext, pieces = gated(ids, gup, g, gdown, hup, h, hdown, shards, width, chips)
-    pieces, image, xs = lax.optimization_barrier((pieces, image, xs))
+    pieces, image = lax.optimization_barrier((pieces, image))
+    image = after(image, *xs[1:])
     p_cots = lax.all_to_all(pieces, "dp", 0, 0, axis_index_groups=same_core)
     chip = me >> 1
     cots = [lax.dynamic_index_in_dim(p_cots, chip ^ k, 0, keepdims=False) for k in range(chips)]
@@ -360,8 +371,8 @@
     share = images_summed(own, after(parts, p_cots))
 
     w1 = w_first.reshape(owned, 9 * c)
-    w1_shards = [w1] + sent_to_chips(after(w1, p_cots))
-    w1_shards = sent_to_pair(after(w1_shards, mine))
+    w1_shards = [w1] + sent_to_chips(after(w1, share))
+    w1_shards = sent_to_pair(w1_shards)
     first = strips_gathered(mine)
     second = strips_shared(share)
     in_grad = plain(ids, pre_ext, w1_shards, width)

time: 161 us -> 150 us (0.932)
  starting transfers between devices: 64.7 us -> 51.8 us
  waiting for transfers between devices: 45 us -> 57.2 us
  local copies, waits for them, and re-layouts: 22.5 us -> 12.4 us
    ppermute x24, waiting for transfers between devices: 19.5 us -> 44 us  [swap(): return lax.ppermute(value, axis, xor_pairs(lax.axis_size(axis), k))]
    ppermute x1, waiting for transfers between devices: 22.8 us -> 0.01 us  [per_device(): above = lax.ppermute(tail, 'space', down_pairs)]
    unnamed x42 -> x24, local copies, waits for them, and re-layouts: 15.8 us -> 4.53 us
    ppermute x24, starting transfers between devices: 36.8 us -> 27.2 us  [swap(): return lax.ppermute(value, axis, xor_pairs(lax.axis_size(axis), k))]
    all_to_all x1, waiting for transfers between devices: 0.01 us -> 5.81 us  [images_summed(): got = lax.all_to_all(parts, 'dp', 0, 0)]
    all_to_all x1, waiting for transfers between devices: 0.01 us -> 5.5 us  [per_device(): image = lax.all_to_all(ready, 'space', 0, 0)]
    all_to_all x1, waiting for transfers between devices: 2.63 us -> 0.01 us  [per_device(): p_cots = lax.all_to_all(pieces, 'dp', 0, 0, axis_index_groups=same_core)]
    all_to_all x1, starting transfers between devices: 6.45 us -> 4.05 us  [per_device(): image = lax.all_to_all(ready, 'space', 0, 0)]
  transfers between devices with their start and end apart: 30 -> 30, of which waited for: 6 -> 10; matrix products, arithmetic and copies ran while one was open for 10% -> 9% of each run, Pallas kernels for 6% -> 6%
where the time goes in v5:
time: 150 us; the launch traced here: 149 us
  waiting for transfers between devices  57.2 us (38%)
  starting transfers between devices  51.8 us (35%)
  Pallas kernels  20.5 us (14%)
  local copies, waits for them, and re-layouts  12.4 us (8%)
  other arithmetic  5.85 us (4%)
    ppermute x24, waiting for transfers between devices, swap(): return lax.ppermute(value, axis, xor_pairs(lax.axis_size(axis), k))  44 us
    ppermute x24, starting transfers between devices, swap(): return lax.ppermute(value, axis, xor_pairs(lax.axis_size(axis), k))  27.2 us
    all_to_all x1, starting transfers between devices, strips_shared(): lax.all_to_all(jnp.broadcast_to(mine, (count,) + mine.shape), 'space', 0, 0)  5.93 us
    all_to_all x1, waiting for transfers between devices, images_summed(): got = lax.all_to_all(parts, 'dp', 0, 0)  5.81 us
    pallas_call x1, Pallas kernels, strip_wgrad(): pl.pallas_call(strip_kernel(count, width), out_shape=[half, half], in_spe...  5.66 us
    all_to_all x1, waiting for transfers between devices, per_device(): image = lax.all_to_all(ready, 'space', 0, 0)  5.5 us
    pallas_call x1, Pallas kernels, plain(): pl.pallas_call(plain_kernel(count, width), out_shape=jax.ShapeDtypeStruct...  5.21 us
    pallas_call x1, Pallas kernels, gated(): pl.pallas_call(gated_kernel(count, width), out_shape=[jax.ShapeDtypeStruc...  4.94 us
  transfers between devices with their start and end apart: 30, of which 10 were waited for; matrix products, arithmetic and copies ran while one was open for 9% of the time, Pallas kernels for 6%

profile of v5, /device:TPU:0, one launch (start us, length us, event | category | flops | bytes accessed | tf_op | source)
XLA Modules:
  0.0 148.9 jit_solution(17069043901303385821)
XLA Ops:
  0.6 1.0 fusion.6
  1.7 0.8 slice_bitcast_fusion
  2.5 4.9 %collective-permute-start = (bf16[144,512]{1,0:T(8,128)(2,1)S(1)}, bf16[144,512]{1,0:T(8,128)(2,1)S(1)}, u32[]{:S(2)}, u32[]{:S(2)}) collective-permute-start(bf16[144,512]{1,0:T(8,128)(2,1)S(1)} %pad_maximum_fusion.1), channel_id=1, source_target_pairs={{0,1},{1,2},{2,3},{4,5},{5,6},{6,7},{8,9},{9,10},{10,11},{12,13},{... | collective-permute-start | bytes 442376 | tf_op jit(solution)/shard_map/ppermute | solution.py:351
  7.5 0.0 copy-start.1
  7.5 1.4 collective-permute-start.1
  8.9 0.5 copy.23
  9.5 1.5 %reshape.44.refs_7_ = bf16[64,4608]{1,0:T(8,128)(2,1)} reshape(bf16[64,3,3,512]{3,2,1,0:T(4,128)(2,1)S(1)} %copy.23) | data formatting | bytes 1179648 | tf_op jit(solution)/shard_map/reshape | solution.py:344
  11.0 0.6 prepared.1
  11.6 1.3 copy-done
  12.9 1.9 %collective-permute-done.1 = bf16[144,512]{1,0:T(8,128)(2,1)S(1)} collective-permute-done((bf16[144,512]{1,0:T(8,128)(2,1)S(1)}, bf16[144,512]{1,0:T(8,128)(2,1)S(1)}, u32[]{:S(2)}, u32[]{:S(2)}) %collective-permute-start.1) | collective-permute-done | bytes 147488 | tf_op jit(solution)/shard_map/ppermute | solution.py:352
  14.8 4.0 %all-to-all-start = ((bf16[4,384,640]{2,1,0:T(8,128)(2,1)}), bf16[4,384,640]{2,1,0:T(8,128)(2,1)S(1)}, u32[]{:S(2)}, u32[]{:S(2)}) async-start(bf16[4,384,640]{2,1,0:T(8,128)(2,1)} %copy-done), calls=%async_computation | async-start | bytes 3932160 | tf_op jit(solution)/shard_map/all_to_all | solution.py:354
  18.9 1.5 %collective-permute-start.2 = (bf16[64,4608]{1,0:T(8,128)(2,1)}, bf16[64,4608]{1,0:T(8,128)(2,1)}, u32[]{:S(2)}, u32[]{:S(2)}) collective-permute-start(bf16[64,4608]{1,0:T(8,128)(2,1)} %reshape.44.refs_7_), channel_id=1, source_target_pairs={{0,8},{4,12},{8,0},{12,4},{16,24},{20,28},{24,16},{28,20},{1,9},{5... | collective-permute-start | bytes 1769480 | tf_op jit(solution)/shard_map/ppermute | solution.py:21
  20.4 1.5 %collective-permute-start.3 = (bf16[64,4608]{1,0:T(8,128)(2,1)}, bf16[64,4608]{1,0:T(8,128)(2,1)}, u32[]{:S(2)}, u32[]{:S(2)}) collective-permute-start(bf16[64,4608]{1,0:T(8,128)(2,1)} %reshape.44.refs_7_), channel_id=1, source_target_pairs={{0,16},{4,20},{8,24},{12,28},{16,0},{20,4},{24,8},{28,12},{1,17},{... | collective-permute-start | bytes 1769480 | tf_op jit(solution)/shard_map/ppermute | solution.py:21
  21.9 0.5 collective-permute-start.4
  22.4 13.1 %collective-permute-done.2.refs_9_ = bf16[64,4608]{1,0:T(8,128)(2,1)} collective-permute-done((bf16[64,4608]{1,0:T(8,128)(2,1)}, bf16[64,4608]{1,0:T(8,128)(2,1)}, u32[]{:S(2)}, u32[]{:S(2)}) %collective-permute-start.2) | collective-permute-done | bytes 589856 | tf_op jit(solution)/shard_map/ppermute | solution.py:21
  35.5 11.8 %collective-permute-done.3.refs_11_ = bf16[64,4608]{1,0:T(8,128)(2,1)} collective-permute-done((bf16[64,4608]{1,0:T(8,128)(2,1)}, bf16[64,4608]{1,0:T(8,128)(2,1)}, u32[]{:S(2)}, u32[]{:S(2)}) %collective-permute-start.3) | collective-permute-done | bytes 589856 | tf_op jit(solution)/shard_map/ppermute | solution.py:21
  47.3 0.5 collective-permute-start.7
  47.8 0.5 collective-permute-start.5
  48.3 1.2 collective-permute-start.10
  49.5 0.1 collective-permute-done.6.refs_10_
  49.6 1.5 %collective-permute-start.11 = (bf16[384,512]{1,0:T(8,128)(2,1)}, bf16[384,512]{1,0:T(8,128)(2,1)}, u32[]{:S(2)}, u32[]{:S(2)}) collective-permute-start(bf16[384,512]{1,0:T(8,128)(2,1)} %bitcast.13.refs_1_), channel_id=1, source_target_pairs={{0,16},{4,20},{8,24},{12,28},{16,0},{20,4},{24,8},{28,12},{1,17},{... | collective-permute-start | bytes 1179656 | tf_op jit(solution)/shard_map/ppermute | solution.py:21
  51.1 1.2 collective-permute-start.12
  52.3 0.1 pad_add_fusion.refs_0_.ids
  52.5 4.9 %gated.1 = (bf16[480,512]{1,0:T(8,128)(2,1)S(1)}, bf16[4,480,128]{2,1,0:T(8,128)(2,1)S(1)}) custom-call(s32[3]{0:T(128)S(1)} %pad_add_fusion.refs_0_.ids, bf16[96,512]{1,0:T(8,128)(2,1)S(1)} %slice.44.refs_1_, bf16[384,512]{1,0:T(8,128)(2,1)S(1)} %bitcast.55, bf16[96,512]{1,0:T(8,128)(2,1)S(1)} %slice.45.refs_3_, bf16[48,512]{1,0:T(8,128)(2,1)S(1)} %slice.46.refs_4_, ...), custom_call_target="tpu_custom_call" | custom-call | tf_op jit(solution)/shard_map/gated/pallas_call | solution.py:134
  57.4 0.8 copy-done.3
  58.2 5.5 %all-to-all-done.image = bf16[4,384,640]{2,1,0:T(8,128)(2,1)S(1)} async-done(((bf16[4,384,640]{2,1,0:T(8,128)(2,1)}), bf16[4,384,640]{2,1,0:T(8,128)(2,1)S(1)}, u32[]{:S(2)}, u32[]{:S(2)}) %all-to-all-start) | async-done | bytes 1966112 | tf_op jit(solution)/shard_map/all_to_all | solution.py:354
  63.7 3.7 %all-to-all-start.1 = ((bf16[4,480,128]{2,1,0:T(8,128)(2,1)}), bf16[4,480,128]{2,1,0:T(8,128)(2,1)S(1)}, u32[]{:S(2)}, u32[]{:S(2)}) async-start(bf16[4,480,128]{2,1,0:T(8,128)(2,1)} %copy-done.3), calls=%async_computation.1 | async-start | bytes 983040 | tf_op jit(solution)/shard_map/all_to_all | solution.py:365
  67.4 3.1 %collective-permute-done.11.refs_3_ = bf16[384,512]{1,0:T(8,128)(2,1)} collective-permute-done((bf16[384,512]{1,0:T(8,128)(2,1)}, bf16[384,512]{1,0:T(8,128)(2,1)}, u32[]{:S(2)}, u32[]{:S(2)}) %collective-permute-start.11) | collective-permute-done | bytes 393248 | tf_op jit(solution)/shard_map/ppermute | solution.py:21
  70.6 4.1 %image_wgrad.1 = (f32[9,16,512]{2,1,0:T(8,128)S(1)}, bf16[8,9,16,512]{3,2,1,0:T(8,128)(2,1)}) custom-call(s32[3]{0:T(128)S(1)} %pad_add_fusion.refs_0_.ids, bf16[4,384,640]{2,1,0:T(8,128)(2,1)S(1)} %all-to-all-done.image), custom_call_target="tpu_custom_call" | custom-call | tf_op jit(solution)/shard_map/image_wgrad/pallas_call | solution.py:264
  74.7 5.7 %strip_wgrad.1 = (f32[9,64,512]{2,1,0:T(8,128)S(1)}, f32[9,64,512]{2,1,0:T(8,128)}) custom-call(s32[3]{0:T(128)S(1)} %pad_add_fusion.refs_0_.ids, bf16[384,512]{1,0:T(8,128)(2,1)} %bitcast.13.refs_1_, bf16[384,512]{1,0:T(8,128)(2,1)} %collective-permute-done.10.refs_2_, bf16[384,512]{1,0:T(8,128)(2,1)} %collective-permute-done.11.refs_3_, ...), custom_call_target="tpu_custom_call" | custom-call | tf_op jit(solution)/shard_map/strip_wgrad/pallas_call | solution.py:229
  80.4 4.6 %all-to-all-start.2 = ((bf16[8,9,16,512]{3,2,1,0:T(8,128)(2,1)}), bf16[8,9,16,512]{3,2,1,0:T(8,128)(2,1)}, u32[]{:S(2)}, u32[]{:S(2)}) async-start(bf16[8,9,16,512]{3,2,1,0:T(8,128)(2,1)} %get-tuple-element.45), calls=%async_computation.2 | async-start | bytes 2359296 | tf_op jit(solution)/shard_map/all_to_all | solution.py:304
  85.0 0.5 copy.24
  85.5 1.5 %reshape.47.refs_2_ = bf16[64,4608]{1,0:T(8,128)(2,1)} reshape(bf16[64,3,3,512]{3,2,1,0:T(4,128)(2,1)S(1)} %copy.24) | data formatting | bytes 1179648 | tf_op jit(solution)/shard_map/reshape | solution.py:373
  87.1 1.5 %add.47 = f32[9,64,512]{2,1,0:T(8,128)S(1)} add(f32[9,64,512]{2,1,0:T(8,128)S(1)} %get-tuple-element.51, f32[9,64,512]{2,1,0:T(8,128)} %collective-permute-done.19) | non-fusion elementwise | flops 294912 | bytes 3538944 | tf_op jit(solution)/shard_map/add | solution.py:279
  88.6 1.0 copy-done.4
  89.6 0.8 fusion.4
  90.4 3.5 %collective-permute-start.20 = (bf16[9,16,512]{2,1,0:T(8,128)(2,1)S(1)}, bf16[9,16,512]{2,1,0:T(8,128)(2,1)}, u32[]{:S(2)}, u32[]{:S(2)}) collective-permute-start(bf16[9,16,512]{2,1,0:T(8,128)(2,1)S(1)} %get-tuple-element.53), channel_id=1, source_target_pairs={{0,1},{1,0},{2,3},{3,2},{4,5},{5,4},{6,7},{7,6},{8,9},{9,8},{10,11... | collective-permute-start | bytes 442376 | tf_op jit(solution)/shard_map/ppermute | solution.py:21
  93.9 2.2 %collective-permute-start.21 = (bf16[9,16,512]{2,1,0:T(8,128)(2,1)}, bf16[9,16,512]{2,1,0:T(8,128)(2,1)}, u32[]{:S(2)}, u32[]{:S(2)}) collective-permute-start(bf16[9,16,512]{2,1,0:T(8,128)(2,1)} %get-tuple-element.55), channel_id=1, source_target_pairs={{0,2},{1,3},{2,0},{3,1},{4,6},{5,7},{6,4},{7,5},{8,10},{9,11},{10,... | collective-permute-start | bytes 442376 | tf_op jit(solution)/shard_map/ppermute | solution.py:21
  96.2 0.2 collective-permute-start.22
  96.3 5.8 %all-to-all-done.2 = bf16[8,9,16,512]{3,2,1,0:T(8,128)(2,1)} async-done(((bf16[8,9,16,512]{3,2,1,0:T(8,128)(2,1)}), bf16[8,9,16,512]{3,2,1,0:T(8,128)(2,1)}, u32[]{:S(2)}, u32[]{:S(2)}) %all-to-all-start.2) | async-done | bytes 1179680 | tf_op jit(solution)/shard_map/all_to_all | solution.py:304
  102.1 1.6 %select_reduce_fusion = bf16[9,16,512]{2,1,0:T(8,128)(2,1)S(1)} fusion(bf16[8,9,16,512]{3,2,1,0:T(8,128)(2,1)} %all-to-all-done.2, f32[9,16,512]{2,1,0:T(8,128)S(1)} %get-tuple-element.43, pred[8]{0:T(512)(128)(4,1)S(1)} %iota_compare_fusion), kind=kLoop, calls=%fused_computation | loop fusion | flops 1695744 | bytes 1622024 | tf_op jit(solution)/shard_map/reduce_sum | solution.py:306
  103.7 0.3 collective-permute-start.13
  104.0 1.9 %collective-permute-start.15 = (bf16[64,4608]{1,0:T(8,128)(2,1)S(1)}, bf16[64,4608]{1,0:T(8,128)(2,1)S(1)}, u32[]{:S(2)}, u32[]{:S(2)}) collective-permute-start(bf16[64,4608]{1,0:T(8,128)(2,1)S(1)} %copy-done.5), channel_id=1, source_target_pairs={{0,16},{4,20},{8,24},{12,28},{16,0},{20,4},{24,8},{28,12},{1,17},{... | collective-permute-start | bytes 1769480 | tf_op jit(solution)/shard_map/ppermute | solution.py:21
  105.9 1.4 collective-permute-start.17
  107.3 0.9 broadcast_in_dim.18
  108.2 5.9 %all-to-all-start.3 = ((bf16[4,9,16,512]{3,2,1,0:T(8,128)(2,1)}), bf16[4,9,16,512]{3,2,1,0:T(8,128)(2,1)S(1)}, u32[]{:S(2)}, u32[]{:S(2)}) async-start(bf16[4,9,16,512]{3,2,1,0:T(8,128)(2,1)} %broadcast_in_dim.18), calls=%async_computation.3 | async-start | bytes 1179648 | tf_op jit(solution)/shard_map/all_to_all | solution.py:311
  114.1 1.3 fusion.2
  115.4 2.1 %collective-permute-start.23 = (bf16[9,16,512]{2,1,0:T(8,128)(2,1)S(1)}, bf16[9,16,512]{2,1,0:T(8,128)(2,1)S(1)}, u32[]{:S(2)}, u32[]{:S(2)}) collective-permute-start(bf16[9,16,512]{2,1,0:T(8,128)(2,1)S(1)} %fusion.2), channel_id=1, source_target_pairs={{0,1},{1,0},{2,3},{3,2},{4,5},{5,4},{6,7},{7,6},{8,9},{9,8},{10,11... | collective-permute-start | bytes 442376 | tf_op jit(solution)/shard_map/ppermute | solution.py:21
  117.5 2.4 %collective-permute-start.24 = (bf16[9,16,512]{2,1,0:T(8,128)(2,1)S(1)}, bf16[9,16,512]{2,1,0:T(8,128)(2,1)S(1)}, u32[]{:S(2)}, u32[]{:S(2)}) collective-permute-start(bf16[9,16,512]{2,1,0:T(8,128)(2,1)S(1)} %fusion.2), channel_id=1, source_target_pairs={{0,2},{1,3},{2,0},{3,1},{4,6},{5,7},{6,4},{7,5},{8,10},{9,11},{10,... | collective-permute-start | bytes 442376 | tf_op jit(solution)/shard_map/ppermute | solution.py:21
  119.8 7.8 %collective-permute-done.23 = bf16[9,16,512]{2,1,0:T(8,128)(2,1)S(1)} collective-permute-done((bf16[9,16,512]{2,1,0:T(8,128)(2,1)S(1)}, bf16[9,16,512]{2,1,0:T(8,128)(2,1)S(1)}, u32[]{:S(2)}, u32[]{:S(2)}) %collective-permute-start.23) | collective-permute-done | bytes 147488 | tf_op jit(solution)/shard_map/ppermute | solution.py:21
  127.7 3.9 %collective-permute-start.25 = (bf16[9,16,512]{2,1,0:T(8,128)(2,1)S(1)}, bf16[9,16,512]{2,1,0:T(8,128)(2,1)S(1)}, u32[]{:S(2)}, u32[]{:S(2)}) collective-permute-start(bf16[9,16,512]{2,1,0:T(8,128)(2,1)S(1)} %fusion.2), channel_id=1, source_target_pairs={{0,3},{1,2},{2,1},{3,0},{4,7},{5,6},{6,5},{7,4},{8,11},{9,10},{10,... | collective-permute-start | bytes 442376 | tf_op jit(solution)/shard_map/ppermute | solution.py:21
  131.5 7.3 %collective-permute-done.24 = bf16[9,16,512]{2,1,0:T(8,128)(2,1)S(1)} collective-permute-done((bf16[9,16,512]{2,1,0:T(8,128)(2,1)S(1)}, bf16[9,16,512]{2,1,0:T(8,128)(2,1)S(1)}, u32[]{:S(2)}, u32[]{:S(2)}) %collective-permute-start.24) | collective-permute-done | bytes 147488 | tf_op jit(solution)/shard_map/ppermute | solution.py:21
  138.9 0.5 collective-permute-start.14
  139.4 0.1 collective-permute-start.16
  139.5 0.4 collective-permute-start.18
  139.9 0.1 pad_maximum_fusion
  140.0 0.1 constant_dynamic-slice_fusion.3
  140.1 0.1 copy-done.7
  140.2 0.2 copy-done.8
  140.4 0.1 convert_bitcast_fusion
  140.5 1.2 copy.27
  141.7 1.2 copy_convert_fusion
  142.9 0.7 collective-permute-done.18.refs_9_
  143.5 5.2 %plain.1 = f32[384,512]{1,0:T(8,128)} custom-call(s32[3]{0:T(128)S(1)} %pad_add_fusion.refs_0_.ids, bf16[480,512]{1,0:T(8,128)(2,1)S(1)} %get-tuple-element.35.refs_1_, bf16[64,4608]{1,0:T(8,128)(2,1)} %reshape.47.refs_2_, bf16[64,4608]{1,0:T(8,128)(2,1)} %collective-permute-done.9.refs_3_, bf16[64,4608]{1,0:T(8,128)(2,1)} %copy-done.6, ...), custom_call_target="tpu_custom_call" | custom-call | tf_op jit(solution)/shard_map/plain/pallas_call | solution.py:171
  (48 shorter events, 0.2 us)
Async XLA Ops:
  0.6 8.3 %copy-start.9 = (bf16[64,3,3,512]{3,0,2,1:T(8,128)(2,1)S(1)}, bf16[64,3,3,512]{3,0,2,1:T(8,128)(2,1)}, u32[]{:S(2)}) copy-start(bf16[64,3,3,512]{3,0,2,1:T(8,128)(2,1)} %param.9) | copy-start | bytes 1769476
  2.5 10.4 %collective-permute-start = (bf16[144,512]{1,0:T(8,128)(2,1)S(1)}, bf16[144,512]{1,0:T(8,128)(2,1)S(1)}, u32[]{:S(2)}, u32[]{:S(2)}) collective-permute-start(bf16[144,512]{1,0:T(8,128)(2,1)S(1)} %pad_maximum_fusion.1), channel_id=1, source_target_pairs={{0,1},{1,2},{2,3},{4,5},{5,6},{6,7},{8,9},{9,10},{10,11},{12,13},{... | collective-permute-start | bytes 442376 | tf_op jit(solution)/shard_map/ppermute | solution.py:351
  7.5 3.5 %copy-start.1 = (bf16[1,8,48,512]{3,2,1,0:T(8,128)(2,1)S(1)}, bf16[1,8,48,512]{3,2,1,0:T(8,128)(2,1)}, u32[]{:S(2)}) copy-start(bf16[1,8,48,512]{3,2,1,0:T(8,128)(2,1)} %param.7) | copy-start | bytes 1179652
  7.5 3.5 %copy-start.2 = (bf16[1,8,48,512]{3,2,1,0:T(8,128)(2,1)S(1)}, bf16[1,8,48,512]{3,2,1,0:T(8,128)(2,1)}, u32[]{:S(2)}) copy-start(bf16[1,8,48,512]{3,2,1,0:T(8,128)(2,1)} %param.6) | copy-start | bytes 1179652
  7.5 7.3 %collective-permute-start.1 = (bf16[144,512]{1,0:T(8,128)(2,1)S(1)}, bf16[144,512]{1,0:T(8,128)(2,1)S(1)}, u32[]{:S(2)}, u32[]{:S(2)}) collective-permute-start(bf16[144,512]{1,0:T(8,128)(2,1)S(1)} %pad_maximum_fusion.2), channel_id=1, source_target_pairs={{1,0},{2,1},{3,2},{5,4},{6,5},{7,6},{9,8},{10,9},{11,10},{13,12},{... | collective-permute-start | bytes 442376 | tf_op jit(solution)/shard_map/ppermute | solution.py:352
  11.6 1.3 copy-start
  14.8 48.9 %all-to-all-start = ((bf16[4,384,640]{2,1,0:T(8,128)(2,1)}), bf16[4,384,640]{2,1,0:T(8,128)(2,1)S(1)}, u32[]{:S(2)}, u32[]{:S(2)}) async-start(bf16[4,384,640]{2,1,0:T(8,128)(2,1)} %copy-done), calls=%async_computation | async-start | bytes 3932160 | tf_op jit(solution)/shard_map/all_to_all | solution.py:354
  18.9 16.6 %collective-permute-start.2 = (bf16[64,4608]{1,0:T(8,128)(2,1)}, bf16[64,4608]{1,0:T(8,128)(2,1)}, u32[]{:S(2)}, u32[]{:S(2)}) collective-permute-start(bf16[64,4608]{1,0:T(8,128)(2,1)} %reshape.44.refs_7_), channel_id=1, source_target_pairs={{0,8},{4,12},{8,0},{12,4},{16,24},{20,28},{24,16},{28,20},{1,9},{5... | collective-permute-start | bytes 1769480 | tf_op jit(solution)/shard_map/ppermute | solution.py:21
  20.4 26.9 %collective-permute-start.3 = (bf16[64,4608]{1,0:T(8,128)(2,1)}, bf16[64,4608]{1,0:T(8,128)(2,1)}, u32[]{:S(2)}, u32[]{:S(2)}) collective-permute-start(bf16[64,4608]{1,0:T(8,128)(2,1)} %reshape.44.refs_7_), channel_id=1, source_target_pairs={{0,16},{4,20},{8,24},{12,28},{16,0},{20,4},{24,8},{28,12},{1,17},{... | collective-permute-start | bytes 1769480 | tf_op jit(solution)/shard_map/ppermute | solution.py:21
  21.9 25.4 %collective-permute-start.4 = (bf16[64,4608]{1,0:T(8,128)(2,1)}, bf16[64,4608]{1,0:T(8,128)(2,1)}, u32[]{:S(2)}, u32[]{:S(2)}) collective-permute-start(bf16[64,4608]{1,0:T(8,128)(2,1)} %reshape.44.refs_7_), channel_id=1, source_target_pairs={{0,24},{4,28},{8,16},{12,20},{16,8},{20,12},{24,0},{28,4},{1,25},{... | collective-permute-start | bytes 1769480 | tf_op jit(solution)/shard_map/ppermute | solution.py:21
  47.3 2.3 %collective-permute-start.6 = (bf16[64,4608]{1,0:T(8,128)(2,1)}, bf16[64,4608]{1,0:T(8,128)(2,1)}, u32[]{:S(2)}, u32[]{:S(2)}) collective-permute-start(bf16[64,4608]{1,0:T(8,128)(2,1)} %collective-permute-done.2.refs_9_), channel_id=1, source_target_pairs={{0,4},{4,0},{8,12},{12,8},{16,20},{20,16},{24,28},{28,24},{1,5},{5... | collective-permute-start | bytes 1769480 | tf_op jit(solution)/shard_map/ppermute | solution.py:21
  47.3 3.9 %collective-permute-start.7 = (bf16[64,4608]{1,0:T(8,128)(2,1)}, bf16[64,4608]{1,0:T(8,128)(2,1)}, u32[]{:S(2)}, u32[]{:S(2)}) collective-permute-start(bf16[64,4608]{1,0:T(8,128)(2,1)} %collective-permute-done.3.refs_11_), channel_id=1, source_target_pairs={{0,4},{4,0},{8,12},{12,8},{16,20},{20,16},{24,28},{28,24},{1,5},{5... | collective-permute-start | bytes 1769480 | tf_op jit(solution)/shard_map/ppermute | solution.py:21
  47.8 4.7 %collective-permute-start.8 = (bf16[64,4608]{1,0:T(8,128)(2,1)}, bf16[64,4608]{1,0:T(8,128)(2,1)}, u32[]{:S(2)}, u32[]{:S(2)}) collective-permute-start(bf16[64,4608]{1,0:T(8,128)(2,1)} %collective-permute-done.4.refs_13_), channel_id=1, source_target_pairs={{0,4},{4,0},{8,12},{12,8},{16,20},{20,16},{24,28},{28,24},{1,5},{5... | collective-permute-start | bytes 1769480 | tf_op jit(solution)/shard_map/ppermute | solution.py:21
  47.8 4.7 %collective-permute-start.5 = (bf16[64,4608]{1,0:T(8,128)(2,1)}, bf16[64,4608]{1,0:T(8,128)(2,1)}, u32[]{:S(2)}, u32[]{:S(2)}) collective-permute-start(bf16[64,4608]{1,0:T(8,128)(2,1)} %reshape.44.refs_7_), channel_id=1, source_target_pairs={{0,4},{4,0},{8,12},{12,8},{16,20},{20,16},{24,28},{28,24},{1,5},{5... | collective-permute-start | bytes 1769480 | tf_op jit(solution)/shard_map/ppermute | solution.py:21
  48.3 19.1 %collective-permute-start.10 = (bf16[384,512]{1,0:T(8,128)(2,1)}, bf16[384,512]{1,0:T(8,128)(2,1)}, u32[]{:S(2)}, u32[]{:S(2)}) collective-permute-start(bf16[384,512]{1,0:T(8,128)(2,1)} %bitcast.13.refs_1_), channel_id=1, source_target_pairs={{0,8},{4,12},{8,0},{12,4},{16,24},{20,28},{24,16},{28,20},{1,9},{5... | collective-permute-start | bytes 1179656 | tf_op jit(solution)/shard_map/ppermute | solution.py:21
  49.6 20.9 %collective-permute-start.11 = (bf16[384,512]{1,0:T(8,128)(2,1)}, bf16[384,512]{1,0:T(8,128)(2,1)}, u32[]{:S(2)}, u32[]{:S(2)}) collective-permute-start(bf16[384,512]{1,0:T(8,128)(2,1)} %bitcast.13.refs_1_), channel_id=1, source_target_pairs={{0,16},{4,20},{8,24},{12,28},{16,0},{20,4},{24,8},{28,12},{1,17},{... | collective-permute-start | bytes 1179656 | tf_op jit(solution)/shard_map/ppermute | solution.py:21
  51.1 19.4 %collective-permute-start.12 = (bf16[384,512]{1,0:T(8,128)(2,1)}, bf16[384,512]{1,0:T(8,128)(2,1)}, u32[]{:S(2)}, u32[]{:S(2)}) collective-permute-start(bf16[384,512]{1,0:T(8,128)(2,1)} %bitcast.13.refs_1_), channel_id=1, source_target_pairs={{0,24},{4,28},{8,16},{12,20},{16,8},{20,12},{24,0},{28,4},{1,25},{... | collective-permute-start | bytes 1179656 | tf_op jit(solution)/shard_map/ppermute | solution.py:21
  57.4 0.8 copy-start.3
  63.7 11.0 %all-to-all-start.1 = ((bf16[4,480,128]{2,1,0:T(8,128)(2,1)}), bf16[4,480,128]{2,1,0:T(8,128)(2,1)S(1)}, u32[]{:S(2)}, u32[]{:S(2)}) async-start(bf16[4,480,128]{2,1,0:T(8,128)(2,1)} %copy-done.3), calls=%async_computation.1 | async-start | bytes 983040 | tf_op jit(solution)/shard_map/all_to_all | solution.py:365
  80.4 6.7 %collective-permute-start.19 = (f32[9,64,512]{2,1,0:T(8,128)}, f32[9,64,512]{2,1,0:T(8,128)}, u32[]{:S(2)}, u32[]{:S(2)}) collective-permute-start(f32[9,64,512]{2,1,0:T(8,128)} %get-tuple-element.52), channel_id=1, source_target_pairs={{0,4},{4,0},{8,12},{12,8},{16,20},{20,16},{24,28},{28,24},{1,5},{5... | collective-permute-start | bytes 3538952 | tf_op jit(solution)/shard_map/ppermute | solution.py:21
  80.4 4.6 %copy-start.10 = (bf16[64,3,3,512]{3,0,2,1:T(8,128)(2,1)S(1)}, bf16[64,3,3,512]{3,0,2,1:T(8,128)(2,1)}, u32[]{:S(2)}) copy-start(bf16[64,3,3,512]{3,0,2,1:T(8,128)(2,1)} %param.8) | copy-start | bytes 1769476
  80.4 21.7 %all-to-all-start.2 = ((bf16[8,9,16,512]{3,2,1,0:T(8,128)(2,1)}), bf16[8,9,16,512]{3,2,1,0:T(8,128)(2,1)}, u32[]{:S(2)}, u32[]{:S(2)}) async-start(bf16[8,9,16,512]{3,2,1,0:T(8,128)(2,1)} %get-tuple-element.45), calls=%async_computation.2 | async-start | bytes 2359296 | tf_op jit(solution)/shard_map/all_to_all | solution.py:304
  88.6 1.0 copy-start.4
  89.6 14.1 %copy-start.5 = (bf16[64,4608]{1,0:T(8,128)(2,1)S(1)}, bf16[64,4608]{1,0:T(8,128)(2,1)}, u32[]{:S(2)}) copy-start(bf16[64,4608]{1,0:T(8,128)(2,1)} %reshape.47.refs_2_) | copy-start | bytes 1769476
  90.4 15.5 %collective-permute-start.20 = (bf16[9,16,512]{2,1,0:T(8,128)(2,1)S(1)}, bf16[9,16,512]{2,1,0:T(8,128)(2,1)}, u32[]{:S(2)}, u32[]{:S(2)}) collective-permute-start(bf16[9,16,512]{2,1,0:T(8,128)(2,1)S(1)} %get-tuple-element.53), channel_id=1, source_target_pairs={{0,1},{1,0},{2,3},{3,2},{4,5},{5,4},{6,7},{7,6},{8,9},{9,8},{10,11... | collective-permute-start | bytes 442376 | tf_op jit(solution)/shard_map/ppermute | solution.py:21
  93.9 20.2 %collective-permute-start.21 = (bf16[9,16,512]{2,1,0:T(8,128)(2,1)}, bf16[9,16,512]{2,1,0:T(8,128)(2,1)}, u32[]{:S(2)}, u32[]{:S(2)}) collective-permute-start(bf16[9,16,512]{2,1,0:T(8,128)(2,1)} %get-tuple-element.55), channel_id=1, source_target_pairs={{0,2},{1,3},{2,0},{3,1},{4,6},{5,7},{6,4},{7,5},{8,10},{9,11},{10,... | collective-permute-start | bytes 442376 | tf_op jit(solution)/shard_map/ppermute | solution.py:21
  96.2 17.9 %collective-permute-start.22 = (bf16[9,16,512]{2,1,0:T(8,128)(2,1)}, bf16[9,16,512]{2,1,0:T(8,128)(2,1)}, u32[]{:S(2)}, u32[]{:S(2)}) collective-permute-start(bf16[9,16,512]{2,1,0:T(8,128)(2,1)} %get-tuple-element.54), channel_id=1, source_target_pairs={{0,3},{1,2},{2,1},{3,0},{4,7},{5,6},{6,5},{7,4},{8,11},{9,10},{10,... | collective-permute-start | bytes 442376 | tf_op jit(solution)/shard_map/ppermute | solution.py:21
  103.7 35.1 %collective-permute-start.13 = (bf16[64,4608]{1,0:T(8,128)(2,1)S(1)}, bf16[64,4608]{1,0:T(8,128)(2,1)S(1)}, u32[]{:S(2)}, u32[]{:S(2)}) collective-permute-start(bf16[64,4608]{1,0:T(8,128)(2,1)S(1)} %copy-done.5), channel_id=1, source_target_pairs={{0,8},{4,12},{8,0},{12,4},{16,24},{20,28},{24,16},{28,20},{1,9},{5... | collective-permute-start | bytes 1769480 | tf_op jit(solution)/shard_map/ppermute | solution.py:21
  104.0 35.4 %collective-permute-start.15 = (bf16[64,4608]{1,0:T(8,128)(2,1)S(1)}, bf16[64,4608]{1,0:T(8,128)(2,1)S(1)}, u32[]{:S(2)}, u32[]{:S(2)}) collective-permute-start(bf16[64,4608]{1,0:T(8,128)(2,1)S(1)} %copy-done.5), channel_id=1, source_target_pairs={{0,16},{4,20},{8,24},{12,28},{16,0},{20,4},{24,8},{28,12},{1,17},{... | collective-permute-start | bytes 1769480 | tf_op jit(solution)/shard_map/ppermute | solution.py:21
  105.9 33.6 %collective-permute-start.17 = (bf16[64,4608]{1,0:T(8,128)(2,1)S(1)}, bf16[64,4608]{1,0:T(8,128)(2,1)S(1)}, u32[]{:S(2)}, u32[]{:S(2)}) collective-permute-start(bf16[64,4608]{1,0:T(8,128)(2,1)S(1)} %copy-done.5), channel_id=1, source_target_pairs={{0,24},{4,28},{8,16},{12,20},{16,8},{20,12},{24,0},{28,4},{1,25},{... | collective-permute-start | bytes 1769480 | tf_op jit(solution)/shard_map/ppermute | solution.py:21
  108.2 33.5 %all-to-all-start.3 = ((bf16[4,9,16,512]{3,2,1,0:T(8,128)(2,1)}), bf16[4,9,16,512]{3,2,1,0:T(8,128)(2,1)S(1)}, u32[]{:S(2)}, u32[]{:S(2)}) async-start(bf16[4,9,16,512]{3,2,1,0:T(8,128)(2,1)} %broadcast_in_dim.18), calls=%async_computation.3 | async-start | bytes 1179648 | tf_op jit(solution)/shard_map/all_to_all | solution.py:311
  115.4 12.3 %collective-permute-start.23 = (bf16[9,16,512]{2,1,0:T(8,128)(2,1)S(1)}, bf16[9,16,512]{2,1,0:T(8,128)(2,1)S(1)}, u32[]{:S(2)}, u32[]{:S(2)}) collective-permute-start(bf16[9,16,512]{2,1,0:T(8,128)(2,1)S(1)} %fusion.2), channel_id=1, source_target_pairs={{0,1},{1,0},{2,3},{3,2},{4,5},{5,4},{6,7},{7,6},{8,9},{9,8},{10,11... | collective-permute-start | bytes 442376 | tf_op jit(solution)/shard_map/ppermute | solution.py:21
  117.5 21.4 %collective-permute-start.24 = (bf16[9,16,512]{2,1,0:T(8,128)(2,1)S(1)}, bf16[9,16,512]{2,1,0:T(8,128)(2,1)S(1)}, u32[]{:S(2)}, u32[]{:S(2)}) collective-permute-start(bf16[9,16,512]{2,1,0:T(8,128)(2,1)S(1)} %fusion.2), channel_id=1, source_target_pairs={{0,2},{1,3},{2,0},{3,1},{4,6},{5,7},{6,4},{7,5},{8,10},{9,11},{10,... | collective-permute-start | bytes 442376 | tf_op jit(solution)/shard_map/ppermute | solution.py:21
  127.7 12.3 %collective-permute-start.25 = (bf16[9,16,512]{2,1,0:T(8,128)(2,1)S(1)}, bf16[9,16,512]{2,1,0:T(8,128)(2,1)S(1)}, u32[]{:S(2)}, u32[]{:S(2)}) collective-permute-start(bf16[9,16,512]{2,1,0:T(8,128)(2,1)S(1)} %fusion.2), channel_id=1, source_target_pairs={{0,3},{1,2},{2,1},{3,0},{4,7},{5,6},{6,5},{7,4},{8,11},{9,10},{10,... | collective-permute-start | bytes 442376 | tf_op jit(solution)/shard_map/ppermute | solution.py:21
  138.9 4.0 %collective-permute-start.9 = (bf16[64,4608]{1,0:T(8,128)(2,1)S(1)}, bf16[64,4608]{1,0:T(8,128)(2,1)}, u32[]{:S(2)}, u32[]{:S(2)}) collective-permute-start(bf16[64,4608]{1,0:T(8,128)(2,1)S(1)} %copy-done.5), channel_id=1, source_target_pairs={{0,4},{4,0},{8,12},{12,8},{16,20},{20,16},{24,28},{28,24},{1,5},{5... | collective-permute-start | bytes 1769480 | tf_op jit(solution)/shard_map/ppermute | solution.py:21
  138.9 1.2 copy-start.6
  138.9 4.0 %collective-permute-start.14 = (bf16[64,4608]{1,0:T(8,128)(2,1)S(1)}, bf16[64,4608]{1,0:T(8,128)(2,1)}, u32[]{:S(2)}, u32[]{:S(2)}) collective-permute-start(bf16[64,4608]{1,0:T(8,128)(2,1)S(1)} %collective-permute-done.13.refs_4_), channel_id=1, source_target_pairs={{0,4},{4,0},{8,12},{12,8},{16,20},{20,16},{24,28},{28,24},{1,5},{5... | collective-permute-start | bytes 1769480 | tf_op jit(solution)/shard_map/ppermute | solution.py:21
  139.4 0.8 copy-start.7
  139.4 3.5 %collective-permute-start.16 = (bf16[64,4608]{1,0:T(8,128)(2,1)S(1)}, bf16[64,4608]{1,0:T(8,128)(2,1)}, u32[]{:S(2)}, u32[]{:S(2)}) collective-permute-start(bf16[64,4608]{1,0:T(8,128)(2,1)S(1)} %collective-permute-done.15.refs_6_), channel_id=1, source_target_pairs={{0,4},{4,0},{8,12},{12,8},{16,20},{20,16},{24,28},{28,24},{1,5},{5... | collective-permute-start | bytes 1769480 | tf_op jit(solution)/shard_map/ppermute | solution.py:21
  139.5 1.0 copy-start.8
  139.5 4.1 %collective-permute-start.18 = (bf16[64,4608]{1,0:T(8,128)(2,1)S(1)}, bf16[64,4608]{1,0:T(8,128)(2,1)}, u32[]{:S(2)}, u32[]{:S(2)}) collective-permute-start(bf16[64,4608]{1,0:T(8,128)(2,1)S(1)} %collective-permute-done.17.refs_8_), channel_id=1, source_target_pairs={{0,4},{4,0},{8,12},{12,8},{16,20},{20,16},{24,28},{28,24},{1,5},{5... | collective-permute-start | bytes 1769480 | tf_op jit(solution)/shard_map/ppermute | solution.py:21

commit v6 on v5

--- a/solution.py
+++ b/solution.py
@@ -210,9 +210,9 @@
     def body(*refs):
         ids = refs[0]
         fields = refs[1 : 1 + count]
-        cots = refs[1 + count : 1 + 2 * count]
-        keep, send, lhs, acc = refs[1 + 2 * count :]
-        wgrad_products(lhs, [cot[...] for cot in cots], fields, acc, width)
+        cots, keep, send, lhs, acc = refs[1 + count :]
+        ordered = [cots[(ids[0] >> 1) ^ i] for i in range(count)]
+        wgrad_products(lhs, ordered, fields, acc, width)
         half = keep.shape[1]
         mine = ids[0] & 1
         keep[...] = acc[:, pl.ds(pl.multiple_of(mine * half, half), half), :]
@@ -224,17 +224,17 @@
 def strip_wgrad(ids, fields, cots, width):
     count = len(fields)
     n, c = fields[0].shape
-    w = cots[0].shape[1]
+    w = cots.shape[2]
     half = jax.ShapeDtypeStruct((9, w // 2, c), F32)
     return pl.pallas_call(
         strip_kernel(count, width),
         out_shape=[half, half],
-        in_specs=[SM] + [VM] * (2 * count),
+        in_specs=[SM] + [VM] * (count + 1),
         out_specs=[VM, VM],
         scratch_shapes=[pltpu.VMEM((9 * w, count * n), BF), pltpu.VMEM((9, w, c), F32)],
         compiler_params=PARAMS,
         name="strip_wgrad",
-    )(ids, *fields, *cots)
+    )(ids, *fields, cots)
 
 
 def image_kernel(width):
@@ -363,11 +363,9 @@
     pieces, image = lax.optimization_barrier((pieces, image))
     image = after(image, *xs[1:])
     p_cots = lax.all_to_all(pieces, "dp", 0, 0, axis_index_groups=same_core)
-    chip = me >> 1
-    cots = [lax.dynamic_index_in_dim(p_cots, chip ^ k, 0, keepdims=False) for k in range(chips)]
     own, parts = image_wgrad(ids, image, c, dp, width)
-    cots, own = lax.optimization_barrier((cots, own))
-    mine = strips_summed(*strip_wgrad(ids, xs, cots, width))
+    p_cots, own = lax.optimization_barrier((p_cots, own))
+    mine = strips_summed(*strip_wgrad(ids, xs, p_cots, width))
     share = images_summed(own, after(parts, p_cots))
 
     w1 = w_first.reshape(owned, 9 * c)

time: 150 us -> 148 us (0.987)
  local copies, waits for them, and re-layouts: 12.4 us -> 15.4 us
  Pallas kernels: 20.5 us -> 18.3 us
    all_to_all x1, waiting for transfers between devices: 5.5 us -> 2.76 us  [per_device(): image = lax.all_to_all(ready, 'space', 0, 0)]
    unnamed x24 -> x28, local copies, waits for them, and re-layouts: 4.53 us -> 6.69 us
    slice x2, local copies, waits for them, and re-layouts: 0.01 us -> 1.7 us  [per_device(): gdown, hdown = (below[:2 * width], below[2 * width:])]
  transfers between devices with their start and end apart: 30 -> 30, of which waited for: 10 -> 12; matrix products, arithmetic and copies ran while one was open for 9% -> 9% of each run, Pallas kernels for 6% -> 6%
where the time goes in v6:
time: 148 us; the launch traced here: 147 us
  waiting for transfers between devices  56 us (38%)
  starting transfers between devices  51.9 us (35%)
  Pallas kernels  18.3 us (12%)
  local copies, waits for them, and re-layouts  15.4 us (10%)
  other arithmetic  4.62 us (3%)
    ppermute x24, waiting for transfers between devices, swap(): return lax.ppermute(value, axis, xor_pairs(lax.axis_size(axis), k))  45.2 us
    ppermute x24, starting transfers between devices, swap(): return lax.ppermute(value, axis, xor_pairs(lax.axis_size(axis), k))  27.5 us
    unnamed x28, local copies, waits for them, and re-layouts  6.69 us
    all_to_all x1, starting transfers between devices, strips_shared(): lax.all_to_all(jnp.broadcast_to(mine, (count,) + mine.shape), 'space', 0, 0)  5.99 us
    all_to_all x1, waiting for transfers between devices, images_summed(): got = lax.all_to_all(parts, 'dp', 0, 0)  5.48 us
    pallas_call x1, Pallas kernels, plain(): pl.pallas_call(plain_kernel(count, width), out_shape=jax.ShapeDtypeStruct...  5.22 us
    ppermute x1, starting transfers between devices, per_device(): above = lax.ppermute(tail, 'space', down_pairs)  4.94 us
    pallas_call x1, Pallas kernels, gated(): pl.pallas_call(gated_kernel(count, width), out_shape=[jax.ShapeDtypeStruc...  4.93 us
  transfers between devices with their start and end apart: 30, of which 12 were waited for; matrix products, arithmetic and copies ran while one was open for 9% of the time, Pallas kernels for 6%

profile of v6, /device:TPU:0, one launch (start us, length us, event | category | flops | bytes accessed | tf_op | source)
XLA Modules:
  0.0 147.4 jit_solution(15904449291277159320)
XLA Ops:
  0.6 1.0 fusion.6
  1.7 0.8 slice_bitcast_fusion
  2.5 4.9 %collective-permute-start = (bf16[144,512]{1,0:T(8,128)(2,1)S(1)}, bf16[144,512]{1,0:T(8,128)(2,1)S(1)}, u32[]{:S(2)}, u32[]{:S(2)}) collective-permute-start(bf16[144,512]{1,0:T(8,128)(2,1)S(1)} %pad_maximum_fusion.1), channel_id=1, source_target_pairs={{0,1},{1,2},{2,3},{4,5},{5,6},{6,7},{8,9},{9,10},{10,11},{12,13},{... | collective-permute-start | bytes 442376 | tf_op jit(solution)/shard_map/ppermute | solution.py:351
  7.5 1.4 collective-permute-start.1
  8.9 0.5 copy.23
  9.5 0.8 reshape.44.refs_7_
  10.3 0.6 prepared.1
  10.9 1.3 copy-done
  12.3 2.6 %collective-permute-done.1 = bf16[144,512]{1,0:T(8,128)(2,1)S(1)} collective-permute-done((bf16[144,512]{1,0:T(8,128)(2,1)S(1)}, bf16[144,512]{1,0:T(8,128)(2,1)S(1)}, u32[]{:S(2)}, u32[]{:S(2)}) %collective-permute-start.1) | collective-permute-done | bytes 147488 | tf_op jit(solution)/shard_map/ppermute | solution.py:352
  14.8 0.7 copy-done.12
  15.5 3.9 %all-to-all-start = ((bf16[4,384,640]{2,1,0:T(8,128)(2,1)}), bf16[4,384,640]{2,1,0:T(8,128)(2,1)S(1)}, u32[]{:S(2)}, u32[]{:S(2)}) async-start(bf16[4,384,640]{2,1,0:T(8,128)(2,1)} %copy-done), calls=%async_computation | async-start | bytes 3932160 | tf_op jit(solution)/shard_map/all_to_all | solution.py:354
  19.3 1.5 %collective-permute-start.2 = (bf16[64,4608]{1,0:T(8,128)(2,1)S(1)}, bf16[64,4608]{1,0:T(8,128)(2,1)}, u32[]{:S(2)}, u32[]{:S(2)}) collective-permute-start(bf16[64,4608]{1,0:T(8,128)(2,1)S(1)} %reshape.44.refs_7_), channel_id=1, source_target_pairs={{0,8},{4,12},{8,0},{12,4},{16,24},{20,28},{24,16},{28,20},{1,9},{5... | collective-permute-start | bytes 1769480 | tf_op jit(solution)/shard_map/ppermute | solution.py:21
  20.8 1.5 %collective-permute-start.3 = (bf16[64,4608]{1,0:T(8,128)(2,1)S(1)}, bf16[64,4608]{1,0:T(8,128)(2,1)}, u32[]{:S(2)}, u32[]{:S(2)}) collective-permute-start(bf16[64,4608]{1,0:T(8,128)(2,1)S(1)} %reshape.44.refs_7_), channel_id=1, source_target_pairs={{0,16},{4,20},{8,24},{12,28},{16,0},{20,4},{24,8},{28,12},{1,17},{... | collective-permute-start | bytes 1769480 | tf_op jit(solution)/shard_map/ppermute | solution.py:21
  22.4 0.5 collective-permute-start.4
  22.8 12.9 %collective-permute-done.2.refs_9_ = bf16[64,4608]{1,0:T(8,128)(2,1)} collective-permute-done((bf16[64,4608]{1,0:T(8,128)(2,1)S(1)}, bf16[64,4608]{1,0:T(8,128)(2,1)}, u32[]{:S(2)}, u32[]{:S(2)}) %collective-permute-start.2) | collective-permute-done | bytes 589856 | tf_op jit(solution)/shard_map/ppermute | solution.py:21
  35.7 11.3 %collective-permute-done.3.refs_11_ = bf16[64,4608]{1,0:T(8,128)(2,1)} collective-permute-done((bf16[64,4608]{1,0:T(8,128)(2,1)S(1)}, bf16[64,4608]{1,0:T(8,128)(2,1)}, u32[]{:S(2)}, u32[]{:S(2)}) %collective-permute-start.3) | collective-permute-done | bytes 589856 | tf_op jit(solution)/shard_map/ppermute | solution.py:21
  47.1 0.5 collective-permute-start.7
  47.6 0.5 collective-permute-start.5
  48.1 1.2 collective-permute-start.10
  49.3 0.1 collective-permute-done.6.refs_10_
  49.4 1.5 %collective-permute-start.11 = (bf16[384,512]{1,0:T(8,128)(2,1)}, bf16[384,512]{1,0:T(8,128)(2,1)}, u32[]{:S(2)}, u32[]{:S(2)}) collective-permute-start(bf16[384,512]{1,0:T(8,128)(2,1)} %bitcast.9.refs_1_), channel_id=1, source_target_pairs={{0,16},{4,20},{8,24},{12,28},{16,0},{20,4},{24,8},{28,12},{1,17},{... | collective-permute-start | bytes 1179656 | tf_op jit(solution)/shard_map/ppermute | solution.py:21
  50.9 0.2 collective-permute-done.7.refs_12_
  51.1 1.5 %collective-permute-start.12 = (bf16[384,512]{1,0:T(8,128)(2,1)}, bf16[384,512]{1,0:T(8,128)(2,1)}, u32[]{:S(2)}, u32[]{:S(2)}) collective-permute-start(bf16[384,512]{1,0:T(8,128)(2,1)} %bitcast.9.refs_1_), channel_id=1, source_target_pairs={{0,24},{4,28},{8,16},{12,20},{16,8},{20,12},{24,0},{28,4},{1,25},{... | collective-permute-start | bytes 1179656 | tf_op jit(solution)/shard_map/ppermute | solution.py:21
  52.7 0.9 slice.45.refs_3_
  53.6 0.8 slice.47.refs_6_
  54.4 4.9 %gated.1 = (bf16[480,512]{1,0:T(8,128)(2,1)S(1)}, bf16[4,480,128]{2,1,0:T(8,128)(2,1)S(1)}) custom-call(s32[3]{0:T(128)S(1)} %pad_add_fusion.refs_0_.ids, bf16[96,512]{1,0:T(8,128)(2,1)S(1)} %slice.44.refs_1_, bf16[384,512]{1,0:T(8,128)(2,1)S(1)} %bitcast.47, bf16[96,512]{1,0:T(8,128)(2,1)S(1)} %slice.45.refs_3_, bf16[48,512]{1,0:T(8,128)(2,1)S(1)} %slice.46.refs_4_, ...), custom_call_target="tpu_custom_call" | custom-call | tf_op jit(solution)/shard_map/gated/pallas_call | solution.py:134
  59.3 0.8 copy-done.4
  60.1 0.8 copy-done.6
  60.9 2.8 %all-to-all-done.image = bf16[4,384,640]{2,1,0:T(8,128)(2,1)S(1)} async-done(((bf16[4,384,640]{2,1,0:T(8,128)(2,1)}), bf16[4,384,640]{2,1,0:T(8,128)(2,1)S(1)}, u32[]{:S(2)}, u32[]{:S(2)}) %all-to-all-start) | async-done | bytes 1966112 | tf_op jit(solution)/shard_map/all_to_all | solution.py:354
  63.7 3.7 %all-to-all-start.1 = ((bf16[4,480,128]{2,1,0:T(8,128)(2,1)}), bf16[4,480,128]{2,1,0:T(8,128)(2,1)S(1)}, u32[]{:S(2)}, u32[]{:S(2)}) async-start(bf16[4,480,128]{2,1,0:T(8,128)(2,1)} %copy-done.6), calls=%async_computation.1 | async-start | bytes 983040 | tf_op jit(solution)/shard_map/all_to_all | solution.py:365
  67.4 3.1 %collective-permute-done.11.refs_3_ = bf16[384,512]{1,0:T(8,128)(2,1)} collective-permute-done((bf16[384,512]{1,0:T(8,128)(2,1)}, bf16[384,512]{1,0:T(8,128)(2,1)}, u32[]{:S(2)}, u32[]{:S(2)}) %collective-permute-start.11) | collective-permute-done | bytes 393248 | tf_op jit(solution)/shard_map/ppermute | solution.py:21
  70.5 3.0 %image_wgrad.1 = (f32[9,16,512]{2,1,0:T(8,128)S(1)}, bf16[8,9,16,512]{3,2,1,0:T(8,128)(2,1)S(1)}) custom-call(s32[3]{0:T(128)S(1)} %pad_add_fusion.refs_0_.ids, bf16[4,384,640]{2,1,0:T(8,128)(2,1)S(1)} %all-to-all-done.image), custom_call_target="tpu_custom_call" | custom-call | tf_op jit(solution)/shard_map/image_wgrad/pallas_call | solution.py:264
  73.6 1.0 copy-done.3
  74.6 4.5 %strip_wgrad.1 = (f32[9,64,512]{2,1,0:T(8,128)S(1)}, f32[9,64,512]{2,1,0:T(8,128)S(1)}) custom-call(s32[3]{0:T(128)S(1)} %pad_add_fusion.refs_0_.ids, bf16[384,512]{1,0:T(8,128)(2,1)} %bitcast.9.refs_1_, bf16[384,512]{1,0:T(8,128)(2,1)} %collective-permute-done.10.refs_2_, bf16[384,512]{1,0:T(8,128)(2,1)} %collective-permute-done.11.refs_3_, ...), custom_call_target="tpu_custom_call" | custom-call | tf_op jit(solution)/shard_map/strip_wgrad/pallas_call | solution.py:229
  79.2 4.4 %all-to-all-start.2 = ((bf16[8,9,16,512]{3,2,1,0:T(8,128)(2,1)}), bf16[8,9,16,512]{3,2,1,0:T(8,128)(2,1)}, u32[]{:S(2)}, u32[]{:S(2)}) async-start(bf16[8,9,16,512]{3,2,1,0:T(8,128)(2,1)} %copy-done.3), calls=%async_computation.2 | async-start | bytes 2359296 | tf_op jit(solution)/shard_map/all_to_all | solution.py:304
  83.7 1.6 %copy.24 = bf16[64,3,3,512]{3,2,1,0:T(4,128)(2,1)S(1)} copy(bf16[64,3,3,512]{3,0,2,1:T(8,128)(2,1)} %param.8) | data formatting | bytes 1179648 | tf_op args[3]
  85.3 1.5 %reshape.47.refs_2_ = bf16[64,4608]{1,0:T(8,128)(2,1)} reshape(bf16[64,3,3,512]{3,2,1,0:T(4,128)(2,1)S(1)} %copy.24) | data formatting | bytes 1179648 | tf_op jit(solution)/shard_map/reshape | solution.py:371
  86.8 1.5 %add.30 = f32[9,64,512]{2,1,0:T(8,128)S(1)} add(f32[9,64,512]{2,1,0:T(8,128)S(1)} %get-tuple-element.45, f32[9,64,512]{2,1,0:T(8,128)} %collective-permute-done.19) | non-fusion elementwise | flops 294912 | bytes 3538944 | tf_op jit(solution)/shard_map/add | solution.py:279
  88.3 0.7 fusion.4
  89.1 3.5 %collective-permute-start.20 = (bf16[9,16,512]{2,1,0:T(8,128)(2,1)S(1)}, bf16[9,16,512]{2,1,0:T(8,128)(2,1)S(1)}, u32[]{:S(2)}, u32[]{:S(2)}) collective-permute-start(bf16[9,16,512]{2,1,0:T(8,128)(2,1)S(1)} %get-tuple-element.47), channel_id=1, source_target_pairs={{0,1},{1,0},{2,3},{3,2},{4,5},{5,4},{6,7},{7,6},{8,9},{9,8},{10,11... | collective-permute-start | bytes 442376 | tf_op jit(solution)/shard_map/ppermute | solution.py:21
  92.6 1.9 %collective-permute-start.21 = (bf16[9,16,512]{2,1,0:T(8,128)(2,1)}, bf16[9,16,512]{2,1,0:T(8,128)(2,1)S(1)}, u32[]{:S(2)}, u32[]{:S(2)}) collective-permute-start(bf16[9,16,512]{2,1,0:T(8,128)(2,1)} %get-tuple-element.49), channel_id=1, source_target_pairs={{0,2},{1,3},{2,0},{3,1},{4,6},{5,7},{6,4},{7,5},{8,10},{9,11},{10,... | collective-permute-start | bytes 442376 | tf_op jit(solution)/shard_map/ppermute | solution.py:21
  94.4 0.5 collective-permute-start.22
  94.9 5.5 %all-to-all-done.2 = bf16[8,9,16,512]{3,2,1,0:T(8,128)(2,1)} async-done(((bf16[8,9,16,512]{3,2,1,0:T(8,128)(2,1)}), bf16[8,9,16,512]{3,2,1,0:T(8,128)(2,1)}, u32[]{:S(2)}, u32[]{:S(2)}) %all-to-all-start.2) | async-done | bytes 1179680 | tf_op jit(solution)/shard_map/all_to_all | solution.py:304
  100.4 1.6 %select_reduce_fusion = bf16[9,16,512]{2,1,0:T(8,128)(2,1)S(1)} fusion(bf16[8,9,16,512]{3,2,1,0:T(8,128)(2,1)} %all-to-all-done.2, f32[9,16,512]{2,1,0:T(8,128)S(1)} %get-tuple-element.40, pred[8]{0:T(512)(128)(4,1)S(1)} %iota_compare_fusion), kind=kLoop, calls=%fused_computation | loop fusion | flops 1695744 | bytes 1622024 | tf_op jit(solution)/shard_map/reduce_sum | solution.py:306
  102.0 0.5 collective-permute-start.13
  102.5 1.7 %collective-permute-start.15 = (bf16[64,4608]{1,0:T(8,128)(2,1)S(1)}, bf16[64,4608]{1,0:T(8,128)(2,1)}, u32[]{:S(2)}, u32[]{:S(2)}) collective-permute-start(bf16[64,4608]{1,0:T(8,128)(2,1)S(1)} %copy-done.7), channel_id=1, source_target_pairs={{0,16},{4,20},{8,24},{12,28},{16,0},{20,4},{24,8},{28,12},{1,17},{... | collective-permute-start | bytes 1769480 | tf_op jit(solution)/shard_map/ppermute | solution.py:21
  104.2 1.4 collective-permute-start.17
  105.5 0.9 broadcast_in_dim.18
  106.4 6.0 %all-to-all-start.3 = ((bf16[4,9,16,512]{3,2,1,0:T(8,128)(2,1)}), bf16[4,9,16,512]{3,2,1,0:T(8,128)(2,1)S(1)}, u32[]{:S(2)}, u32[]{:S(2)}) async-start(bf16[4,9,16,512]{3,2,1,0:T(8,128)(2,1)} %broadcast_in_dim.18), calls=%async_computation.3 | async-start | bytes 1179648 | tf_op jit(solution)/shard_map/all_to_all | solution.py:311
  112.4 0.1 fusion.2
  112.5 2.1 %collective-permute-start.23 = (bf16[9,16,512]{2,1,0:T(8,128)(2,1)S(1)}, bf16[9,16,512]{2,1,0:T(8,128)(2,1)S(1)}, u32[]{:S(2)}, u32[]{:S(2)}) collective-permute-start(bf16[9,16,512]{2,1,0:T(8,128)(2,1)S(1)} %fusion.2), channel_id=1, source_target_pairs={{0,1},{1,0},{2,3},{3,2},{4,5},{5,4},{6,7},{7,6},{8,9},{9,8},{10,11... | collective-permute-start | bytes 442376 | tf_op jit(solution)/shard_map/ppermute | solution.py:21
  114.6 2.4 %collective-permute-start.24 = (bf16[9,16,512]{2,1,0:T(8,128)(2,1)S(1)}, bf16[9,16,512]{2,1,0:T(8,128)(2,1)S(1)}, u32[]{:S(2)}, u32[]{:S(2)}) collective-permute-start(bf16[9,16,512]{2,1,0:T(8,128)(2,1)S(1)} %fusion.2), channel_id=1, source_target_pairs={{0,2},{1,3},{2,0},{3,1},{4,6},{5,7},{6,4},{7,5},{8,10},{9,11},{10,... | collective-permute-start | bytes 442376 | tf_op jit(solution)/shard_map/ppermute | solution.py:21
  117.0 9.0 %collective-permute-done.23 = bf16[9,16,512]{2,1,0:T(8,128)(2,1)S(1)} collective-permute-done((bf16[9,16,512]{2,1,0:T(8,128)(2,1)S(1)}, bf16[9,16,512]{2,1,0:T(8,128)(2,1)S(1)}, u32[]{:S(2)}, u32[]{:S(2)}) %collective-permute-start.23) | collective-permute-done | bytes 147488 | tf_op jit(solution)/shard_map/ppermute | solution.py:21
  126.0 3.9 %collective-permute-start.25 = (bf16[9,16,512]{2,1,0:T(8,128)(2,1)S(1)}, bf16[9,16,512]{2,1,0:T(8,128)(2,1)S(1)}, u32[]{:S(2)}, u32[]{:S(2)}) collective-permute-start(bf16[9,16,512]{2,1,0:T(8,128)(2,1)S(1)} %fusion.2), channel_id=1, source_target_pairs={{0,3},{1,2},{2,1},{3,0},{4,7},{5,6},{6,5},{7,4},{8,11},{9,10},{10,... | collective-permute-start | bytes 442376 | tf_op jit(solution)/shard_map/ppermute | solution.py:21
  129.8 7.3 %collective-permute-done.24 = bf16[9,16,512]{2,1,0:T(8,128)(2,1)S(1)} collective-permute-done((bf16[9,16,512]{2,1,0:T(8,128)(2,1)S(1)}, bf16[9,16,512]{2,1,0:T(8,128)(2,1)S(1)}, u32[]{:S(2)}, u32[]{:S(2)}) %collective-permute-start.24) | collective-permute-done | bytes 147488 | tf_op jit(solution)/shard_map/ppermute | solution.py:21
  137.2 0.5 collective-permute-start.14
  137.8 0.4 collective-permute-start.18
  138.2 0.1 pad_maximum_fusion
  138.3 0.1 convert_bitcast_fusion
  138.5 1.2 copy.27
  139.6 1.2 copy_convert_fusion
  140.8 0.4 collective-permute-done.16.refs_7_
  141.2 0.8 collective-permute-done.18.refs_9_
  142.1 5.2 %plain.1 = f32[384,512]{1,0:T(8,128)} custom-call(s32[3]{0:T(128)S(1)} %pad_add_fusion.refs_0_.ids, bf16[480,512]{1,0:T(8,128)(2,1)S(1)} %copy-done.5, bf16[64,4608]{1,0:T(8,128)(2,1)} %reshape.47.refs_2_, bf16[64,4608]{1,0:T(8,128)(2,1)} %copy-done.9, bf16[64,4608]{1,0:T(8,128)(2,1)} %collective-permute-done.13.refs_4_, bf16[64,4608]{1,0:T(8,128)(2,1)} %copy-done.10, ...), custom_call_target="tpu_custom_call" | custom-call | tf_op jit(solution)/shard_map/plain/pallas_call | solution.py:171
  (51 shorter events, 0.4 us)
Async XLA Ops:
  0.6 8.3 %copy-start.11 = (bf16[64,3,3,512]{3,0,2,1:T(8,128)(2,1)S(1)}, bf16[64,3,3,512]{3,0,2,1:T(8,128)(2,1)}, u32[]{:S(2)}) copy-start(bf16[64,3,3,512]{3,0,2,1:T(8,128)(2,1)} %param.9) | copy-start | bytes 1769476
  2.5 9.8 %collective-permute-start = (bf16[144,512]{1,0:T(8,128)(2,1)S(1)}, bf16[144,512]{1,0:T(8,128)(2,1)S(1)}, u32[]{:S(2)}, u32[]{:S(2)}) collective-permute-start(bf16[144,512]{1,0:T(8,128)(2,1)S(1)} %pad_maximum_fusion.1), channel_id=1, source_target_pairs={{0,1},{1,2},{2,3},{4,5},{5,6},{6,7},{8,9},{9,10},{10,11},{12,13},{... | collective-permute-start | bytes 442376 | tf_op jit(solution)/shard_map/ppermute | solution.py:351
  7.5 2.8 %copy-start.1 = (bf16[1,8,48,512]{3,2,1,0:T(8,128)(2,1)S(1)}, bf16[1,8,48,512]{3,2,1,0:T(8,128)(2,1)}, u32[]{:S(2)}) copy-start(bf16[1,8,48,512]{3,2,1,0:T(8,128)(2,1)} %param.7) | copy-start | bytes 1179652
  7.5 2.8 %copy-start.2 = (bf16[1,8,48,512]{3,2,1,0:T(8,128)(2,1)S(1)}, bf16[1,8,48,512]{3,2,1,0:T(8,128)(2,1)}, u32[]{:S(2)}) copy-start(bf16[1,8,48,512]{3,2,1,0:T(8,128)(2,1)} %param.6) | copy-start | bytes 1179652
  7.5 7.3 %collective-permute-start.1 = (bf16[144,512]{1,0:T(8,128)(2,1)S(1)}, bf16[144,512]{1,0:T(8,128)(2,1)S(1)}, u32[]{:S(2)}, u32[]{:S(2)}) collective-permute-start(bf16[144,512]{1,0:T(8,128)(2,1)S(1)} %pad_maximum_fusion.2), channel_id=1, source_target_pairs={{1,0},{2,1},{3,2},{5,4},{6,5},{7,6},{9,8},{10,9},{11,10},{13,12},{... | collective-permute-start | bytes 442376 | tf_op jit(solution)/shard_map/ppermute | solution.py:352
  10.3 37.3 %copy-start.8 = (bf16[64,4608]{1,0:T(8,128)(2,1)}, bf16[64,4608]{1,0:T(8,128)(2,1)S(1)}, u32[]{:S(2)}) copy-start(bf16[64,4608]{1,0:T(8,128)(2,1)S(1)} %reshape.44.refs_7_) | copy-start | bytes 1769476
  10.9 1.3 copy-start
  14.8 0.7 copy-start.12
  15.5 48.2 %all-to-all-start = ((bf16[4,384,640]{2,1,0:T(8,128)(2,1)}), bf16[4,384,640]{2,1,0:T(8,128)(2,1)S(1)}, u32[]{:S(2)}, u32[]{:S(2)}) async-start(bf16[4,384,640]{2,1,0:T(8,128)(2,1)} %copy-done), calls=%async_computation | async-start | bytes 3932160 | tf_op jit(solution)/shard_map/all_to_all | solution.py:354
  19.3 16.4 %collective-permute-start.2 = (bf16[64,4608]{1,0:T(8,128)(2,1)S(1)}, bf16[64,4608]{1,0:T(8,128)(2,1)}, u32[]{:S(2)}, u32[]{:S(2)}) collective-permute-start(bf16[64,4608]{1,0:T(8,128)(2,1)S(1)} %reshape.44.refs_7_), channel_id=1, source_target_pairs={{0,8},{4,12},{8,0},{12,4},{16,24},{20,28},{24,16},{28,20},{1,9},{5... | collective-permute-start | bytes 1769480 | tf_op jit(solution)/shard_map/ppermute | solution.py:21
  20.8 26.2 %collective-permute-start.3 = (bf16[64,4608]{1,0:T(8,128)(2,1)S(1)}, bf16[64,4608]{1,0:T(8,128)(2,1)}, u32[]{:S(2)}, u32[]{:S(2)}) collective-permute-start(bf16[64,4608]{1,0:T(8,128)(2,1)S(1)} %reshape.44.refs_7_), channel_id=1, source_target_pairs={{0,16},{4,20},{8,24},{12,28},{16,0},{20,4},{24,8},{28,12},{1,17},{... | collective-permute-start | bytes 1769480 | tf_op jit(solution)/shard_map/ppermute | solution.py:21
  22.4 24.7 %collective-permute-start.4 = (bf16[64,4608]{1,0:T(8,128)(2,1)S(1)}, bf16[64,4608]{1,0:T(8,128)(2,1)}, u32[]{:S(2)}, u32[]{:S(2)}) collective-permute-start(bf16[64,4608]{1,0:T(8,128)(2,1)S(1)} %reshape.44.refs_7_), channel_id=1, source_target_pairs={{0,24},{4,28},{8,16},{12,20},{16,8},{20,12},{24,0},{28,4},{1,25},{... | collective-permute-start | bytes 1769480 | tf_op jit(solution)/shard_map/ppermute | solution.py:21
  47.0 2.3 %collective-permute-start.6 = (bf16[64,4608]{1,0:T(8,128)(2,1)}, bf16[64,4608]{1,0:T(8,128)(2,1)}, u32[]{:S(2)}, u32[]{:S(2)}) collective-permute-start(bf16[64,4608]{1,0:T(8,128)(2,1)} %collective-permute-done.2.refs_9_), channel_id=1, source_target_pairs={{0,4},{4,0},{8,12},{12,8},{16,20},{20,16},{24,28},{28,24},{1,5},{5... | collective-permute-start | bytes 1769480 | tf_op jit(solution)/shard_map/ppermute | solution.py:21
  47.1 4.0 %collective-permute-start.7 = (bf16[64,4608]{1,0:T(8,128)(2,1)}, bf16[64,4608]{1,0:T(8,128)(2,1)}, u32[]{:S(2)}, u32[]{:S(2)}) collective-permute-start(bf16[64,4608]{1,0:T(8,128)(2,1)} %collective-permute-done.3.refs_11_), channel_id=1, source_target_pairs={{0,4},{4,0},{8,12},{12,8},{16,20},{20,16},{24,28},{28,24},{1,5},{5... | collective-permute-start | bytes 1769480 | tf_op jit(solution)/shard_map/ppermute | solution.py:21
  47.6 6.8 %collective-permute-start.8 = (bf16[64,4608]{1,0:T(8,128)(2,1)}, bf16[64,4608]{1,0:T(8,128)(2,1)}, u32[]{:S(2)}, u32[]{:S(2)}) collective-permute-start(bf16[64,4608]{1,0:T(8,128)(2,1)} %collective-permute-done.4.refs_13_), channel_id=1, source_target_pairs={{0,4},{4,0},{8,12},{12,8},{16,20},{20,16},{24,28},{28,24},{1,5},{5... | collective-permute-start | bytes 1769480 | tf_op jit(solution)/shard_map/ppermute | solution.py:21
  47.6 6.8 %collective-permute-start.5 = (bf16[64,4608]{1,0:T(8,128)(2,1)S(1)}, bf16[64,4608]{1,0:T(8,128)(2,1)}, u32[]{:S(2)}, u32[]{:S(2)}) collective-permute-start(bf16[64,4608]{1,0:T(8,128)(2,1)S(1)} %reshape.44.refs_7_), channel_id=1, source_target_pairs={{0,4},{4,0},{8,12},{12,8},{16,20},{20,16},{24,28},{28,24},{1,5},{5... | collective-permute-start | bytes 1769480 | tf_op jit(solution)/shard_map/ppermute | solution.py:21
  48.1 19.3 %collective-permute-start.10 = (bf16[384,512]{1,0:T(8,128)(2,1)}, bf16[384,512]{1,0:T(8,128)(2,1)}, u32[]{:S(2)}, u32[]{:S(2)}) collective-permute-start(bf16[384,512]{1,0:T(8,128)(2,1)} %bitcast.9.refs_1_), channel_id=1, source_target_pairs={{0,8},{4,12},{8,0},{12,4},{16,24},{20,28},{24,16},{28,20},{1,9},{5... | collective-permute-start | bytes 1179656 | tf_op jit(solution)/shard_map/ppermute | solution.py:21
  49.4 21.1 %collective-permute-start.11 = (bf16[384,512]{1,0:T(8,128)(2,1)}, bf16[384,512]{1,0:T(8,128)(2,1)}, u32[]{:S(2)}, u32[]{:S(2)}) collective-permute-start(bf16[384,512]{1,0:T(8,128)(2,1)} %bitcast.9.refs_1_), channel_id=1, source_target_pairs={{0,16},{4,20},{8,24},{12,28},{16,0},{20,4},{24,8},{28,12},{1,17},{... | collective-permute-start | bytes 1179656 | tf_op jit(solution)/shard_map/ppermute | solution.py:21
  51.1 19.5 %collective-permute-start.12 = (bf16[384,512]{1,0:T(8,128)(2,1)}, bf16[384,512]{1,0:T(8,128)(2,1)}, u32[]{:S(2)}, u32[]{:S(2)}) collective-permute-start(bf16[384,512]{1,0:T(8,128)(2,1)} %bitcast.9.refs_1_), channel_id=1, source_target_pairs={{0,24},{4,28},{8,16},{12,20},{16,8},{20,12},{24,0},{28,4},{1,25},{... | collective-permute-start | bytes 1179656 | tf_op jit(solution)/shard_map/ppermute | solution.py:21
  59.3 0.8 copy-start.4
  60.1 0.8 copy-start.6
  63.7 10.9 %all-to-all-start.1 = ((bf16[4,480,128]{2,1,0:T(8,128)(2,1)}), bf16[4,480,128]{2,1,0:T(8,128)(2,1)S(1)}, u32[]{:S(2)}, u32[]{:S(2)}) async-start(bf16[4,480,128]{2,1,0:T(8,128)(2,1)} %copy-done.6), calls=%async_computation.1 | async-start | bytes 983040 | tf_op jit(solution)/shard_map/all_to_all | solution.py:365
  73.6 1.0 copy-start.3
  79.2 7.7 %collective-permute-start.19 = (f32[9,64,512]{2,1,0:T(8,128)S(1)}, f32[9,64,512]{2,1,0:T(8,128)}, u32[]{:S(2)}, u32[]{:S(2)}) collective-permute-start(f32[9,64,512]{2,1,0:T(8,128)S(1)} %get-tuple-element.46), channel_id=1, source_target_pairs={{0,4},{4,0},{8,12},{12,8},{16,20},{20,16},{24,28},{28,24},{1,5},{5... | collective-permute-start | bytes 3538952 | tf_op jit(solution)/shard_map/ppermute | solution.py:21
  79.2 21.2 %all-to-all-start.2 = ((bf16[8,9,16,512]{3,2,1,0:T(8,128)(2,1)}), bf16[8,9,16,512]{3,2,1,0:T(8,128)(2,1)}, u32[]{:S(2)}, u32[]{:S(2)}) async-start(bf16[8,9,16,512]{3,2,1,0:T(8,128)(2,1)} %copy-done.3), calls=%async_computation.2 | async-start | bytes 2359296 | tf_op jit(solution)/shard_map/all_to_all | solution.py:304
  88.3 13.6 %copy-start.7 = (bf16[64,4608]{1,0:T(8,128)(2,1)S(1)}, bf16[64,4608]{1,0:T(8,128)(2,1)}, u32[]{:S(2)}) copy-start(bf16[64,4608]{1,0:T(8,128)(2,1)} %reshape.47.refs_2_) | copy-start | bytes 1769476
  89.1 15.1 %collective-permute-start.20 = (bf16[9,16,512]{2,1,0:T(8,128)(2,1)S(1)}, bf16[9,16,512]{2,1,0:T(8,128)(2,1)S(1)}, u32[]{:S(2)}, u32[]{:S(2)}) collective-permute-start(bf16[9,16,512]{2,1,0:T(8,128)(2,1)S(1)} %get-tuple-element.47), channel_id=1, source_target_pairs={{0,1},{1,0},{2,3},{3,2},{4,5},{5,4},{6,7},{7,6},{8,9},{9,8},{10,11... | collective-permute-start | bytes 442376 | tf_op jit(solution)/shard_map/ppermute | solution.py:21
  92.6 19.9 %collective-permute-start.21 = (bf16[9,16,512]{2,1,0:T(8,128)(2,1)}, bf16[9,16,512]{2,1,0:T(8,128)(2,1)S(1)}, u32[]{:S(2)}, u32[]{:S(2)}) collective-permute-start(bf16[9,16,512]{2,1,0:T(8,128)(2,1)} %get-tuple-element.49), channel_id=1, source_target_pairs={{0,2},{1,3},{2,0},{3,1},{4,6},{5,7},{6,4},{7,5},{8,10},{9,11},{10,... | collective-permute-start | bytes 442376 | tf_op jit(solution)/shard_map/ppermute | solution.py:21
  94.4 18.0 %collective-permute-start.22 = (bf16[9,16,512]{2,1,0:T(8,128)(2,1)S(1)}, bf16[9,16,512]{2,1,0:T(8,128)(2,1)S(1)}, u32[]{:S(2)}, u32[]{:S(2)}) collective-permute-start(bf16[9,16,512]{2,1,0:T(8,128)(2,1)S(1)} %get-tuple-element.48), channel_id=1, source_target_pairs={{0,3},{1,2},{2,1},{3,0},{4,7},{5,6},{6,5},{7,4},{8,11},{9,10},{10,... | collective-permute-start | bytes 442376 | tf_op jit(solution)/shard_map/ppermute | solution.py:21
  102.0 35.2 %collective-permute-start.13 = (bf16[64,4608]{1,0:T(8,128)(2,1)S(1)}, bf16[64,4608]{1,0:T(8,128)(2,1)}, u32[]{:S(2)}, u32[]{:S(2)}) collective-permute-start(bf16[64,4608]{1,0:T(8,128)(2,1)S(1)} %copy-done.7), channel_id=1, source_target_pairs={{0,8},{4,12},{8,0},{12,4},{16,24},{20,28},{24,16},{28,20},{1,9},{5... | collective-permute-start | bytes 1769480 | tf_op jit(solution)/shard_map/ppermute | solution.py:21
  102.5 35.2 %collective-permute-start.15 = (bf16[64,4608]{1,0:T(8,128)(2,1)S(1)}, bf16[64,4608]{1,0:T(8,128)(2,1)}, u32[]{:S(2)}, u32[]{:S(2)}) collective-permute-start(bf16[64,4608]{1,0:T(8,128)(2,1)S(1)} %copy-done.7), channel_id=1, source_target_pairs={{0,16},{4,20},{8,24},{12,28},{16,0},{20,4},{24,8},{28,12},{1,17},{... | collective-permute-start | bytes 1769480 | tf_op jit(solution)/shard_map/ppermute | solution.py:21
  104.2 33.6 %collective-permute-start.17 = (bf16[64,4608]{1,0:T(8,128)(2,1)S(1)}, bf16[64,4608]{1,0:T(8,128)(2,1)}, u32[]{:S(2)}, u32[]{:S(2)}) collective-permute-start(bf16[64,4608]{1,0:T(8,128)(2,1)S(1)} %copy-done.7), channel_id=1, source_target_pairs={{0,24},{4,28},{8,16},{12,20},{16,8},{20,12},{24,0},{28,4},{1,25},{... | collective-permute-start | bytes 1769480 | tf_op jit(solution)/shard_map/ppermute | solution.py:21
  106.4 33.2 %all-to-all-start.3 = ((bf16[4,9,16,512]{3,2,1,0:T(8,128)(2,1)}), bf16[4,9,16,512]{3,2,1,0:T(8,128)(2,1)S(1)}, u32[]{:S(2)}, u32[]{:S(2)}) async-start(bf16[4,9,16,512]{3,2,1,0:T(8,128)(2,1)} %broadcast_in_dim.18), calls=%async_computation.3 | async-start | bytes 1179648 | tf_op jit(solution)/shard_map/all_to_all | solution.py:311
  112.5 13.5 %collective-permute-start.23 = (bf16[9,16,512]{2,1,0:T(8,128)(2,1)S(1)}, bf16[9,16,512]{2,1,0:T(8,128)(2,1)S(1)}, u32[]{:S(2)}, u32[]{:S(2)}) collective-permute-start(bf16[9,16,512]{2,1,0:T(8,128)(2,1)S(1)} %fusion.2), channel_id=1, source_target_pairs={{0,1},{1,0},{2,3},{3,2},{4,5},{5,4},{6,7},{7,6},{8,9},{9,8},{10,11... | collective-permute-start | bytes 442376 | tf_op jit(solution)/shard_map/ppermute | solution.py:21
  114.6 22.6 %collective-permute-start.24 = (bf16[9,16,512]{2,1,0:T(8,128)(2,1)S(1)}, bf16[9,16,512]{2,1,0:T(8,128)(2,1)S(1)}, u32[]{:S(2)}, u32[]{:S(2)}) collective-permute-start(bf16[9,16,512]{2,1,0:T(8,128)(2,1)S(1)} %fusion.2), channel_id=1, source_target_pairs={{0,2},{1,3},{2,0},{3,1},{4,6},{5,7},{6,4},{7,5},{8,10},{9,11},{10,... | collective-permute-start | bytes 442376 | tf_op jit(solution)/shard_map/ppermute | solution.py:21
  126.0 12.2 %collective-permute-start.25 = (bf16[9,16,512]{2,1,0:T(8,128)(2,1)S(1)}, bf16[9,16,512]{2,1,0:T(8,128)(2,1)S(1)}, u32[]{:S(2)}, u32[]{:S(2)}) collective-permute-start(bf16[9,16,512]{2,1,0:T(8,128)(2,1)S(1)} %fusion.2), channel_id=1, source_target_pairs={{0,3},{1,2},{2,1},{3,0},{4,7},{5,6},{6,5},{7,4},{8,11},{9,10},{10,... | collective-permute-start | bytes 442376 | tf_op jit(solution)/shard_map/ppermute | solution.py:21
  137.2 3.6 %collective-permute-start.9 = (bf16[64,4608]{1,0:T(8,128)(2,1)S(1)}, bf16[64,4608]{1,0:T(8,128)(2,1)S(1)}, u32[]{:S(2)}, u32[]{:S(2)}) collective-permute-start(bf16[64,4608]{1,0:T(8,128)(2,1)S(1)} %copy-done.7), channel_id=1, source_target_pairs={{0,4},{4,0},{8,12},{12,8},{16,20},{20,16},{24,28},{28,24},{1,5},{5... | collective-permute-start | bytes 1769480 | tf_op jit(solution)/shard_map/ppermute | solution.py:21
  137.2 3.6 %collective-permute-start.14 = (bf16[64,4608]{1,0:T(8,128)(2,1)}, bf16[64,4608]{1,0:T(8,128)(2,1)S(1)}, u32[]{:S(2)}, u32[]{:S(2)}) collective-permute-start(bf16[64,4608]{1,0:T(8,128)(2,1)} %collective-permute-done.13.refs_4_), channel_id=1, source_target_pairs={{0,4},{4,0},{8,12},{12,8},{16,20},{20,16},{24,28},{28,24},{1,5},{5... | collective-permute-start | bytes 1769480 | tf_op jit(solution)/shard_map/ppermute | solution.py:21
  137.7 3.5 %collective-permute-start.16 = (bf16[64,4608]{1,0:T(8,128)(2,1)}, bf16[64,4608]{1,0:T(8,128)(2,1)}, u32[]{:S(2)}, u32[]{:S(2)}) collective-permute-start(bf16[64,4608]{1,0:T(8,128)(2,1)} %collective-permute-done.15.refs_6_), channel_id=1, source_target_pairs={{0,4},{4,0},{8,12},{12,8},{16,20},{20,16},{24,28},{28,24},{1,5},{5... | collective-permute-start | bytes 1769480 | tf_op jit(solution)/shard_map/ppermute | solution.py:21
  137.8 4.3 %collective-permute-start.18 = (bf16[64,4608]{1,0:T(8,128)(2,1)}, bf16[64,4608]{1,0:T(8,128)(2,1)}, u32[]{:S(2)}, u32[]{:S(2)}) collective-permute-start(bf16[64,4608]{1,0:T(8,128)(2,1)} %collective-permute-done.17.refs_8_), channel_id=1, source_target_pairs={{0,4},{4,0},{8,12},{12,8},{16,20},{20,16},{24,28},{28,24},{1,5},{5... | collective-permute-start | bytes 1769480 | tf_op jit(solution)/shard_map/ppermute | solution.py:21
  139.6 2.4 %copy-start.5 = (bf16[480,512]{1,0:T(8,128)(2,1)S(1)}, bf16[480,512]{1,0:T(8,128)(2,1)}, u32[]{:S(2)}) copy-start(bf16[480,512]{1,0:T(8,128)(2,1)} %copy-done.4) | copy-start | bytes 1474564
  140.8 1.3 copy-start.9
  140.8 1.3 copy-start.10

commit v7 on v6

--- a/solution.py
+++ b/solution.py
@@ -352,12 +352,12 @@
     below = lax.ppermute(head, "space", up_pairs)
     w2, ready, above, below = lax.optimization_barrier((w2, ready, above, below))
     image = lax.all_to_all(ready, "space", 0, 0)
-    w2_shards = lax.optimization_barrier([w2] + sent_to_chips(w2))
+    w2_shards = [w2] + sent_to_chips(w2)
     shards = sent_to_pair(w2_shards)
     gup, hup = above[: 2 * width], above[2 * width :]
     gdown, hdown = below[: 2 * width], below[2 * width :]
 
-    xs = [x] + sent_to_chips(after(x, *w2_shards[1:]))
+    xs = [x] + sent_to_chips(after(x, w2_shards[1]))
 
     pre_ext, pieces = gated(ids, gup, g, gdown, hup, h, hdown, shards, width, chips)
     pieces, image = lax.optimization_barrier((pieces, image))

time: 148 us -> 146 us (0.986)
  starting transfers between devices: 51.9 us -> 48.4 us
  waiting for transfers between devices: 56 us -> 57.6 us
    ppermute x24, waiting for transfers between devices: 45.2 us -> 41.9 us  [swap(): return lax.ppermute(value, axis, xor_pairs(lax.axis_size(axis), k))]
    all_to_all x1, starting transfers between devices: 5.99 us -> 3.86 us  [strips_shared(): lax.all_to_all(jnp.broadcast_to(mine, (count,) + mine.shape), 'space', 0, 0)]
    all_to_all x1, waiting for transfers between devices: 0.01 us -> 2.06 us  [per_device(): p_cots = lax.all_to_all(pieces, 'dp', 0, 0, axis_index_groups=same_core)]
    all_to_all x1, waiting for transfers between devices: 2.76 us -> 4.28 us  [per_device(): image = lax.all_to_all(ready, 'space', 0, 0)]
  transfers between devices with their start and end apart: 30 -> 30, of which waited for: 12 -> 11; matrix products, arithmetic and copies ran while one was open for 9% -> 9% of each run, Pallas kernels for 6% -> 6%
where the time goes in v7:
time: 146 us; the launch traced here: 145 us
  waiting for transfers between devices  57.6 us (39%)
  starting transfers between devices  48.4 us (33%)
  Pallas kernels  18.3 us (13%)
  local copies, waits for them, and re-layouts  15.4 us (11%)
  other arithmetic  4.62 us (3%)
    ppermute x24, waiting for transfers between devices, swap(): return lax.ppermute(value, axis, xor_pairs(lax.axis_size(axis), k))  41.9 us
    ppermute x24, starting transfers between devices, swap(): return lax.ppermute(value, axis, xor_pairs(lax.axis_size(axis), k))  26.1 us
    all_to_all x1, waiting for transfers between devices, images_summed(): got = lax.all_to_all(parts, 'dp', 0, 0)  6.86 us
    unnamed x28, local copies, waits for them, and re-layouts  6.69 us
    pallas_call x1, Pallas kernels, plain(): pl.pallas_call(plain_kernel(count, width), out_shape=jax.ShapeDtypeStruct...  5.22 us
    ppermute x1, starting transfers between devices, per_device(): above = lax.ppermute(tail, 'space', down_pairs)  4.94 us
    pallas_call x1, Pallas kernels, gated(): pl.pallas_call(gated_kernel(count, width), out_shape=[jax.ShapeDtypeStruc...  4.93 us
    pallas_call x1, Pallas kernels, strip_wgrad(): pl.pallas_call(strip_kernel(count, width), out_shape=[half, half], in_spe...  4.53 us
  transfers between devices with their start and end apart: 30, of which 11 were waited for; matrix products, arithmetic and copies ran while one was open for 9% of the time, Pallas kernels for 6%

profile of v7, /device:TPU:0, one launch (start us, length us, event | category | flops | bytes accessed | tf_op | source)
XLA Modules:
  0.0 145.5 jit_solution(12448450016432052458)
XLA Ops:
  0.6 1.0 fusion.6
  1.7 0.8 slice_bitcast_fusion
  2.5 4.9 %collective-permute-start = (bf16[144,512]{1,0:T(8,128)(2,1)S(1)}, bf16[144,512]{1,0:T(8,128)(2,1)S(1)}, u32[]{:S(2)}, u32[]{:S(2)}) collective-permute-start(bf16[144,512]{1,0:T(8,128)(2,1)S(1)} %pad_maximum_fusion.1), channel_id=1, source_target_pairs={{0,1},{1,2},{2,3},{4,5},{5,6},{6,7},{8,9},{9,10},{10,11},{12,13},{... | collective-permute-start | bytes 442376 | tf_op jit(solution)/shard_map/ppermute | solution.py:351
  7.5 1.4 collective-permute-start.1
  8.9 0.5 copy.23
  9.5 0.8 reshape.44.refs_7_
  10.3 0.6 prepared.1
  10.9 1.3 copy-done
  12.3 2.6 %collective-permute-done.1 = bf16[144,512]{1,0:T(8,128)(2,1)S(1)} collective-permute-done((bf16[144,512]{1,0:T(8,128)(2,1)S(1)}, bf16[144,512]{1,0:T(8,128)(2,1)S(1)}, u32[]{:S(2)}, u32[]{:S(2)}) %collective-permute-start.1) | collective-permute-done | bytes 147488 | tf_op jit(solution)/shard_map/ppermute | solution.py:352
  14.8 0.7 copy-done.12
  15.5 3.9 %all-to-all-start = ((bf16[4,384,640]{2,1,0:T(8,128)(2,1)}), bf16[4,384,640]{2,1,0:T(8,128)(2,1)S(1)}, u32[]{:S(2)}, u32[]{:S(2)}) async-start(bf16[4,384,640]{2,1,0:T(8,128)(2,1)} %copy-done), calls=%async_computation | async-start | bytes 3932160 | tf_op jit(solution)/shard_map/all_to_all | solution.py:354
  19.3 1.5 %collective-permute-start.3 = (bf16[64,4608]{1,0:T(8,128)(2,1)S(1)}, bf16[64,4608]{1,0:T(8,128)(2,1)}, u32[]{:S(2)}, u32[]{:S(2)}) collective-permute-start(bf16[64,4608]{1,0:T(8,128)(2,1)S(1)} %reshape.44.refs_7_), channel_id=1, source_target_pairs={{0,8},{4,12},{8,0},{12,4},{16,24},{20,28},{24,16},{28,20},{1,9},{5... | collective-permute-start | bytes 1769480 | tf_op jit(solution)/shard_map/ppermute | solution.py:21
  20.8 1.5 %collective-permute-start.5 = (bf16[64,4608]{1,0:T(8,128)(2,1)S(1)}, bf16[64,4608]{1,0:T(8,128)(2,1)}, u32[]{:S(2)}, u32[]{:S(2)}) collective-permute-start(bf16[64,4608]{1,0:T(8,128)(2,1)S(1)} %reshape.44.refs_7_), channel_id=1, source_target_pairs={{0,16},{4,20},{8,24},{12,28},{16,0},{20,4},{24,8},{28,12},{1,17},{... | collective-permute-start | bytes 1769480 | tf_op jit(solution)/shard_map/ppermute | solution.py:21
  22.4 0.5 collective-permute-start.7
  22.8 12.9 %collective-permute-done.3.refs_9_ = bf16[64,4608]{1,0:T(8,128)(2,1)} collective-permute-done((bf16[64,4608]{1,0:T(8,128)(2,1)S(1)}, bf16[64,4608]{1,0:T(8,128)(2,1)}, u32[]{:S(2)}, u32[]{:S(2)}) %collective-permute-start.3) | collective-permute-done | bytes 589856 | tf_op jit(solution)/shard_map/ppermute | solution.py:21
  35.7 11.3 %collective-permute-done.5.refs_11_ = bf16[64,4608]{1,0:T(8,128)(2,1)} collective-permute-done((bf16[64,4608]{1,0:T(8,128)(2,1)S(1)}, bf16[64,4608]{1,0:T(8,128)(2,1)}, u32[]{:S(2)}, u32[]{:S(2)}) %collective-permute-start.5) | collective-permute-done | bytes 589856 | tf_op jit(solution)/shard_map/ppermute | solution.py:21
  47.1 0.5 collective-permute-start.8
  47.6 0.7 collective-permute-start.10
  48.3 1.3 collective-permute-start.11
  49.6 1.4 collective-permute-start.12
  51.1 0.1 pad_add_fusion.refs_0_.ids
  51.2 0.9 slice.45.refs_3_
  52.1 0.8 slice.47.refs_6_
  52.9 4.9 %gated.1 = (bf16[480,512]{1,0:T(8,128)(2,1)S(1)}, bf16[4,480,128]{2,1,0:T(8,128)(2,1)S(1)}) custom-call(s32[3]{0:T(128)S(1)} %pad_add_fusion.refs_0_.ids, bf16[96,512]{1,0:T(8,128)(2,1)S(1)} %slice.44.refs_1_, bf16[384,512]{1,0:T(8,128)(2,1)S(1)} %bitcast.47, bf16[96,512]{1,0:T(8,128)(2,1)S(1)} %slice.45.refs_3_, bf16[48,512]{1,0:T(8,128)(2,1)S(1)} %slice.46.refs_4_, ...), custom_call_target="tpu_custom_call" | custom-call | tf_op jit(solution)/shard_map/gated/pallas_call | solution.py:134
  57.8 0.8 copy-done.4
  58.6 0.8 copy-done.6
  59.4 4.3 %all-to-all-done.image = bf16[4,384,640]{2,1,0:T(8,128)(2,1)S(1)} async-done(((bf16[4,384,640]{2,1,0:T(8,128)(2,1)}), bf16[4,384,640]{2,1,0:T(8,128)(2,1)S(1)}, u32[]{:S(2)}, u32[]{:S(2)}) %all-to-all-start) | async-done | bytes 1966112 | tf_op jit(solution)/shard_map/all_to_all | solution.py:354
  63.7 3.7 %all-to-all-start.1 = ((bf16[4,480,128]{2,1,0:T(8,128)(2,1)}), bf16[4,480,128]{2,1,0:T(8,128)(2,1)S(1)}, u32[]{:S(2)}, u32[]{:S(2)}) async-start(bf16[4,480,128]{2,1,0:T(8,128)(2,1)} %copy-done.6), calls=%async_computation.1 | async-start | bytes 983040 | tf_op jit(solution)/shard_map/all_to_all | solution.py:365
  67.4 0.9 collective-permute-done.12.refs_4_
  68.3 3.0 %image_wgrad.1 = (f32[9,16,512]{2,1,0:T(8,128)S(1)}, bf16[8,9,16,512]{3,2,1,0:T(8,128)(2,1)S(1)}) custom-call(s32[3]{0:T(128)S(1)} %pad_add_fusion.refs_0_.ids, bf16[4,384,640]{2,1,0:T(8,128)(2,1)S(1)} %all-to-all-done.image), custom_call_target="tpu_custom_call" | custom-call | tf_op jit(solution)/shard_map/image_wgrad/pallas_call | solution.py:264
  71.3 1.0 copy-done.3
  72.3 2.1 %all-to-all-done.1.refs_5_ = bf16[4,480,128]{2,1,0:T(8,128)(2,1)S(1)} async-done(((bf16[4,480,128]{2,1,0:T(8,128)(2,1)}), bf16[4,480,128]{2,1,0:T(8,128)(2,1)S(1)}, u32[]{:S(2)}, u32[]{:S(2)}) %all-to-all-start.1) | async-done | bytes 491552 | tf_op jit(solution)/shard_map/all_to_all | solution.py:365
  74.4 4.5 %strip_wgrad.1 = (f32[9,64,512]{2,1,0:T(8,128)S(1)}, f32[9,64,512]{2,1,0:T(8,128)S(1)}) custom-call(s32[3]{0:T(128)S(1)} %pad_add_fusion.refs_0_.ids, bf16[384,512]{1,0:T(8,128)(2,1)} %bitcast.9.refs_1_, bf16[384,512]{1,0:T(8,128)(2,1)} %collective-permute-done.10.refs_2_, bf16[384,512]{1,0:T(8,128)(2,1)} %collective-permute-done.11.refs_3_, ...), custom_call_target="tpu_custom_call" | custom-call | tf_op jit(solution)/shard_map/strip_wgrad/pallas_call | solution.py:229
  78.9 0.1 collective-permute-start.19
  79.0 4.4 %all-to-all-start.2 = ((bf16[8,9,16,512]{3,2,1,0:T(8,128)(2,1)}), bf16[8,9,16,512]{3,2,1,0:T(8,128)(2,1)}, u32[]{:S(2)}, u32[]{:S(2)}) async-start(bf16[8,9,16,512]{3,2,1,0:T(8,128)(2,1)} %copy-done.3), calls=%async_computation.2 | async-start | bytes 2359296 | tf_op jit(solution)/shard_map/all_to_all | solution.py:304
  83.5 1.6 %copy.24 = bf16[64,3,3,512]{3,2,1,0:T(4,128)(2,1)S(1)} copy(bf16[64,3,3,512]{3,0,2,1:T(8,128)(2,1)} %param.8) | data formatting | bytes 1179648 | tf_op args[3]
  85.1 1.5 %reshape.47.refs_2_ = bf16[64,4608]{1,0:T(8,128)(2,1)} reshape(bf16[64,3,3,512]{3,2,1,0:T(4,128)(2,1)S(1)} %copy.24) | data formatting | bytes 1179648 | tf_op jit(solution)/shard_map/reshape | solution.py:371
  86.6 1.5 %add.30 = f32[9,64,512]{2,1,0:T(8,128)S(1)} add(f32[9,64,512]{2,1,0:T(8,128)S(1)} %get-tuple-element.37, f32[9,64,512]{2,1,0:T(8,128)} %collective-permute-done.19) | non-fusion elementwise | flops 294912 | bytes 3538944 | tf_op jit(solution)/shard_map/add | solution.py:279
  88.1 0.7 fusion.4
  88.9 0.8 collective-permute-start.20
  89.7 2.4 %collective-permute-start.21 = (bf16[9,16,512]{2,1,0:T(8,128)(2,1)}, bf16[9,16,512]{2,1,0:T(8,128)(2,1)S(1)}, u32[]{:S(2)}, u32[]{:S(2)}) collective-permute-start(bf16[9,16,512]{2,1,0:T(8,128)(2,1)} %get-tuple-element.41), channel_id=1, source_target_pairs={{0,2},{1,3},{2,0},{3,1},{4,6},{5,7},{6,4},{7,5},{8,10},{9,11},{10,... | collective-permute-start | bytes 442376 | tf_op jit(solution)/shard_map/ppermute | solution.py:21
  92.0 1.2 collective-permute-start.22
  93.3 6.9 %all-to-all-done.2 = bf16[8,9,16,512]{3,2,1,0:T(8,128)(2,1)} async-done(((bf16[8,9,16,512]{3,2,1,0:T(8,128)(2,1)}), bf16[8,9,16,512]{3,2,1,0:T(8,128)(2,1)}, u32[]{:S(2)}, u32[]{:S(2)}) %all-to-all-start.2) | async-done | bytes 1179680 | tf_op jit(solution)/shard_map/all_to_all | solution.py:304
  100.1 1.6 %select_reduce_fusion = bf16[9,16,512]{2,1,0:T(8,128)(2,1)S(1)} fusion(bf16[8,9,16,512]{3,2,1,0:T(8,128)(2,1)} %all-to-all-done.2, f32[9,16,512]{2,1,0:T(8,128)S(1)} %get-tuple-element.32, pred[8]{0:T(512)(128)(4,1)S(1)} %iota_compare_fusion), kind=kLoop, calls=%fused_computation | loop fusion | flops 1695744 | bytes 1622024 | tf_op jit(solution)/shard_map/reduce_sum | solution.py:306
  101.7 0.6 collective-permute-start.13
  102.3 0.7 collective-permute-start.15
  102.9 2.3 %collective-permute-start.17 = (bf16[64,4608]{1,0:T(8,128)(2,1)S(1)}, bf16[64,4608]{1,0:T(8,128)(2,1)}, u32[]{:S(2)}, u32[]{:S(2)}) collective-permute-start(bf16[64,4608]{1,0:T(8,128)(2,1)S(1)} %copy-done.7), channel_id=1, source_target_pairs={{0,24},{4,28},{8,16},{12,20},{16,8},{20,12},{24,0},{28,4},{1,25},{... | collective-permute-start | bytes 1769480 | tf_op jit(solution)/shard_map/ppermute | solution.py:21
  105.3 0.9 broadcast_in_dim.18
  106.1 3.9 %all-to-all-start.3 = ((bf16[4,9,16,512]{3,2,1,0:T(8,128)(2,1)}), bf16[4,9,16,512]{3,2,1,0:T(8,128)(2,1)S(1)}, u32[]{:S(2)}, u32[]{:S(2)}) async-start(bf16[4,9,16,512]{3,2,1,0:T(8,128)(2,1)} %broadcast_in_dim.18), calls=%async_computation.3 | async-start | bytes 1179648 | tf_op jit(solution)/shard_map/all_to_all | solution.py:311
  110.0 0.1 fusion.2
  110.1 2.1 %collective-permute-start.23 = (bf16[9,16,512]{2,1,0:T(8,128)(2,1)S(1)}, bf16[9,16,512]{2,1,0:T(8,128)(2,1)S(1)}, u32[]{:S(2)}, u32[]{:S(2)}) collective-permute-start(bf16[9,16,512]{2,1,0:T(8,128)(2,1)S(1)} %fusion.2), channel_id=1, source_target_pairs={{0,1},{1,0},{2,3},{3,2},{4,5},{5,4},{6,7},{7,6},{8,9},{9,8},{10,11... | collective-permute-start | bytes 442376 | tf_op jit(solution)/shard_map/ppermute | solution.py:21
  112.2 2.4 %collective-permute-start.24 = (bf16[9,16,512]{2,1,0:T(8,128)(2,1)S(1)}, bf16[9,16,512]{2,1,0:T(8,128)(2,1)S(1)}, u32[]{:S(2)}, u32[]{:S(2)}) collective-permute-start(bf16[9,16,512]{2,1,0:T(8,128)(2,1)S(1)} %fusion.2), channel_id=1, source_target_pairs={{0,2},{1,3},{2,0},{3,1},{4,6},{5,7},{6,4},{7,5},{8,10},{9,11},{10,... | collective-permute-start | bytes 442376 | tf_op jit(solution)/shard_map/ppermute | solution.py:21
  114.6 8.2 %collective-permute-done.23 = bf16[9,16,512]{2,1,0:T(8,128)(2,1)S(1)} collective-permute-done((bf16[9,16,512]{2,1,0:T(8,128)(2,1)S(1)}, bf16[9,16,512]{2,1,0:T(8,128)(2,1)S(1)}, u32[]{:S(2)}, u32[]{:S(2)}) %collective-permute-start.23) | collective-permute-done | bytes 147488 | tf_op jit(solution)/shard_map/ppermute | solution.py:21
  122.7 5.1 %collective-permute-start.25 = (bf16[9,16,512]{2,1,0:T(8,128)(2,1)S(1)}, bf16[9,16,512]{2,1,0:T(8,128)(2,1)S(1)}, u32[]{:S(2)}, u32[]{:S(2)}) collective-permute-start(bf16[9,16,512]{2,1,0:T(8,128)(2,1)S(1)} %fusion.2), channel_id=1, source_target_pairs={{0,3},{1,2},{2,1},{3,0},{4,7},{5,6},{6,5},{7,4},{8,11},{9,10},{10,... | collective-permute-start | bytes 442376 | tf_op jit(solution)/shard_map/ppermute | solution.py:21
  127.9 7.3 %collective-permute-done.24 = bf16[9,16,512]{2,1,0:T(8,128)(2,1)S(1)} collective-permute-done((bf16[9,16,512]{2,1,0:T(8,128)(2,1)S(1)}, bf16[9,16,512]{2,1,0:T(8,128)(2,1)S(1)}, u32[]{:S(2)}, u32[]{:S(2)}) %collective-permute-start.24) | collective-permute-done | bytes 147488 | tf_op jit(solution)/shard_map/ppermute | solution.py:21
  135.2 0.5 collective-permute-start.14
  135.8 0.4 collective-permute-start.18
  136.2 0.1 pad_maximum_fusion
  136.4 0.1 convert_bitcast_fusion
  136.5 1.2 copy.27
  137.6 1.2 copy_convert_fusion
  138.8 0.4 collective-permute-done.16.refs_7_
  139.2 0.8 collective-permute-done.18.refs_9_
  140.1 5.2 %plain.1 = f32[384,512]{1,0:T(8,128)} custom-call(s32[3]{0:T(128)S(1)} %pad_add_fusion.refs_0_.ids, bf16[480,512]{1,0:T(8,128)(2,1)S(1)} %copy-done.5, bf16[64,4608]{1,0:T(8,128)(2,1)} %reshape.47.refs_2_, bf16[64,4608]{1,0:T(8,128)(2,1)} %copy-done.9, bf16[64,4608]{1,0:T(8,128)(2,1)} %collective-permute-done.13.refs_4_, bf16[64,4608]{1,0:T(8,128)(2,1)} %copy-done.10, ...), custom_call_target="tpu_custom_call" | custom-call | tf_op jit(solution)/shard_map/plain/pallas_call | solution.py:171
  (51 shorter events, 0.3 us)
Async XLA Ops:
  0.6 8.3 %copy-start.11 = (bf16[64,3,3,512]{3,0,2,1:T(8,128)(2,1)S(1)}, bf16[64,3,3,512]{3,0,2,1:T(8,128)(2,1)}, u32[]{:S(2)}) copy-start(bf16[64,3,3,512]{3,0,2,1:T(8,128)(2,1)} %param.9) | copy-start | bytes 1769476
  2.5 9.8 %collective-permute-start = (bf16[144,512]{1,0:T(8,128)(2,1)S(1)}, bf16[144,512]{1,0:T(8,128)(2,1)S(1)}, u32[]{:S(2)}, u32[]{:S(2)}) collective-permute-start(bf16[144,512]{1,0:T(8,128)(2,1)S(1)} %pad_maximum_fusion.1), channel_id=1, source_target_pairs={{0,1},{1,2},{2,3},{4,5},{5,6},{6,7},{8,9},{9,10},{10,11},{12,13},{... | collective-permute-start | bytes 442376 | tf_op jit(solution)/shard_map/ppermute | solution.py:351
  7.5 2.8 %copy-start.1 = (bf16[1,8,48,512]{3,2,1,0:T(8,128)(2,1)S(1)}, bf16[1,8,48,512]{3,2,1,0:T(8,128)(2,1)}, u32[]{:S(2)}) copy-start(bf16[1,8,48,512]{3,2,1,0:T(8,128)(2,1)} %param.7) | copy-start | bytes 1179652
  7.5 2.8 %copy-start.2 = (bf16[1,8,48,512]{3,2,1,0:T(8,128)(2,1)S(1)}, bf16[1,8,48,512]{3,2,1,0:T(8,128)(2,1)}, u32[]{:S(2)}) copy-start(bf16[1,8,48,512]{3,2,1,0:T(8,128)(2,1)} %param.6) | copy-start | bytes 1179652
  7.5 7.3 %collective-permute-start.1 = (bf16[144,512]{1,0:T(8,128)(2,1)S(1)}, bf16[144,512]{1,0:T(8,128)(2,1)S(1)}, u32[]{:S(2)}, u32[]{:S(2)}) collective-permute-start(bf16[144,512]{1,0:T(8,128)(2,1)S(1)} %pad_maximum_fusion.2), channel_id=1, source_target_pairs={{1,0},{2,1},{3,2},{5,4},{6,5},{7,6},{9,8},{10,9},{11,10},{13,12},{... | collective-permute-start | bytes 442376 | tf_op jit(solution)/shard_map/ppermute | solution.py:352
  10.3 12.5 %copy-start.8 = (bf16[64,4608]{1,0:T(8,128)(2,1)}, bf16[64,4608]{1,0:T(8,128)(2,1)S(1)}, u32[]{:S(2)}) copy-start(bf16[64,4608]{1,0:T(8,128)(2,1)S(1)} %reshape.44.refs_7_) | copy-start | bytes 1769476
  10.9 1.3 copy-start
  14.8 0.7 copy-start.12
  15.5 48.2 %all-to-all-start = ((bf16[4,384,640]{2,1,0:T(8,128)(2,1)}), bf16[4,384,640]{2,1,0:T(8,128)(2,1)S(1)}, u32[]{:S(2)}, u32[]{:S(2)}) async-start(bf16[4,384,640]{2,1,0:T(8,128)(2,1)} %copy-done), calls=%async_computation | async-start | bytes 3932160 | tf_op jit(solution)/shard_map/all_to_all | solution.py:354
  19.3 16.4 %collective-permute-start.3 = (bf16[64,4608]{1,0:T(8,128)(2,1)S(1)}, bf16[64,4608]{1,0:T(8,128)(2,1)}, u32[]{:S(2)}, u32[]{:S(2)}) collective-permute-start(bf16[64,4608]{1,0:T(8,128)(2,1)S(1)} %reshape.44.refs_7_), channel_id=1, source_target_pairs={{0,8},{4,12},{8,0},{12,4},{16,24},{20,28},{24,16},{28,20},{1,9},{5... | collective-permute-start | bytes 1769480 | tf_op jit(solution)/shard_map/ppermute | solution.py:21
  20.8 26.2 %collective-permute-start.5 = (bf16[64,4608]{1,0:T(8,128)(2,1)S(1)}, bf16[64,4608]{1,0:T(8,128)(2,1)}, u32[]{:S(2)}, u32[]{:S(2)}) collective-permute-start(bf16[64,4608]{1,0:T(8,128)(2,1)S(1)} %reshape.44.refs_7_), channel_id=1, source_target_pairs={{0,16},{4,20},{8,24},{12,28},{16,0},{20,4},{24,8},{28,12},{1,17},{... | collective-permute-start | bytes 1769480 | tf_op jit(solution)/shard_map/ppermute | solution.py:21
  22.4 24.7 %collective-permute-start.7 = (bf16[64,4608]{1,0:T(8,128)(2,1)S(1)}, bf16[64,4608]{1,0:T(8,128)(2,1)}, u32[]{:S(2)}, u32[]{:S(2)}) collective-permute-start(bf16[64,4608]{1,0:T(8,128)(2,1)S(1)} %reshape.44.refs_7_), channel_id=1, source_target_pairs={{0,24},{4,28},{8,16},{12,20},{16,8},{20,12},{24,0},{28,4},{1,25},{... | collective-permute-start | bytes 1769480 | tf_op jit(solution)/shard_map/ppermute | solution.py:21
  22.8 25.5 %collective-permute-start.2 = (bf16[64,4608]{1,0:T(8,128)(2,1)S(1)}, bf16[64,4608]{1,0:T(8,128)(2,1)}, u32[]{:S(2)}, u32[]{:S(2)}) collective-permute-start(bf16[64,4608]{1,0:T(8,128)(2,1)S(1)} %reshape.44.refs_7_), channel_id=1, source_target_pairs={{0,4},{4,0},{8,12},{12,8},{16,20},{20,16},{24,28},{28,24},{1,5},{5... | collective-permute-start | bytes 1769480 | tf_op jit(solution)/shard_map/ppermute | solution.py:21
  35.7 13.9 %collective-permute-start.4 = (bf16[64,4608]{1,0:T(8,128)(2,1)}, bf16[64,4608]{1,0:T(8,128)(2,1)}, u32[]{:S(2)}, u32[]{:S(2)}) collective-permute-start(bf16[64,4608]{1,0:T(8,128)(2,1)} %collective-permute-done.3.refs_9_), channel_id=1, source_target_pairs={{0,4},{4,0},{8,12},{12,8},{16,20},{20,16},{24,28},{28,24},{1,5},{5... | collective-permute-start | bytes 1769480 | tf_op jit(solution)/shard_map/ppermute | solution.py:21
  47.0 5.8 %collective-permute-start.6 = (bf16[64,4608]{1,0:T(8,128)(2,1)}, bf16[64,4608]{1,0:T(8,128)(2,1)}, u32[]{:S(2)}, u32[]{:S(2)}) collective-permute-start(bf16[64,4608]{1,0:T(8,128)(2,1)} %collective-permute-done.5.refs_11_), channel_id=1, source_target_pairs={{0,4},{4,0},{8,12},{12,8},{16,20},{20,16},{24,28},{28,24},{1,5},{5... | collective-permute-start | bytes 1769480 | tf_op jit(solution)/shard_map/ppermute | solution.py:21
  47.1 5.8 %collective-permute-start.8 = (bf16[64,4608]{1,0:T(8,128)(2,1)}, bf16[64,4608]{1,0:T(8,128)(2,1)}, u32[]{:S(2)}, u32[]{:S(2)}) collective-permute-start(bf16[64,4608]{1,0:T(8,128)(2,1)} %collective-permute-done.7.refs_13_), channel_id=1, source_target_pairs={{0,4},{4,0},{8,12},{12,8},{16,20},{20,16},{24,28},{28,24},{1,5},{5... | collective-permute-start | bytes 1769480 | tf_op jit(solution)/shard_map/ppermute | solution.py:21
  47.6 19.8 %collective-permute-start.10 = (bf16[384,512]{1,0:T(8,128)(2,1)}, bf16[384,512]{1,0:T(8,128)(2,1)}, u32[]{:S(2)}, u32[]{:S(2)}) collective-permute-start(bf16[384,512]{1,0:T(8,128)(2,1)} %bitcast.9.refs_1_), channel_id=1, source_target_pairs={{0,8},{4,12},{8,0},{12,4},{16,24},{20,28},{24,16},{28,20},{1,9},{5... | collective-permute-start | bytes 1179656 | tf_op jit(solution)/shard_map/ppermute | solution.py:21
  48.3 19.1 %collective-permute-start.11 = (bf16[384,512]{1,0:T(8,128)(2,1)}, bf16[384,512]{1,0:T(8,128)(2,1)}, u32[]{:S(2)}, u32[]{:S(2)}) collective-permute-start(bf16[384,512]{1,0:T(8,128)(2,1)} %bitcast.9.refs_1_), channel_id=1, source_target_pairs={{0,16},{4,20},{8,24},{12,28},{16,0},{20,4},{24,8},{28,12},{1,17},{... | collective-permute-start | bytes 1179656 | tf_op jit(solution)/shard_map/ppermute | solution.py:21
  49.6 18.7 %collective-permute-start.12 = (bf16[384,512]{1,0:T(8,128)(2,1)}, bf16[384,512]{1,0:T(8,128)(2,1)}, u32[]{:S(2)}, u32[]{:S(2)}) collective-permute-start(bf16[384,512]{1,0:T(8,128)(2,1)} %bitcast.9.refs_1_), channel_id=1, source_target_pairs={{0,24},{4,28},{8,16},{12,20},{16,8},{20,12},{24,0},{28,4},{1,25},{... | collective-permute-start | bytes 1179656 | tf_op jit(solution)/shard_map/ppermute | solution.py:21
  57.8 0.8 copy-start.4
  58.6 0.8 copy-start.6
  63.7 10.7 %all-to-all-start.1 = ((bf16[4,480,128]{2,1,0:T(8,128)(2,1)}), bf16[4,480,128]{2,1,0:T(8,128)(2,1)S(1)}, u32[]{:S(2)}, u32[]{:S(2)}) async-start(bf16[4,480,128]{2,1,0:T(8,128)(2,1)} %copy-done.6), calls=%async_computation.1 | async-start | bytes 983040 | tf_op jit(solution)/shard_map/all_to_all | solution.py:365
  71.3 1.0 copy-start.3
  78.9 7.7 %collective-permute-start.19 = (f32[9,64,512]{2,1,0:T(8,128)S(1)}, f32[9,64,512]{2,1,0:T(8,128)}, u32[]{:S(2)}, u32[]{:S(2)}) collective-permute-start(f32[9,64,512]{2,1,0:T(8,128)S(1)} %get-tuple-element.38), channel_id=1, source_target_pairs={{0,4},{4,0},{8,12},{12,8},{16,20},{20,16},{24,28},{28,24},{1,5},{5... | collective-permute-start | bytes 3538952 | tf_op jit(solution)/shard_map/ppermute | solution.py:21
  79.0 21.1 %all-to-all-start.2 = ((bf16[8,9,16,512]{3,2,1,0:T(8,128)(2,1)}), bf16[8,9,16,512]{3,2,1,0:T(8,128)(2,1)}, u32[]{:S(2)}, u32[]{:S(2)}) async-start(bf16[8,9,16,512]{3,2,1,0:T(8,128)(2,1)} %copy-done.3), calls=%async_computation.2 | async-start | bytes 2359296 | tf_op jit(solution)/shard_map/all_to_all | solution.py:304
  88.1 13.6 %copy-start.7 = (bf16[64,4608]{1,0:T(8,128)(2,1)S(1)}, bf16[64,4608]{1,0:T(8,128)(2,1)}, u32[]{:S(2)}) copy-start(bf16[64,4608]{1,0:T(8,128)(2,1)} %reshape.47.refs_2_) | copy-start | bytes 1769476
  88.9 14.1 %collective-permute-start.20 = (bf16[9,16,512]{2,1,0:T(8,128)(2,1)S(1)}, bf16[9,16,512]{2,1,0:T(8,128)(2,1)S(1)}, u32[]{:S(2)}, u32[]{:S(2)}) collective-permute-start(bf16[9,16,512]{2,1,0:T(8,128)(2,1)S(1)} %get-tuple-element.39), channel_id=1, source_target_pairs={{0,1},{1,0},{2,3},{3,2},{4,5},{5,4},{6,7},{7,6},{8,9},{9,8},{10,11... | collective-permute-start | bytes 442376 | tf_op jit(solution)/shard_map/ppermute | solution.py:21
  89.7 20.3 %collective-permute-start.21 = (bf16[9,16,512]{2,1,0:T(8,128)(2,1)}, bf16[9,16,512]{2,1,0:T(8,128)(2,1)S(1)}, u32[]{:S(2)}, u32[]{:S(2)}) collective-permute-start(bf16[9,16,512]{2,1,0:T(8,128)(2,1)} %get-tuple-element.41), channel_id=1, source_target_pairs={{0,2},{1,3},{2,0},{3,1},{4,6},{5,7},{6,4},{7,5},{8,10},{9,11},{10,... | collective-permute-start | bytes 442376 | tf_op jit(solution)/shard_map/ppermute | solution.py:21
  92.0 18.0 %collective-permute-start.22 = (bf16[9,16,512]{2,1,0:T(8,128)(2,1)S(1)}, bf16[9,16,512]{2,1,0:T(8,128)(2,1)S(1)}, u32[]{:S(2)}, u32[]{:S(2)}) collective-permute-start(bf16[9,16,512]{2,1,0:T(8,128)(2,1)S(1)} %get-tuple-element.40), channel_id=1, source_target_pairs={{0,3},{1,2},{2,1},{3,0},{4,7},{5,6},{6,5},{7,4},{8,11},{9,10},{10,... | collective-permute-start | bytes 442376 | tf_op jit(solution)/shard_map/ppermute | solution.py:21
  101.7 33.5 %collective-permute-start.13 = (bf16[64,4608]{1,0:T(8,128)(2,1)S(1)}, bf16[64,4608]{1,0:T(8,128)(2,1)}, u32[]{:S(2)}, u32[]{:S(2)}) collective-permute-start(bf16[64,4608]{1,0:T(8,128)(2,1)S(1)} %copy-done.7), channel_id=1, source_target_pairs={{0,8},{4,12},{8,0},{12,4},{16,24},{20,28},{24,16},{28,20},{1,9},{5... | collective-permute-start | bytes 1769480 | tf_op jit(solution)/shard_map/ppermute | solution.py:21
  102.3 33.4 %collective-permute-start.15 = (bf16[64,4608]{1,0:T(8,128)(2,1)S(1)}, bf16[64,4608]{1,0:T(8,128)(2,1)}, u32[]{:S(2)}, u32[]{:S(2)}) collective-permute-start(bf16[64,4608]{1,0:T(8,128)(2,1)S(1)} %copy-done.7), channel_id=1, source_target_pairs={{0,16},{4,20},{8,24},{12,28},{16,0},{20,4},{24,8},{28,12},{1,17},{... | collective-permute-start | bytes 1769480 | tf_op jit(solution)/shard_map/ppermute | solution.py:21
  102.9 32.9 %collective-permute-start.17 = (bf16[64,4608]{1,0:T(8,128)(2,1)S(1)}, bf16[64,4608]{1,0:T(8,128)(2,1)}, u32[]{:S(2)}, u32[]{:S(2)}) collective-permute-start(bf16[64,4608]{1,0:T(8,128)(2,1)S(1)} %copy-done.7), channel_id=1, source_target_pairs={{0,24},{4,28},{8,16},{12,20},{16,8},{20,12},{24,0},{28,4},{1,25},{... | collective-permute-start | bytes 1769480 | tf_op jit(solution)/shard_map/ppermute | solution.py:21
  106.1 31.5 %all-to-all-start.3 = ((bf16[4,9,16,512]{3,2,1,0:T(8,128)(2,1)}), bf16[4,9,16,512]{3,2,1,0:T(8,128)(2,1)S(1)}, u32[]{:S(2)}, u32[]{:S(2)}) async-start(bf16[4,9,16,512]{3,2,1,0:T(8,128)(2,1)} %broadcast_in_dim.18), calls=%async_computation.3 | async-start | bytes 1179648 | tf_op jit(solution)/shard_map/all_to_all | solution.py:311
  110.1 12.6 %collective-permute-start.23 = (bf16[9,16,512]{2,1,0:T(8,128)(2,1)S(1)}, bf16[9,16,512]{2,1,0:T(8,128)(2,1)S(1)}, u32[]{:S(2)}, u32[]{:S(2)}) collective-permute-start(bf16[9,16,512]{2,1,0:T(8,128)(2,1)S(1)} %fusion.2), channel_id=1, source_target_pairs={{0,1},{1,0},{2,3},{3,2},{4,5},{5,4},{6,7},{7,6},{8,9},{9,8},{10,11... | collective-permute-start | bytes 442376 | tf_op jit(solution)/shard_map/ppermute | solution.py:21
  112.2 23.0 %collective-permute-start.24 = (bf16[9,16,512]{2,1,0:T(8,128)(2,1)S(1)}, bf16[9,16,512]{2,1,0:T(8,128)(2,1)S(1)}, u32[]{:S(2)}, u32[]{:S(2)}) collective-permute-start(bf16[9,16,512]{2,1,0:T(8,128)(2,1)S(1)} %fusion.2), channel_id=1, source_target_pairs={{0,2},{1,3},{2,0},{3,1},{4,6},{5,7},{6,4},{7,5},{8,10},{9,11},{10,... | collective-permute-start | bytes 442376 | tf_op jit(solution)/shard_map/ppermute | solution.py:21
  122.7 13.5 %collective-permute-start.25 = (bf16[9,16,512]{2,1,0:T(8,128)(2,1)S(1)}, bf16[9,16,512]{2,1,0:T(8,128)(2,1)S(1)}, u32[]{:S(2)}, u32[]{:S(2)}) collective-permute-start(bf16[9,16,512]{2,1,0:T(8,128)(2,1)S(1)} %fusion.2), channel_id=1, source_target_pairs={{0,3},{1,2},{2,1},{3,0},{4,7},{5,6},{6,5},{7,4},{8,11},{9,10},{10,... | collective-permute-start | bytes 442376 | tf_op jit(solution)/shard_map/ppermute | solution.py:21
  135.2 3.6 %collective-permute-start.9 = (bf16[64,4608]{1,0:T(8,128)(2,1)S(1)}, bf16[64,4608]{1,0:T(8,128)(2,1)S(1)}, u32[]{:S(2)}, u32[]{:S(2)}) collective-permute-start(bf16[64,4608]{1,0:T(8,128)(2,1)S(1)} %copy-done.7), channel_id=1, source_target_pairs={{0,4},{4,0},{8,12},{12,8},{16,20},{20,16},{24,28},{28,24},{1,5},{5... | collective-permute-start | bytes 1769480 | tf_op jit(solution)/shard_map/ppermute | solution.py:21
  135.2 3.6 %collective-permute-start.14 = (bf16[64,4608]{1,0:T(8,128)(2,1)}, bf16[64,4608]{1,0:T(8,128)(2,1)S(1)}, u32[]{:S(2)}, u32[]{:S(2)}) collective-permute-start(bf16[64,4608]{1,0:T(8,128)(2,1)} %collective-permute-done.13.refs_4_), channel_id=1, source_target_pairs={{0,4},{4,0},{8,12},{12,8},{16,20},{20,16},{24,28},{28,24},{1,5},{5... | collective-permute-start | bytes 1769480 | tf_op jit(solution)/shard_map/ppermute | solution.py:21
  135.7 3.5 %collective-permute-start.16 = (bf16[64,4608]{1,0:T(8,128)(2,1)}, bf16[64,4608]{1,0:T(8,128)(2,1)}, u32[]{:S(2)}, u32[]{:S(2)}) collective-permute-start(bf16[64,4608]{1,0:T(8,128)(2,1)} %collective-permute-done.15.refs_6_), channel_id=1, source_target_pairs={{0,4},{4,0},{8,12},{12,8},{16,20},{20,16},{24,28},{28,24},{1,5},{5... | collective-permute-start | bytes 1769480 | tf_op jit(solution)/shard_map/ppermute | solution.py:21
  135.8 4.3 %collective-permute-start.18 = (bf16[64,4608]{1,0:T(8,128)(2,1)}, bf16[64,4608]{1,0:T(8,128)(2,1)}, u32[]{:S(2)}, u32[]{:S(2)}) collective-permute-start(bf16[64,4608]{1,0:T(8,128)(2,1)} %collective-permute-done.17.refs_8_), channel_id=1, source_target_pairs={{0,4},{4,0},{8,12},{12,8},{16,20},{20,16},{24,28},{28,24},{1,5},{5... | collective-permute-start | bytes 1769480 | tf_op jit(solution)/shard_map/ppermute | solution.py:21
  137.6 2.4 %copy-start.5 = (bf16[480,512]{1,0:T(8,128)(2,1)S(1)}, bf16[480,512]{1,0:T(8,128)(2,1)}, u32[]{:S(2)}) copy-start(bf16[480,512]{1,0:T(8,128)(2,1)} %copy-done.4) | copy-start | bytes 1474564
  138.8 1.3 copy-start.9
  138.8 1.3 copy-start.10
